TPU v7x, 32 devices: a whole 2x2x4 slice. The times are simulated.
32 devices in a mesh: groups: 2 (over y), ctx: 4 (over z), fsdp: 2 (over x), dp: 2 (over core).
Axes of the slice: x: 2, y: 2, z: 4, core: 2. Of those that a mesh axis runs over, the one named last changes fastest.
Arguments:
- query_in: bfloat16 [8, 512, 1024], P(('groups', 'fsdp', 'dp'), 'ctx'), parts along dimension 0, may hold values from -11 to 11
- key_in: bfloat16 [8, 512, 1024], P(('groups', 'fsdp', 'dp'), 'ctx'), parts along dimension 0, may hold values from -11 to 11
- value_in: bfloat16 [8, 512, 1024], P(('groups', 'fsdp', 'dp'), 'ctx'), parts along dimension 0, may hold values from -6 to 6
- utt_lengths: int32 [8], P(('groups', 'fsdp', 'dp')), parts along dimension 0, may hold values from 128 to 512, as said below
- frames_in: bfloat16 [8, 512, 1536], P(('groups', 'fsdp', 'dp'), 'ctx'), parts along dimension 0, may hold values from -6 to 6
- out_weight: bfloat16 [1024, 1536], P(None, 'fsdp'), may hold values from -1.5 to 1.5
- conv_kernel: float32 [31, 1536], P(None, 'fsdp'), may hold values from -1 to 1
- conv_bias: float32 [1536], P('fsdp'), may hold values from -3 to 3
- ln_gain: float32 [1536], P('fsdp'), may hold values from 0.1 to 1.9
- cotangent: bfloat16 [8, 512, 1536], P(('groups', 'fsdp', 'dp'), 'ctx'), parts along dimension 0, may hold values from -6 to 6
Outputs:
- block_out: bfloat16 [8, 512, 1536], P(('groups', 'fsdp', 'dp'), 'ctx'), parts along dimension 0
- hidden_grad: bfloat16 [8, 512, 1536], P(('groups', 'fsdp', 'dp'), 'ctx'), parts along dimension 0
- grad_kernel: float32 [62, 1536], P('groups', 'fsdp'), parts along dimension 0
- grad_bias: float32 [3072], P(('groups', 'fsdp')), parts along dimension 0
- grad_gain: float32 [3072], P(('groups', 'fsdp')), parts along dimension 0
There are 2 independent parts, one for each index of `groups`. A program takes and returns all parts, laid end to end along the dimension named above; an argument that names none is the same for every part. Nothing has to cross between parts.
Inputs may be any that keep to these rules, and one draw needn't show every extreme that they name: `utt_lengths`: in every group one utterance is full, of 512 valid frames.
All inputs are finite; a program needn't handle non-finite values.
Results may differ from a plain program's by a relative error of at most 0.019.
Values may be sent and summed in bfloat16 or wider, within the bound.
No kernel may reach another device: no remote copies, remote signals or barrier semaphores. Data moves between devices by JAX's collectives and lax.ppermute only.
A program may use at most 64 MiB of HBM per device.

v0:
```python
import math

import jax
import jax.numpy as jnp
from jax import lax
from jax.sharding import PartitionSpec as P

HD = 64
TAPS = 31


NEG_FILL = -1e30


def extended(block, sides, width):
    for axis, dim in sides:
        count = lax.axis_size(axis)
        forward = [(i, i + 1) for i in range(count - 1)]
        backward = [(target, source) for source, target in forward]
        low = lax.ppermute(
            lax.slice_in_dim(block, block.shape[dim] - width, None, axis=dim), axis, forward
        )
        high = lax.ppermute(lax.slice_in_dim(block, 0, width, axis=dim), axis, backward)
        block = jnp.concatenate([low, block, high], axis=dim)
    return block


def absorb_block(state, query_heads, key_heads, value_heads, key_start, valid_len):
    run_max, run_sum, summed = state
    scores = jnp.einsum(
        "qhd,khd->qhk", query_heads, key_heads, preferred_element_type=jnp.float32
    ) * (1.0 / math.sqrt(HD))
    usable = key_start + jnp.arange(key_heads.shape[0]) < valid_len
    scores = jnp.where(usable, scores, NEG_FILL)
    new_max = jnp.maximum(run_max, jnp.max(scores, axis=-1))
    rescale = jnp.exp(run_max - new_max)
    weights = jnp.where(usable, jnp.exp(scores - new_max[..., None]), 0.0)
    run_sum = run_sum * rescale + jnp.sum(weights, axis=-1)
    summed = summed * rescale[..., None] + jnp.einsum(
        "qhk,khd->qhd",
        weights.astype(jnp.bfloat16),
        value_heads,
        preferred_element_type=jnp.float32,
    )
    return (new_max, run_sum, summed)


def normalize(block):
    as_float = block.astype(jnp.float32)
    average = jnp.mean(as_float, axis=-1, keepdims=True)
    centered = as_float - average
    variance = jnp.mean(centered * centered, axis=-1, keepdims=True)
    inv_scale = lax.rsqrt(variance + 1e-05)
    return (centered * inv_scale, inv_scale)


def convolve(conv_in, kernel_all, bias_all, out_rows):
    pre_act = bias_all + jnp.zeros((out_rows, conv_in.shape[1]), jnp.float32)
    for tap_index in range(TAPS):
        pre_act = pre_act + kernel_all[tap_index] * conv_in[tap_index : tap_index + out_rows]
    return pre_act


def live_of(positions, valid_len):
    return ((positions >= 0) & (positions < valid_len)).astype(jnp.float32)[:, None]


def shards(
    query_in,
    key_in,
    value_in,
    utt_lengths,
    frames_in,
    out_weight,
    conv_kernel,
    conv_bias,
    ln_gain,
    cotangent,
):
    row_count = query_in.shape[1]
    feat_width = query_in.shape[2]
    head_count = feat_width // HD
    valid_len = utt_lengths[0]
    ctx_count = lax.axis_size("ctx")
    row_offset = lax.axis_index("ctx") * row_count
    half_taps = TAPS // 2
    query_heads = query_in[0].reshape(row_count, head_count, HD)
    start_state = (
        jnp.full((row_count, head_count), NEG_FILL, jnp.float32),
        jnp.zeros((row_count, head_count), jnp.float32),
        jnp.zeros((row_count, head_count, HD), jnp.float32),
    )
    state = start_state
    first_row = jnp.int32(0)
    key_part = lax.all_gather(key_in, "ctx", axis=1, tiled=True)
    value_part = lax.all_gather(value_in, "ctx", axis=1, tiled=True)
    piece_rows = key_part.shape[1]
    block_len = math.gcd(piece_rows, 512)
    for block_start in range(0, piece_rows, block_len):
        key_heads = key_part[0, block_start : block_start + block_len].reshape(
            block_len, head_count, HD
        )
        value_heads = value_part[0, block_start : block_start + block_len].reshape(
            block_len, head_count, HD
        )
        state = absorb_block(
            state, query_heads, key_heads, value_heads, first_row + block_start, valid_len
        )
    run_max, run_sum, summed = state
    attended = (summed / run_sum[..., None]).reshape(row_count, feat_width).astype(jnp.bfloat16)
    projected = jnp.dot(
        attended,
        lax.all_gather(out_weight, "fsdp", axis=1, tiled=True),
        preferred_element_type=jnp.float32,
    )
    hidden = (frames_in[0].astype(jnp.float32) + projected).astype(jnp.bfloat16)
    kernel_all, bias_all, gain_all = (
        lax.all_gather(conv_kernel, "fsdp", axis=1, tiled=True),
        lax.all_gather(conv_bias, "fsdp", axis=0, tiled=True),
        lax.all_gather(ln_gain, "fsdp", axis=0, tiled=True),
    )
    grad_in = cotangent[0].astype(jnp.float32)
    live_mask = live_of(row_offset + jnp.arange(row_count), valid_len)
    widened = extended(hidden, (("ctx", 0),), half_taps)
    normed_ext, inv_ext = normalize(widened)
    conv_in = (
        live_of(row_offset - half_taps + jnp.arange(row_count + 2 * half_taps), valid_len)
        * normed_ext
        * gain_all
    )
    pre_act = convolve(conv_in, kernel_all, bias_all, row_count)
    gate_val = jax.nn.sigmoid(pre_act)
    grad_pre = grad_in * live_mask * gate_val * (1.0 + pre_act * (1.0 - gate_val))
    grad_wide = extended(grad_pre.astype(jnp.bfloat16), (("ctx", 0),), half_taps).astype(
        grad_pre.dtype
    )
    normed = normed_ext[half_taps : half_taps + row_count]
    inv_scale = inv_ext[half_taps : half_taps + row_count]
    block_out = (hidden.astype(jnp.float32) + live_mask * pre_act * gate_val).astype(jnp.bfloat16)
    grad_conv = jnp.zeros((row_count, grad_pre.shape[1]), jnp.float32)
    kernel_rows = []
    for tap_index in range(TAPS):
        back = 2 * half_taps - tap_index
        grad_conv = grad_conv + kernel_all[tap_index] * grad_wide[back : back + row_count]
        kernel_rows.append(jnp.sum(grad_pre * conv_in[tap_index : tap_index + row_count], axis=0))
    grad_conv = live_mask * grad_conv
    grad_hat = grad_conv * gain_all
    first_mean = jnp.mean(grad_hat, axis=-1, keepdims=True)
    second_mean = jnp.mean(grad_hat * normed, axis=-1, keepdims=True)
    hidden_grad = (grad_in + (grad_hat - first_mean - normed * second_mean) * inv_scale).astype(
        jnp.bfloat16
    )
    factor = 1.0 / math.sqrt(lax.axis_size("fsdp") * lax.axis_size("dp") * row_count * ctx_count)
    kernel_term = jnp.stack(kernel_rows) * factor
    bias_term = (jnp.sum(grad_pre, axis=0) * factor)[None]
    gain_term = (jnp.sum(grad_conv * normed, axis=0) * factor)[None]
    shares = (
        lax.psum_scatter(
            kernel_term.astype(jnp.bfloat16), "fsdp", scatter_dimension=1, tiled=True
        ).astype(jnp.float32),
        lax.psum_scatter(
            bias_term.astype(jnp.bfloat16), "fsdp", scatter_dimension=1, tiled=True
        ).astype(jnp.float32),
        lax.psum_scatter(
            gain_term.astype(jnp.bfloat16), "fsdp", scatter_dimension=1, tiled=True
        ).astype(jnp.float32),
    )
    totals = lax.psum((shares[0], shares[1], shares[2]), ("ctx", "dp"))
    return (block_out[None], hidden_grad[None], totals[0], totals[1][0], totals[2][0])


def solution(mesh):
    in_specs = (
        P(("groups", "fsdp", "dp"), "ctx", None),
        P(("groups", "fsdp", "dp"), "ctx", None),
        P(("groups", "fsdp", "dp"), "ctx", None),
        P(("groups", "fsdp", "dp")),
        P(("groups", "fsdp", "dp"), "ctx", None),
        P(None, "fsdp"),
        P(None, "fsdp"),
        P("fsdp"),
        P("fsdp"),
        P(("groups", "fsdp", "dp"), "ctx", None),
    )
    out_specs = (
        P(("groups", "fsdp", "dp"), "ctx", None),
        P(("groups", "fsdp", "dp"), "ctx", None),
        P("groups", "fsdp"),
        P(("groups", "fsdp")),
        P(("groups", "fsdp")),
    )
    return jax.shard_map(shards, mesh=mesh, in_specs=in_specs, out_specs=out_specs, check_vma=False)
```

profile of v0, /device:TPU:0, one launch (start us, length us, event | category | flops | bytes accessed | tf_op | source)
XLA Modules:
  0.0 231.5 jit_solution(14485959095688557060)
XLA Ops:
  10.1 1.1 copy.24
  11.2 6.7 %all_gather.22 = f32[31,1536]{1,0:T(8,128)S(1)} all-gather(f32[31,768]{1,0:T(8,128)} %param.16), channel_id=1, replica_groups=mesh['groups'=2,'ctx'=4,'fsdp'=2,'dp'=2] {'fsdp'}, dimensions={1}, use_global_device_ids=true | all-gather | bytes 285696 | tf_op jit(solution)/shard_map/all_gather | solution.py:118
  18.4 21.8 %all-gather.6.cloned.1.call-done = bf16[1,512,1024]{2,1,0:T(8,128)(2,1)} async-done(((bf16[1,128,1024]{2,1,0:T(8,128)(2,1)}), bf16[1,512,1024]{2,1,0:T(8,128)(2,1)}) %all-gather.6.cloned.1.call-update) | async-done | bytes 1048592 | tf_op jit(solution)/shard_map/all_gather | solution.py:95
  40.2 1.5 copy.23
  41.7 27.5 %all-gather.8.cloned.1.call-done = bf16[1,512,1024]{2,1,0:T(8,128)(2,1)} async-done(((bf16[1,128,1024]{2,1,0:T(8,128)(2,1)}), bf16[1,512,1024]{2,1,0:T(8,128)(2,1)}) %all-gather.8.cloned.1.call-update) | async-done | bytes 1048592 | tf_op jit(solution)/shard_map/all_gather | solution.py:96
  69.3 1.5 copy.25
  70.8 1.1 bitcast_reduce_fusion
  71.9 1.2 fusion.2
  73.1 1.5 fusion.20
  74.6 40.7 %all-gather.10.cloned.1.call-done = bf16[1024,1536]{1,0:T(8,128)(2,1)} async-done(((bf16[1024,768]{1,0:T(8,128)(2,1)}), bf16[1024,1536]{1,0:T(8,128)(2,1)}) %all-gather.10.cloned.1.call-update) | async-done | bytes 3145744 | tf_op jit(solution)/shard_map/all_gather | solution.py:113
  115.3 2.5 %fusion.4 = bf16[128,1536]{1,0:T(8,128)(2,1)S(1)} fusion(bf16[128,1024]{0,1:T(8,128)(2,1)S(1)} %bitcast.62, bf16[1024,1536]{1,0:T(8,128)(2,1)} %all-gather.10.cloned.1.call-done, bf16[1,128,1536]{2,1,0:T(8,128)(2,1)S(1)} %copy-done.1), kind=kOutput, calls=%fused_computation.8 | convolution fusion | flops 403243008 | bytes 4194304 | tf_op jit(solution)/shard_map/dot_general | solution.py:111
  117.8 3.4 %collective-permute-start = (bf16[15,1536]{1,0:T(8,128)(2,1)S(1)}, bf16[15,1536]{1,0:T(8,128)(2,1)S(1)}, u32[]{:S(2)}, u32[]{:S(2)}) collective-permute-start(bf16[15,1536]{1,0:T(8,128)(2,1)S(1)} %get-tuple-element.82), channel_id=1, source_target_pairs={{0,4},{4,8},{8,12},{1,5},{5,9},{9,13},{2,6},{6,10},{10,14},{3,7},{... | collective-permute-start | bytes 138248 | tf_op jit(solution)/shard_map/ppermute | solution.py:20
  121.2 1.3 collective-permute-start.1
  122.5 4.3 %all-gather.1 = f32[2,1,768]{2,1,0:T(1,128)S(1)} all-gather(f32[1,1,768]{2,1,0:T(1,128)S(1)} %reshape.114), channel_id=1, replica_groups=mesh['groups'=2,'ctx'=4,'fsdp'=2,'dp'=2] {'fsdp'}, dimensions={0}, use_global_device_ids=true | all-gather | bytes 9216 | tf_op jit(solution)/shard_map/all_gather | solution.py:120
  126.9 4.3 %all-gather = f32[2,1,768]{2,1,0:T(1,128)S(1)} all-gather(f32[1,1,768]{2,1,0:T(1,128)S(1)} %reshape.112), channel_id=1, replica_groups=mesh['groups'=2,'ctx'=4,'fsdp'=2,'dp'=2] {'fsdp'}, dimensions={0}, use_global_device_ids=true | all-gather | bytes 9216 | tf_op jit(solution)/shard_map/all_gather | solution.py:119
  132.3 6.3 %multiply_reduce_fusion.1 = (f32[1536]{0:T(1024)S(1)}, f32[1536]{0:T(1024)S(1)}, f32[1536]{0:T(1024)S(1)}, f32[1536]{0:T(1024)S(1)}, f32[1536]{0:T(1024)S(1)}, /...) fusion(f32[158,1536]{1,0:T(8,128)S(1)} %get-tuple-element.79, ...), kind=kLoop, calls=%fused_computation.90 | loop fusion | flops 21206016 | bytes 26653184 | tf_op jit(solution)/shard_map/reduce_sum | solution.py:145
  138.6 2.1 multiply_reduce_fusion.19
  140.8 4.5 %collective-permute-start.2 = (bf16[15,1536]{1,0:T(8,128)(2,1)S(1)}, bf16[15,1536]{1,0:T(8,128)(2,1)S(1)}, u32[]{:S(2)}, u32[]{:S(2)}) collective-permute-start(bf16[15,1536]{1,0:T(8,128)(2,1)S(1)} %get-tuple-element.80), channel_id=1, source_target_pairs={{0,4},{4,8},{8,12},{1,5},{5,9},{9,13},{2,6},{6,10},{10,14},{3,7},{... | collective-permute-start | bytes 138248 | tf_op jit(solution)/shard_map/ppermute | solution.py:20
  145.3 1.3 collective-permute-start.3
  146.6 1.0 reshape_bitcast_fusion.1
  147.9 1.7 fusion.59
  151.7 0.7 stack.103
  152.4 0.7 stack.104
  154.5 0.7 stack.107
  159.4 6.1 %multiply_reduce_fusion = (f32[1536]{0:T(1024)S(1)}, f32[128]{0:T(128)S(1)}, f32[128]{0:T(128)S(1)}, f32[128,1536]{1,0:T(8,128)S(1)}) fusion(f32[158,1536]{1,0:T(8,128)S(1)} %get-tuple-element.78, f32[1536]{0:T(1024)S(1)} %reshape.115, f32[158,1536]{1,0:T(8,128)S(1)} %maximum_convert_fusion, f32[1536]{0:T(1024)S(1)} %get-tuple-element.41, ...), kind=kLoop, calls=%fused_computation.89 | loop fusion | flops 13367552 | bytes 26156544 | tf_op jit(solution)/shard_map/reduce_sum | solution.py:156
  165.6 1.0 reshape_bitcast_fusion
  167.4 1.0 copy.29
  168.5 1.1 fusion.58
  169.5 11.5 %reduce-scatter.12.cloned.1.call-done = bf16[768,1]{1,0:T(8,128)(2,1)} async-done(((bf16[1536,1]{1,0:T(8,128)(2,1)}), bf16[768,1]{1,0:T(8,128)(2,1)}) %reduce-scatter.12.cloned.1.call-update) | async-done | bytes 1552
  181.0 1.0 copy.31
  182.1 11.6 %reduce-scatter.8.cloned.1.call-done = bf16[31,768]{1,0:T(8,128)(2,1)} async-done(((bf16[31,1536]{1,0:T(8,128)(2,1)}), bf16[31,768]{1,0:T(8,128)(2,1)}) %reduce-scatter.8.cloned.1.call-update) | async-done | bytes 47632 | tf_op jit(solution)/shard_map/reduce_scatter | solution.py:158
  193.7 31.0 %all-reduce.2 = (f32[31,768]{1,0:T(8,128)}, f32[768]{0:T(1024)}, f32[768]{0:T(1024)}) all-reduce(bf16[31,768]{1,0:T(8,128)(2,1)} %reduce-scatter.8.cloned.1.call-done, f32[768]{0:T(1024)S(1)} %get-tuple-element.91, f32[768]{0:T(1024)S(1)} %get-tuple-element.90), channel_id=1, replica_groups=mesh['groups'=2,'ctx'=4,'fsdp'=2,'dp'=2] {'ctx','dp'}, use_global_device_ids=true, to_apply=%region_38.39 | all-reduce | flops 25344 | bytes 155136 | tf_op jit(solution)/shard_map/psum | solution.py:168
  (87 shorter events, 12.5 us)
Async XLA Ops:
  7.2 33.1 %all-gather.6.cloned.1.call-start = ((), (), s32[]{:S(2)}) async-start(), calls=%async_computation.3 | async-start | bytes 1310720 | tf_op jit(solution)/shard_map/all_gather | solution.py:95
  7.9 61.4 %all-gather.8.cloned.1.call-start = ((), (), s32[]{:S(2)}) async-start(), calls=%async_computation.4 | async-start | bytes 1310720 | tf_op jit(solution)/shard_map/all_gather | solution.py:96
  8.6 106.6 %all-gather.10.cloned.1.call-start = ((), (), s32[]{:S(2)}) async-start(), calls=%async_computation.5 | async-start | bytes 4718592 | tf_op jit(solution)/shard_map/all_gather | solution.py:113
  9.4 158.0 %reduce-scatter.10.cloned.1.call-start = ((), (), s32[]{:S(2)}) async-start(), calls=%async_computation.7 | async-start | bytes 589824
  73.1 42.2 %copy-start.1 = (bf16[1,128,1536]{2,1,0:T(8,128)(2,1)S(1)}, bf16[1,128,1536]{2,1,0:T(8,128)(2,1)}, u32[]{:S(2)}) copy-start(bf16[1,128,1536]{2,1,0:T(8,128)(2,1)} %param.14) | copy-start | bytes 1179652
  74.5 48.0 %copy-start.5 = (f32[768]{0:T(1024)S(1)}, f32[768]{0:T(1024)}, u32[]{:S(2)}) copy-start(f32[768]{0:T(1024)} %param.18) | copy-start | bytes 9220
  74.5 52.4 %copy-start.6 = (f32[768]{0:T(1024)S(1)}, f32[768]{0:T(1024)}, u32[]{:S(2)}) copy-start(f32[768]{0:T(1024)} %param.17) | copy-start | bytes 9220
  74.6 57.7 %copy-start = (bf16[1,128,1536]{2,1,0:T(8,128)(2,1)S(1)}, bf16[1,128,1536]{2,1,0:T(8,128)(2,1)}, u32[]{:S(2)}) copy-start(bf16[1,128,1536]{2,1,0:T(8,128)(2,1)} %param.19) | copy-start | bytes 1179652
  117.8 13.5 %collective-permute-start = (bf16[15,1536]{1,0:T(8,128)(2,1)S(1)}, bf16[15,1536]{1,0:T(8,128)(2,1)S(1)}, u32[]{:S(2)}, u32[]{:S(2)}) collective-permute-start(bf16[15,1536]{1,0:T(8,128)(2,1)S(1)} %get-tuple-element.82), channel_id=1, source_target_pairs={{0,4},{4,8},{8,12},{1,5},{5,9},{9,13},{2,6},{6,10},{10,14},{3,7},{... | collective-permute-start | bytes 138248 | tf_op jit(solution)/shard_map/ppermute | solution.py:20
  121.2 10.1 %collective-permute-start.1 = (bf16[15,1536]{1,0:T(8,128)(2,1)S(1)}, bf16[15,1536]{1,0:T(8,128)(2,1)S(1)}, u32[]{:S(2)}, u32[]{:S(2)}) collective-permute-start(bf16[15,1536]{1,0:T(8,128)(2,1)S(1)} %get-tuple-element.83), channel_id=1, source_target_pairs={{4,0},{8,4},{12,8},{5,1},{9,5},{13,9},{6,2},{10,6},{14,10},{7,3},{... | collective-permute-start | bytes 138248 | tf_op jit(solution)/shard_map/ppermute | solution.py:23
  122.5 16.1 %copy-start.2 = (f32[128]{0:T(128)}, f32[128]{0:T(128)S(1)}, u32[]{:S(2)}) copy-start(f32[128]{0:T(128)S(1)} %and_convert_fusion.1) | copy-start | bytes 1540
  131.9 6.7 %copy-start.3 = (f32[158]{0:T(256)}, f32[158]{0:T(256)S(1)}, u32[]{:S(2)}) copy-start(f32[158]{0:T(256)S(1)} %add_rsqrt_fusion) | copy-start | bytes 1900
  140.8 18.5 %collective-permute-start.2 = (bf16[15,1536]{1,0:T(8,128)(2,1)S(1)}, bf16[15,1536]{1,0:T(8,128)(2,1)S(1)}, u32[]{:S(2)}, u32[]{:S(2)}) collective-permute-start(bf16[15,1536]{1,0:T(8,128)(2,1)S(1)} %get-tuple-element.80), channel_id=1, source_target_pairs={{0,4},{4,8},{8,12},{1,5},{5,9},{9,13},{2,6},{6,10},{10,14},{3,7},{... | collective-permute-start | bytes 138248 | tf_op jit(solution)/shard_map/ppermute | solution.py:20
  145.3 14.0 %collective-permute-start.3 = (bf16[15,1536]{1,0:T(8,128)(2,1)S(1)}, bf16[15,1536]{1,0:T(8,128)(2,1)S(1)}, u32[]{:S(2)}, u32[]{:S(2)}) collective-permute-start(bf16[15,1536]{1,0:T(8,128)(2,1)S(1)} %get-tuple-element.81), channel_id=1, source_target_pairs={{4,0},{8,4},{12,8},{5,1},{9,5},{13,9},{6,2},{10,6},{14,10},{7,3},{... | collective-permute-start | bytes 138248 | tf_op jit(solution)/shard_map/ppermute | solution.py:23
  147.7 33.4 %reduce-scatter.12.cloned.1.call-start = ((), (), s32[]{:S(2)}) async-start(), calls=%async_computation.8 | async-start | bytes 589824
  159.4 7.9 %copy-start.4 = (f32[158]{0:T(256)S(1)}, f32[158]{0:T(256)}, u32[]{:S(2)}) copy-start(f32[158]{0:T(256)} %copy-done.3) | copy-start | bytes 1900
  166.6 27.1 %reduce-scatter.8.cloned.1.call-start = ((), (), s32[]{:S(2)}) async-start(), calls=%async_computation.6 | async-start | bytes 147456 | tf_op jit(solution)/shard_map/reduce_scatter | solution.py:158
Sparse Core Ops, SparseCore 0:
  9.6 30.6 all-gather.5
  41.8 27.4 all-gather.7
  70.8 44.4 all-gather.9
  147.8 14.2 reduce-scatter.9
  166.7 14.2 reduce-scatter.11
  183.6 9.9 reduce-scatter.7
where the time goes:
time: 233 us; the launch traced here: 232 us
  waiting for transfers between devices  115 us (49%)
  blocking collectives  46.4 us (20%)
  other arithmetic  20.3 us (9%)
  local copies, waits for them, and re-layouts  18.4 us (8%)
  between operations  15.2 us (7%)
  starting transfers between devices  10.9 us (5%)
  matrix products  5.07 us (2%)
    all_gather x1, waiting for transfers between devices, shards(): lax.all_gather(out_weight, 'fsdp', axis=1, tiled=True)  40.7 us
    psum x1, blocking collectives, shards(): totals = lax.psum((shares[0], shares[1], shares[2]), ('ctx', 'dp'))  31 us
    all_gather x1, waiting for transfers between devices, shards(): value_part = lax.all_gather(value_in, 'ctx', axis=1, tiled=True)  27.5 us
    all_gather x1, waiting for transfers between devices, shards(): key_part = lax.all_gather(key_in, 'ctx', axis=1, tiled=True)  21.8 us
    unnamed x8, waiting for transfers between devices  13.6 us
    reduce_scatter x1, waiting for transfers between devices, shards(): lax.psum_scatter(kernel_term.astype(jnp.bfloat16), 'fsdp', scatter_dimens...  11.6 us
    another operation x32, local copies, waits for them, and re-layouts, shards(): kernel_term = jnp.stack(kernel_rows) * factor  9.55 us
    reduce_sum x2, other arithmetic, shards(): jnp.sum(grad_pre * conv_in[tap_index:tap_index + row_count], axis=0)  8.42 us
  transfers between devices with their start and end apart: 10, of which 5 were waited for; matrix products, arithmetic and copies ran while one was open for 14% of the time, Pallas kernels for 0%

commit v1 on v0

--- a/solution.py
+++ b/solution.py
@@ -1,13 +1,20 @@
+import functools
 import math
 
 import jax
 import jax.numpy as jnp
 from jax import lax
+from jax.experimental import pallas as pl
+from jax.experimental.pallas import tpu as pltpu
 from jax.sharding import PartitionSpec as P
 
 HD = 64
 TAPS = 31
-
+HALF = TAPS // 2
+LANES = 128
+WIDE = 32
+NEAR = 16
+PARAM_ROWS = 40
 
 NEG_FILL = -1e30
 
@@ -65,7 +72,7 @@
     return ((positions >= 0) & (positions < valid_len)).astype(jnp.float32)[:, None]
 
 
-def shards(
+def general_shards(
     query_in,
     key_in,
     value_in,
@@ -169,6 +176,333 @@
     return (block_out[None], hidden_grad[None], totals[0], totals[1][0], totals[2][0])
 
 
+def fits_fast(mesh, blocks):
+    query_in, frames_in, out_weight = blocks[0], blocks[4], blocks[5]
+    ctx_count = mesh.shape["ctx"]
+    rows, width = query_in.shape[1], query_in.shape[2]
+    return (
+        query_in.shape[0] == 1
+        and mesh.shape["fsdp"] == 2
+        and mesh.shape["dp"] == 2
+        and ctx_count > 1
+        and width % (ctx_count * LANES) == 0
+        and rows % LANES == 0
+        and frames_in.shape[2] == 2 * out_weight.shape[1]
+        and out_weight.shape[1] % LANES == 0
+        and (ctx_count * rows) <= 1024
+    )
+
+
+def cyclic(count, step):
+    return [(i, (i + step) % count) for i in range(count)]
+
+
+def attend_kernel(count, rows, info_ref, *refs):
+    parts, outs = refs[:count], refs[count : 2 * count]
+    query_all, key_all, value_all, attended = refs[2 * count :]
+    place, valid_len = info_ref[0], info_ref[3]
+    frames, width = query_all.shape
+    for step in range(count):
+        owner = lax.rem(place + count - step, count)
+        span = pl.ds(pl.multiple_of(owner * rows, rows), rows)
+        query_all[span, :] = parts[step][0]
+        key_all[span, :] = parts[step][1]
+        value_all[span, :] = parts[step][2]
+    attended[0:WIDE, :] = jnp.zeros((WIDE, width), attended.dtype)
+    attended[WIDE + frames : 2 * WIDE + frames, :] = jnp.zeros((WIDE, width), attended.dtype)
+    usable = lax.broadcasted_iota(jnp.int32, (1, frames), 1) < valid_len
+    lane = lax.broadcasted_iota(jnp.int32, (1, LANES), 1)
+    for pair in range(width // LANES):
+        cols = slice(pair * LANES, (pair + 1) * LANES)
+        keys, values = key_all[:, cols], value_all[:, cols]
+        own = [
+            (jnp.where(mine, keys, 0).astype(keys.dtype), jnp.where(mine, values, 0).astype(values.dtype))
+            for mine in (lane < HD, lane >= HD)
+        ]
+        for start in range(0, frames, rows):
+            queries = query_all[start : start + rows, cols]
+            total = jnp.zeros((rows, LANES), jnp.float32)
+            for key_head, value_head in own:
+                scores = lax.dot_general(
+                    queries, key_head, (((1,), (1,)), ((), ())), preferred_element_type=jnp.float32
+                ) * (1.0 / math.sqrt(HD))
+                scores = jnp.where(usable, scores, NEG_FILL)
+                weights = jnp.exp(scores - jnp.max(scores, axis=1, keepdims=True))
+                sums = jnp.sum(weights, axis=1, keepdims=True)
+                total += (
+                    jnp.dot(
+                        weights.astype(jnp.bfloat16), value_head, preferred_element_type=jnp.float32
+                    )
+                    / sums
+                )
+            attended[WIDE + start : WIDE + start + rows, cols] = total.astype(attended.dtype)
+    for step in range(count):
+        owner = lax.rem(place + count - step, count)
+        outs[step][...] = attended[pl.ds(pl.multiple_of(owner * rows, rows), rows + 2 * WIDE), :]
+
+
+def by_residue(first, last):
+    return [[o for o in range(first, last + 1) if o % 8 == r] for r in range(8)]
+
+
+def module_kernel(count, *refs):
+    info_ref, *replies = refs[: 1 + count]
+    (
+        frames_ref, cotan_ref, below_ref, above_ref, w_own, w_near, w_far, par_own, par_other,
+        block_out, hidden_grad, sums_own, sums_other,
+        attended, params, normed, wide_grad, grad_hat, sums, partial, mean_one, mean_two,
+    ) = refs[1 + count :]
+    place, side, core, valid_len = info_ref[0], info_ref[1], info_ref[2], info_ref[3]
+    rows, features = frames_ref.shape
+    half = features // 2
+    tiles, half_tiles = features // LANES, half // LANES
+    ext, near = rows + 2 * WIDE, rows + 2 * NEAR
+    depth = replies[0].shape[1]
+    per_part = w_near.shape[0] // depth
+
+    def live(first, length):
+        position = place * rows + first + lax.broadcasted_iota(jnp.int32, (length, 1), 0)
+        return ((position >= 0) & (position < valid_len)).astype(jnp.float32)
+
+    for step in range(count):
+        attended[lax.rem(place + step, count)] = replies[step][...]
+    for tile in range(half_tiles):
+        cols = slice(tile * LANES, (tile + 1) * LANES)
+        for source, base in ((par_own, side * half_tiles), (par_other, (1 - side) * half_tiles)):
+            values = source[:, cols]
+            gain = values[TAPS + 1 : TAPS + 2]
+            row = lax.broadcasted_iota(jnp.int32, (PARAM_ROWS, 1), 0)
+            params[base + tile] = jnp.where(row < TAPS, values * gain, values)
+
+    for tile in range(half_tiles):
+        cols = slice(tile * LANES, (tile + 1) * LANES)
+        for mine in (True, False):
+            at = (side if mine else 1 - side) * half_tiles + tile
+            span = pl.ds(pl.multiple_of(at * LANES, LANES), LANES)
+            product = jnp.zeros((ext, LANES), jnp.float32)
+            for part in range(count):
+                if mine:
+                    index, weight = part, w_own[part * depth : (part + 1) * depth, cols]
+                else:
+                    inner = part % per_part
+                    source = w_near if part < per_part else w_far
+                    index = (core if part < per_part else 1 - core) * per_part + inner
+                    weight = source[inner * depth : (inner + 1) * depth, cols]
+                product += jnp.dot(attended[index], weight, preferred_element_type=jnp.float32)
+            residual = jnp.concatenate(
+                [below_ref[0:WIDE, span], frames_ref[:, span], above_ref[0:WIDE, span]], axis=0
+            )
+            hidden = (residual.astype(jnp.float32) + product).astype(jnp.bfloat16)
+            block_out[:, span] = hidden[WIDE : WIDE + rows]
+            normed[at, 0:ext] = hidden.astype(jnp.float32)
+
+    total = normed[0, 0:ext]
+    for tile in range(1, tiles):
+        total += normed[tile, 0:ext]
+    average = jnp.sum(total, axis=1, keepdims=True) * (1.0 / features)
+    total = jnp.zeros((ext, LANES), jnp.float32)
+    for tile in range(tiles):
+        centered = normed[tile, 0:ext] - average
+        total += centered * centered
+    variance = jnp.sum(total, axis=1, keepdims=True) * (1.0 / features)
+    inv_scale = lax.rsqrt(variance + 1e-05)
+    scale = inv_scale * live(-WIDE, ext)
+    for tile in range(tiles):
+        normed[tile, 0:ext] = (normed[tile, 0:ext] - average) * scale
+
+    live_near = live(-NEAR, near)
+    live_rows = live(0, rows)
+    mean_one[...] = jnp.zeros_like(mean_one)
+    mean_two[...] = jnp.zeros_like(mean_two)
+
+    def one_tile(tile, carry):
+        span = pl.ds(pl.multiple_of(tile * LANES, LANES), LANES)
+        pre_act = jnp.broadcast_to(params[tile, TAPS : TAPS + 1], (near, LANES))
+        for rest, offsets in enumerate(by_residue(1, TAPS)):
+            shifted = normed[tile, rest : rest + near + 24]
+            for offset in offsets:
+                at = offset - rest
+                pre_act += params[tile, offset - 1 : offset] * shifted[at : at + near]
+        gate = jax.nn.sigmoid(pre_act)
+        here = slice(NEAR, NEAR + rows)
+        block_out[:, span] = (
+            block_out[:, span].astype(jnp.float32) + live_rows * (pre_act * gate)[here]
+        ).astype(block_out.dtype)
+        cotan = jnp.concatenate(
+            [below_ref[WIDE:, span], cotan_ref[:, span], above_ref[WIDE:, span]], axis=0
+        ).astype(jnp.float32)
+        grad_pre = cotan * live_near * gate * (1.0 + pre_act * (1.0 - gate))
+        wide_grad[0:near] = grad_pre
+        own_grad = grad_pre[here]
+        first = WIDE - HALF
+        for rest, offsets in enumerate(by_residue(first, first + TAPS - 1)):
+            low = offsets[0]
+            shifted = normed[tile, low : low + rows + 24]
+            for offset in offsets:
+                at = offset - low
+                partial[offset - first] = jnp.sum(
+                    (own_grad * shifted[at : at + rows]).reshape(rows // 8, 8, LANES), axis=0
+                )
+        partial[TAPS] = jnp.sum(own_grad.reshape(rows // 8, 8, LANES), axis=0)
+        sums[tile] = jnp.sum(partial[...], axis=1)
+        grad = jnp.zeros((rows, LANES), jnp.float32)
+        for rest, offsets in enumerate(by_residue(1, TAPS)):
+            shifted = wide_grad[rest : rest + rows + 24]
+            for offset in offsets:
+                at = offset - rest
+                tap = TAPS - offset
+                grad += params[tile, tap : tap + 1] * shifted[at : at + rows]
+        grad = live_rows * grad
+        grad_hat[tile] = grad
+        mean_one[...] += grad
+        mean_two[...] += grad * normed[tile, WIDE : WIDE + rows]
+        return carry
+
+    lax.fori_loop(0, tiles, one_tile, 0)
+    first_mean = jnp.sum(mean_one[...], axis=1, keepdims=True) * (1.0 / features)
+    second_mean = jnp.sum(mean_two[...], axis=1, keepdims=True) * (1.0 / features)
+    inv_rows = inv_scale[WIDE : WIDE + rows]
+    for tile in range(tiles):
+        cols = slice(tile * LANES, (tile + 1) * LANES)
+        inner = grad_hat[tile] - first_mean - normed[tile, WIDE : WIDE + rows] * second_mean
+        hidden_grad[:, cols] = (
+            cotan_ref[:, cols].astype(jnp.float32) + inner * inv_rows
+        ).astype(hidden_grad.dtype)
+    for tile in range(half_tiles):
+        cols = slice(tile * LANES, (tile + 1) * LANES)
+        sums_own[:, cols] = sums[side * half_tiles + tile]
+        sums_other[:, cols] = sums[(1 - side) * half_tiles + tile].astype(sums_other.dtype)
+
+
+def fast_shards(
+    query_in,
+    key_in,
+    value_in,
+    utt_lengths,
+    frames_in,
+    out_weight,
+    conv_kernel,
+    conv_bias,
+    ln_gain,
+    cotangent,
+):
+    count = lax.axis_size("ctx")
+    rows, width = query_in.shape[1], query_in.shape[2]
+    features, half = frames_in.shape[2], out_weight.shape[1]
+    place, side, core = lax.axis_index("ctx"), lax.axis_index("fsdp"), lax.axis_index("dp")
+    info = jnp.stack([place, side, core, utt_lengths[0]]).astype(jnp.int32)
+    share = width // count
+    vmem = pl.BlockSpec(memory_space=pltpu.VMEM)
+    smem = pl.BlockSpec(memory_space=pltpu.SMEM)
+    swap = [(0, 1), (1, 0)]
+
+    stacked = jnp.concatenate([query_in, key_in, value_in], axis=0)
+    pieces = [
+        lax.dynamic_slice_in_dim(stacked, lax.rem(place + step, count) * share, share, axis=2)
+        for step in range(count)
+    ]
+    out_weight_later, conv_kernel_later, _ = lax.optimization_barrier(
+        (out_weight, conv_kernel, pieces)
+    )
+    parts = [
+        piece if step == 0 else lax.ppermute(piece, "ctx", cyclic(count, step))
+        for step, piece in enumerate(pieces)
+    ]
+
+    depth = width // 2
+    w_near = lax.ppermute(
+        lax.dynamic_slice_in_dim(out_weight_later, core * depth, depth, axis=0), "fsdp", swap
+    )
+    par_own = jnp.concatenate(
+        [
+            conv_kernel_later,
+            conv_bias[None],
+            ln_gain[None],
+            jnp.zeros((PARAM_ROWS - TAPS - 2, half), jnp.float32),
+        ],
+        axis=0,
+    )
+    par_other = lax.ppermute(par_own, "fsdp", swap)
+    parts, w_near, frames_later, cotangent_later = lax.optimization_barrier(
+        (parts, w_near, frames_in, cotangent)
+    )
+    w_far = lax.ppermute(w_near, "dp", swap)
+
+    frames, cotan = frames_in[0], cotangent[0]
+    upward = jnp.concatenate(
+        [frames_later[0, rows - WIDE :], cotangent_later[0, rows - NEAR :]], axis=0
+    )
+    downward = jnp.concatenate([frames_later[0, :WIDE], cotangent_later[0, :NEAR]], axis=0)
+    below = lax.ppermute(upward, "ctx", [(i, i + 1) for i in range(count - 1)])
+    above = lax.ppermute(downward, "ctx", [(i + 1, i) for i in range(count - 1)])
+
+    replies = pl.pallas_call(
+        functools.partial(attend_kernel, count, rows),
+        name="attend",
+        out_shape=[jax.ShapeDtypeStruct((rows + 2 * WIDE, share), jnp.bfloat16)] * count,
+        in_specs=[smem] + [vmem] * count,
+        out_specs=[vmem] * count,
+        scratch_shapes=[pltpu.VMEM((count * rows, share), jnp.bfloat16)] * 3
+        + [pltpu.VMEM((count * rows + 2 * WIDE, share), jnp.bfloat16)],
+        compiler_params=pltpu.CompilerParams(vmem_limit_bytes=40 << 20),
+        cost_estimate=pl.CostEstimate(
+            flops=4 * share * (count * rows) ** 2,
+            bytes_accessed=2 * 4 * count * rows * share,
+            transcendentals=(share // HD) * (count * rows) ** 2,
+        ),
+    )(info, *parts)
+    replies = [
+        reply if step == 0 else lax.ppermute(reply, "ctx", cyclic(count, -step))
+        for step, reply in enumerate(replies)
+    ]
+
+    ext, near = rows + 2 * WIDE, rows + 2 * NEAR
+    tiles = features // LANES
+    block_out, hidden_grad, sums_own, sums_other = pl.pallas_call(
+        functools.partial(module_kernel, count),
+        name="conv_module",
+        out_shape=[
+            jax.ShapeDtypeStruct((rows, features), jnp.bfloat16),
+            jax.ShapeDtypeStruct((rows, features), jnp.bfloat16),
+            jax.ShapeDtypeStruct((TAPS + 1, half), jnp.float32),
+            jax.ShapeDtypeStruct((TAPS + 1, half), jnp.bfloat16),
+        ],
+        in_specs=[smem] + [vmem] * (count + 9),
+        out_specs=[vmem] * 4,
+        scratch_shapes=[
+            pltpu.VMEM((count, ext, share), jnp.bfloat16),
+            pltpu.VMEM((tiles, PARAM_ROWS, LANES), jnp.float32),
+            pltpu.VMEM((tiles, ext + 8, LANES), jnp.float32),
+            pltpu.VMEM((near + 8, LANES), jnp.float32),
+            pltpu.VMEM((tiles, rows, LANES), jnp.float32),
+            pltpu.VMEM((tiles, TAPS + 1, LANES), jnp.float32),
+            pltpu.VMEM((TAPS + 1, 8, LANES), jnp.float32),
+            pltpu.VMEM((rows, LANES), jnp.float32),
+            pltpu.VMEM((rows, LANES), jnp.float32),
+        ],
+        compiler_params=pltpu.CompilerParams(vmem_limit_bytes=40 << 20),
+        cost_estimate=pl.CostEstimate(
+            flops=2 * ext * width * features + 6 * TAPS * rows * features,
+            bytes_accessed=2 * width * features + 12 * rows * features,
+            transcendentals=near * features,
+        ),
+    )(info, *replies, frames, cotan, below, above, out_weight, w_near, w_far, par_own, par_other)
+
+    found = sums_own + lax.ppermute(sums_other, "fsdp", swap).astype(jnp.float32)
+    found = found + lax.ppermute(found, "dp", swap)
+    found = found.astype(jnp.bfloat16)
+    arrived = [found] + [lax.ppermute(found, "ctx", cyclic(count, step)) for step in range(1, count)]
+    found = sum(
+        lax.select_n(lax.rem(place + count - block, count), *arrived).astype(jnp.float32)
+        for block in range(count)
+    )
+    factor = 1.0 / math.sqrt(lax.axis_size("fsdp") * lax.axis_size("dp") * rows * count)
+    found = found * factor
+    grad_kernel = found[:TAPS] * ln_gain
+    grad_gain = jnp.sum(found[:TAPS] * conv_kernel, axis=0)
+    return (block_out[None], hidden_grad[None], grad_kernel, found[TAPS], grad_gain)
+
+
 def solution(mesh):
     in_specs = (
         P(("groups", "fsdp", "dp"), "ctx", None),
@@ -189,4 +523,9 @@
         P(("groups", "fsdp")),
         P(("groups", "fsdp")),
     )
+
+    def shards(*blocks):
+        run = fast_shards if fits_fast(mesh, blocks) else general_shards
+        return run(*blocks)
+
     return jax.shard_map(shards, mesh=mesh, in_specs=in_specs, out_specs=out_specs, check_vma=False)

time: 233 us -> 77.6 us (0.33)
  waiting for transfers between devices: 115 us -> 23.6 us
  blocking collectives: 46.4 us -> 0 us
  other arithmetic: 20.3 us -> 2.4 us
  starting transfers between devices: 10.9 us -> 28.1 us
  Pallas kernels: 0 us -> 16 us
  between operations: 15.2 us -> 1.53 us
  local copies, waits for them, and re-layouts: 18.4 us -> 5.57 us
  matrix products: 5.07 us -> 0 us
    all_gather x3 -> x0, waiting for transfers between devices: 90.1 us -> none  [the longest x1 40.7 us: shards(): lax.all_gather(out_weight, 'fsdp', axis=1, tiled=True)]
    psum x1 -> x0, blocking collectives: 31 us -> none  [shards(): totals = lax.psum((shares[0], shares[1], shares[2]), ('ctx', 'dp'))]
    ppermute x4 -> x16, waiting for transfers between devices: 0.01 us -> 23.6 us  [the longest x3 9.13 us: fast_shards(): lax.ppermute(piece, 'ctx', cyclic(count, step))]
    ppermute x4 -> x16, starting transfers between devices: 10.5 us -> 28.1 us  [the longest x3 7.99 us: fast_shards(): lax.ppermute(reply, 'ctx', cyclic(count, -step))]
    pallas_call x0 -> x2, Pallas kernels: none -> 16 us  [the longest x1 10.5 us: fast_shards(): pl.pallas_call(functools.partial(module_kernel, count), name='conv_module...]
    all_gather x3 -> x0, blocking collectives: 15.3 us -> none  [the longest x1 6.66 us: shards(): lax.all_gather(conv_kernel, 'fsdp', axis=1, tiled=True)]
    reduce_sum x6 -> x1, other arithmetic: 16.3 us -> 1.25 us  [fast_shards(): grad_gain = jnp.sum(found[:TAPS] * conv_kernel, axis=0)]
    unnamed x8 -> x0, waiting for transfers between devices: 13.6 us -> none
  transfers between devices with their start and end apart: 10 -> 16, of which waited for: 5 -> 8; matrix products, arithmetic and copies ran while one was open for 14% -> 2% of each run, Pallas kernels for 0% -> 7%
where the time goes in v1:
time: 77.6 us; the launch traced here: 77.3 us
  starting transfers between devices  28.1 us (36%)
  waiting for transfers between devices  23.6 us (30%)
  Pallas kernels  16 us (21%)
  local copies, waits for them, and re-layouts  5.57 us (7%)
  other arithmetic  2.4 us (3%)
  between operations  1.53 us (2%)
    pallas_call x1, Pallas kernels, fast_shards(): pl.pallas_call(functools.partial(module_kernel, count), name='conv_module...  10.5 us
    ppermute x3, waiting for transfers between devices, fast_shards(): lax.ppermute(piece, 'ctx', cyclic(count, step))  9.13 us
    ppermute x3, starting transfers between devices, fast_shards(): lax.ppermute(reply, 'ctx', cyclic(count, -step))  7.99 us
    ppermute x3, starting transfers between devices, fast_shards(): lax.ppermute(found, 'ctx', cyclic(count, step))  7.12 us
    ppermute x3, waiting for transfers between devices, fast_shards(): lax.ppermute(reply, 'ctx', cyclic(count, -step))  7.11 us
    pallas_call x1, Pallas kernels, fast_shards(): pl.pallas_call(functools.partial(attend_kernel, count, rows), name='atten...  5.54 us
    ppermute x3, starting transfers between devices, fast_shards(): lax.ppermute(piece, 'ctx', cyclic(count, step))  5.51 us
    ppermute x1, starting transfers between devices, fast_shards(): lax.ppermute(lax.dynamic_slice_in_dim(out_weight_later, core * depth, dep...  2.94 us
  transfers between devices with their start and end apart: 16, of which 8 were waited for; matrix products, arithmetic and copies ran while one was open for 2% of the time, Pallas kernels for 7%

profile of v1, /device:TPU:0, one launch (start us, length us, event | category | flops | bytes accessed | tf_op | source)
XLA Modules:
  0.0 77.3 jit_solution(14141556831190720030)
XLA Ops:
  0.7 1.1 %constant_dynamic-update-slice_fusion.2 = bf16[3,128,1024]{2,1,0:T(8,128)(2,1)S(1)} fusion(bf16[1,128,1024]{2,1,0:T(8,128)(2,1)} %param.10), kind=kLoop, calls=%fused_computation.14 | loop fusion | bytes 524288
  1.8 1.0 %constant_dynamic-update-slice_fusion.1 = bf16[3,128,1024]{2,1,0:T(8,128)(2,1)S(1)} fusion(bf16[3,128,1024]{2,1,0:T(8,128)(2,1)S(1)} %constant_dynamic-update-slice_fusion.2, bf16[1,128,1024]{2,1,0:T(8,128)(2,1)} %param.11), kind=kLoop, calls=%fused_computation.13 | loop fusion | bytes 524288
  2.8 1.0 %constant_dynamic-update-slice_fusion = bf16[3,128,1024]{2,1,0:T(8,128)(2,1)S(1)} fusion(bf16[3,128,1024]{2,1,0:T(8,128)(2,1)S(1)} %constant_dynamic-update-slice_fusion.1, bf16[1,128,1024]{2,1,0:T(8,128)(2,1)} %param.12), kind=kLoop, calls=%fused_computation.12 | loop fusion | bytes 524288 | tf_op jit(solution)/shard_map/concatenate | solution.py:399
  3.8 0.9 %constant_dynamic-slice_fusion.1 = (bf16[3,128,256]{2,1,0:T(8,128)(2,1)}, bf16[3,128,256]{2,1,0:T(8,128)(2,1)}, bf16[3,128,256]{2,1,0:T(8,128)(2,1)}, bf16[3,128,256]{2,1,0:T(8,128)(2,1)S(1)}) fusion(bf16[3,128,1024]{2,1,0:T(8,128)(2,1)S(1)} %constant_dynamic-update-slice_fusion, s32[]{:T(128)S(6)} %select_n.126, s32[]{:T(128)S(6)} %select_n.125, ...), kind=kLoop, calls=%fused_computation.17 | loop fusion | bytes 1572880 | tf_op jit(solution)/shard_map/dynamic_slice | solution.py:401
  4.6 0.9 %constant_dynamic-slice_fusion = bf16[512,768]{1,0:T(8,128)(2,1)} fusion(bf16[1024,768]{1,0:T(8,128)(2,1)S(1)} %copy-done, s32[]{:T(128)S(6)} %select_n.127), kind=kLoop, calls=%fused_computation.16 | loop fusion | bytes 1572868 | tf_op jit(solution)/shard_map/dynamic_slice | solution.py:414
  5.6 2.9 %collective-permute-start.3 = (bf16[512,768]{1,0:T(8,128)(2,1)}, bf16[512,768]{1,0:T(8,128)(2,1)S(1)}, u32[]{:S(2)}, u32[]{:S(2)}) collective-permute-start(bf16[512,768]{1,0:T(8,128)(2,1)} %constant_dynamic-slice_fusion), channel_id=1, source_target_pairs={{0,2},{2,0},{1,3},{3,1},{4,6},{6,4},{5,7},{7,5},{8,10},{10,8},{9,1... | collective-permute-start | bytes 2359304 | tf_op jit(solution)/shard_map/ppermute | solution.py:413
  8.5 1.6 %collective-permute-start = (bf16[3,128,256]{2,1,0:T(8,128)(2,1)}, bf16[3,128,256]{2,1,0:T(8,128)(2,1)}, u32[]{:S(2)}, u32[]{:S(2)}) collective-permute-start(bf16[3,128,256]{2,1,0:T(8,128)(2,1)} %get-tuple-element.41), channel_id=1, source_target_pairs={{0,4},{4,8},{8,12},{12,0},{1,5},{5,9},{9,13},{13,1},{2,6},{6,10},{... | collective-permute-start | bytes 589832 | tf_op jit(solution)/shard_map/ppermute | solution.py:408
  10.1 2.6 %collective-permute-start.1 = (bf16[3,128,256]{2,1,0:T(8,128)(2,1)}, bf16[3,128,256]{2,1,0:T(8,128)(2,1)}, u32[]{:S(2)}, u32[]{:S(2)}) collective-permute-start(bf16[3,128,256]{2,1,0:T(8,128)(2,1)} %get-tuple-element.40), channel_id=1, source_target_pairs={{0,8},{4,12},{8,0},{12,4},{1,9},{5,13},{9,1},{13,5},{2,10},{6,14},... | collective-permute-start | bytes 589832 | tf_op jit(solution)/shard_map/ppermute | solution.py:408
  12.7 1.3 %collective-permute-start.2 = (bf16[3,128,256]{2,1,0:T(8,128)(2,1)}, bf16[3,128,256]{2,1,0:T(8,128)(2,1)}, u32[]{:S(2)}, u32[]{:S(2)}) collective-permute-start(bf16[3,128,256]{2,1,0:T(8,128)(2,1)} %get-tuple-element.39), channel_id=1, source_target_pairs={{0,12},{4,0},{8,4},{12,8},{1,13},{5,1},{9,5},{13,9},{2,14},{6,2},{... | collective-permute-start | bytes 589832 | tf_op jit(solution)/shard_map/ppermute | solution.py:408
  14.1 1.0 %maximum_maximum_fusion.refs_12_ = f32[40,768]{1,0:T(8,128)S(1)} fusion(f32[1,768]{1,0:T(1,128)S(1)} %broadcast_in_dim.17, f32[1,768]{1,0:T(1,128)S(1)} %broadcast_in_dim.16, f32[31,768]{1,0:T(8,128)} %param.16, f32[40]{0:T(128)S(1)} %pad.3.clone), kind=kLoop, calls=%fused_computation.2 | loop fusion | flops 92160 | bytes 224416 | tf_op jit(solution)/shard_map/concatenate | solution.py:416
  15.1 0.6 collective-permute-start.10
  16.4 0.1 pad_add_fusion.info_ref.refs_0_
  16.4 2.1 %collective-permute-done.refs_1_ = bf16[3,128,256]{2,1,0:T(8,128)(2,1)} collective-permute-done((bf16[3,128,256]{2,1,0:T(8,128)(2,1)}, bf16[3,128,256]{2,1,0:T(8,128)(2,1)}, u32[]{:S(2)}, u32[]{:S(2)}) %collective-permute-start) | collective-permute-done | bytes 196640 | tf_op jit(solution)/shard_map/ppermute | solution.py:408
  18.6 7.0 %collective-permute-done.1.refs_2_ = bf16[3,128,256]{2,1,0:T(8,128)(2,1)} collective-permute-done((bf16[3,128,256]{2,1,0:T(8,128)(2,1)}, bf16[3,128,256]{2,1,0:T(8,128)(2,1)}, u32[]{:S(2)}, u32[]{:S(2)}) %collective-permute-start.1) | collective-permute-done | bytes 196640 | tf_op jit(solution)/shard_map/ppermute | solution.py:408
  25.6 1.5 %collective-permute-done.3.refs_10_ = bf16[512,768]{1,0:T(8,128)(2,1)S(1)} collective-permute-done((bf16[512,768]{1,0:T(8,128)(2,1)}, bf16[512,768]{1,0:T(8,128)(2,1)S(1)}, u32[]{:S(2)}, u32[]{:S(2)}) %collective-permute-start.3) | collective-permute-done | bytes 786464 | tf_op jit(solution)/shard_map/ppermute | solution.py:413
  27.2 1.3 %collective-permute-start.8 = (bf16[48,1536]{1,0:T(8,128)(2,1)S(1)}, bf16[48,1536]{1,0:T(8,128)(2,1)S(1)}, u32[]{:S(2)}, u32[]{:S(2)}) collective-permute-start(bf16[48,1536]{1,0:T(8,128)(2,1)S(1)} %pad_maximum_fusion.1), channel_id=1, source_target_pairs={{4,0},{8,4},{12,8},{5,1},{9,5},{13,9},{6,2},{10,6},{14,10},{7,3},{... | collective-permute-start | bytes 442376 | tf_op jit(solution)/shard_map/ppermute | solution.py:437
  28.5 5.5 %attend.1 = (bf16[192,256]{1,0:T(8,128)(2,1)S(1)}, bf16[192,256]{1,0:T(8,128)(2,1)S(1)}, bf16[192,256]{1,0:T(8,128)(2,1)S(1)}, bf16[192,256]{1,0:T(8,128)(2,1)S(1)}) custom-call(s32[4]{0:T(128)S(1)} %pad_add_fusion.info_ref.refs_0_, bf16[3,128,256]{2,1,0:T(8,128)(2,1)S(1)} %get-tuple-element.23.refs_0_, bf16[3,128,256]{2,1,0:T(8,128)(2,1)} %collective-permute-done.refs_1_, ...), custom_call_target="tpu_custom_call" | custom-call | flops 268435456 | bytes 1048576 | tf_op jit(solution)/shard_map/attend/pallas_call | solution.py:439
  34.1 5.3 %collective-permute-start.4 = (bf16[192,256]{1,0:T(8,128)(2,1)S(1)}, bf16[192,256]{1,0:T(8,128)(2,1)S(1)}, u32[]{:S(2)}, u32[]{:S(2)}) collective-permute-start(bf16[192,256]{1,0:T(8,128)(2,1)S(1)} %get-tuple-element.28), channel_id=1, source_target_pairs={{0,12},{4,0},{8,4},{12,8},{1,13},{5,1},{9,5},{13,9},{2,14},{6,2},{... | collective-permute-start | bytes 294920 | tf_op jit(solution)/shard_map/ppermute | solution.py:455
  39.4 1.3 %collective-permute-start.7 = (bf16[48,1536]{1,0:T(8,128)(2,1)S(1)}, bf16[48,1536]{1,0:T(8,128)(2,1)S(1)}, u32[]{:S(2)}, u32[]{:S(2)}) collective-permute-start(bf16[48,1536]{1,0:T(8,128)(2,1)S(1)} %pad_maximum_fusion), channel_id=1, source_target_pairs={{0,4},{4,8},{8,12},{1,5},{5,9},{9,13},{2,6},{6,10},{10,14},{3,7},{... | collective-permute-start | bytes 442376 | tf_op jit(solution)/shard_map/ppermute | solution.py:436
  40.7 2.7 %collective-permute-start.5 = (bf16[192,256]{1,0:T(8,128)(2,1)S(1)}, bf16[192,256]{1,0:T(8,128)(2,1)S(1)}, u32[]{:S(2)}, u32[]{:S(2)}) collective-permute-start(bf16[192,256]{1,0:T(8,128)(2,1)S(1)} %get-tuple-element.29), channel_id=1, source_target_pairs={{0,8},{4,12},{8,0},{12,4},{1,9},{5,13},{9,1},{13,5},{2,10},{6,14},... | collective-permute-start | bytes 294920 | tf_op jit(solution)/shard_map/ppermute | solution.py:455
  43.4 7.1 %collective-permute-done.5.refs_3_ = bf16[192,256]{1,0:T(8,128)(2,1)S(1)} collective-permute-done((bf16[192,256]{1,0:T(8,128)(2,1)S(1)}, bf16[192,256]{1,0:T(8,128)(2,1)S(1)}, u32[]{:S(2)}, u32[]{:S(2)}) %collective-permute-start.5) | collective-permute-done | bytes 98336 | tf_op jit(solution)/shard_map/ppermute | solution.py:455
  50.6 10.5 %conv_module.1 = (bf16[128,1536]{1,0:T(8,128)(2,1)}, bf16[128,1536]{1,0:T(8,128)(2,1)}, f32[32,768]{1,0:T(8,128)S(1)}, bf16[32,768]{1,0:T(8,128)(2,1)S(1)}) custom-call(s32[4]{0:T(128)S(1)} %pad_add_fusion.info_ref.refs_0_, bf16[192,256]{1,0:T(8,128)(2,1)S(1)} %get-tuple-element.27.refs_1_, bf16[192,256]{1,0:T(8,128)(2,1)S(1)} %collective-permute-done.4.refs_2_, ...), custom_call_target="tpu_custom_call" | custom-call | flops 640548864 | bytes 5505024 | tf_op jit(solution)/shard_map/conv_module/pallas_call | solution.py:461
  61.1 1.2 %collective-permute-start.11 = (bf16[32,768]{1,0:T(8,128)(2,1)S(1)}, bf16[32,768]{1,0:T(8,128)(2,1)S(1)}, u32[]{:S(2)}, u32[]{:S(2)}) collective-permute-start(bf16[32,768]{1,0:T(8,128)(2,1)S(1)} %get-tuple-element.38), channel_id=1, source_target_pairs={{0,2},{2,0},{1,3},{3,1},{4,6},{6,4},{5,7},{7,5},{8,10},{10,8},{9,1... | collective-permute-start | bytes 147464 | tf_op jit(solution)/shard_map/ppermute | solution.py:491
  62.3 2.8 %collective-permute-done.11 = bf16[32,768]{1,0:T(8,128)(2,1)S(1)} collective-permute-done((bf16[32,768]{1,0:T(8,128)(2,1)S(1)}, bf16[32,768]{1,0:T(8,128)(2,1)S(1)}, u32[]{:S(2)}, u32[]{:S(2)}) %collective-permute-start.11) | collective-permute-done | bytes 49184 | tf_op jit(solution)/shard_map/ppermute | solution.py:491
  65.2 1.3 %collective-permute-done.12 = f32[32,768]{1,0:T(8,128)S(1)} collective-permute-done((f32[32,768]{1,0:T(8,128)S(1)}, f32[32,768]{1,0:T(8,128)S(1)}, u32[]{:S(2)}, u32[]{:S(2)}) %collective-permute-start.12) | collective-permute-done | bytes 98336 | tf_op jit(solution)/shard_map/ppermute | solution.py:492
  66.5 2.3 %collective-permute-start.13 = (bf16[32,768]{1,0:T(8,128)(2,1)S(1)}, bf16[32,768]{1,0:T(8,128)(2,1)S(1)}, u32[]{:S(2)}, u32[]{:S(2)}) collective-permute-start(bf16[32,768]{1,0:T(8,128)(2,1)S(1)} %add_convert_fusion), channel_id=1, source_target_pairs={{0,4},{4,8},{8,12},{12,0},{1,5},{5,9},{9,13},{13,1},{2,6},{6,10},{... | collective-permute-start | bytes 147464 | tf_op jit(solution)/shard_map/ppermute | solution.py:494
  68.8 2.0 %collective-permute-start.14 = (bf16[32,768]{1,0:T(8,128)(2,1)S(1)}, bf16[32,768]{1,0:T(8,128)(2,1)S(1)}, u32[]{:S(2)}, u32[]{:S(2)}) collective-permute-start(bf16[32,768]{1,0:T(8,128)(2,1)S(1)} %add_convert_fusion), channel_id=1, source_target_pairs={{0,8},{4,12},{8,0},{12,4},{1,9},{5,13},{9,1},{13,5},{2,10},{6,14},... | collective-permute-start | bytes 147464 | tf_op jit(solution)/shard_map/ppermute | solution.py:494
  70.8 2.8 %collective-permute-start.15 = (bf16[32,768]{1,0:T(8,128)(2,1)S(1)}, bf16[32,768]{1,0:T(8,128)(2,1)S(1)}, u32[]{:S(2)}, u32[]{:S(2)}) collective-permute-start(bf16[32,768]{1,0:T(8,128)(2,1)S(1)} %add_convert_fusion), channel_id=1, source_target_pairs={{0,12},{4,0},{8,4},{12,8},{1,13},{5,1},{9,5},{13,9},{2,14},{6,2},{... | collective-permute-start | bytes 147464 | tf_op jit(solution)/shard_map/ppermute | solution.py:494
  73.7 1.2 %collective-permute-done.14 = bf16[32,768]{1,0:T(8,128)(2,1)S(1)} collective-permute-done((bf16[32,768]{1,0:T(8,128)(2,1)S(1)}, bf16[32,768]{1,0:T(8,128)(2,1)S(1)}, u32[]{:S(2)}, u32[]{:S(2)}) %collective-permute-start.14) | collective-permute-done | bytes 49184 | tf_op jit(solution)/shard_map/ppermute | solution.py:494
  74.9 0.5 collective-permute-done.15
  75.5 1.3 %multiply_reduce_fusion = (f32[768]{0:T(1024)}, f32[31,768]{1,0:T(8,128)}) fusion(f32[31,768]{1,0:T(8,128)S(1)} %copy-done.3, f32[32,768]{1,0:T(8,128)S(1)} %add_multiply_fusion, f32[768]{0:T(1024)S(1)} %copy-done.4), kind=kLoop, calls=%fused_computation.3 | loop fusion | flops 70656 | bytes 291840 | tf_op jit(solution)/shard_map/reduce_sum | solution.py:502
  76.7 0.6 slice_reduce_fusion
  (34 shorter events, 0.4 us)
Async XLA Ops:
  0.7 4.0 %copy-start = (bf16[1024,768]{1,0:T(8,128)(2,1)S(1)}, bf16[1024,768]{1,0:T(8,128)(2,1)}, u32[]{:S(2)}) copy-start(bf16[1024,768]{1,0:T(8,128)(2,1)} %refs_9_.1) | copy-start | bytes 4718596
  3.7 10.3 %copy-start.5 = (f32[768]{0:T(1024)S(1)}, f32[768]{0:T(1024)}, u32[]{:S(2)}) copy-start(f32[768]{0:T(1024)} %param.17) | copy-start | bytes 9220
  3.7 10.3 %copy-start.4 = (f32[768]{0:T(1024)S(1)}, f32[768]{0:T(1024)}, u32[]{:S(2)}) copy-start(f32[768]{0:T(1024)} %param.18) | copy-start | bytes 9220
  3.8 23.3 %copy-start.1 = (bf16[1,128,1536]{2,1,0:T(8,128)(2,1)S(1)}, bf16[1,128,1536]{2,1,0:T(8,128)(2,1)}, u32[]{:S(2)}) copy-start(bf16[1,128,1536]{2,1,0:T(8,128)(2,1)} %param.14) | copy-start | bytes 1179652
  3.8 23.4 %copy-start.2 = (bf16[1,128,1536]{2,1,0:T(8,128)(2,1)S(1)}, bf16[1,128,1536]{2,1,0:T(8,128)(2,1)}, u32[]{:S(2)}) copy-start(bf16[1,128,1536]{2,1,0:T(8,128)(2,1)} %param.19) | copy-start | bytes 1179652
  5.6 21.5 %collective-permute-start.3 = (bf16[512,768]{1,0:T(8,128)(2,1)}, bf16[512,768]{1,0:T(8,128)(2,1)S(1)}, u32[]{:S(2)}, u32[]{:S(2)}) collective-permute-start(bf16[512,768]{1,0:T(8,128)(2,1)} %constant_dynamic-slice_fusion), channel_id=1, source_target_pairs={{0,2},{2,0},{1,3},{3,1},{4,6},{6,4},{5,7},{7,5},{8,10},{10,8},{9,1... | collective-permute-start | bytes 2359304 | tf_op jit(solution)/shard_map/ppermute | solution.py:413
  8.5 10.0 %collective-permute-start = (bf16[3,128,256]{2,1,0:T(8,128)(2,1)}, bf16[3,128,256]{2,1,0:T(8,128)(2,1)}, u32[]{:S(2)}, u32[]{:S(2)}) collective-permute-start(bf16[3,128,256]{2,1,0:T(8,128)(2,1)} %get-tuple-element.41), channel_id=1, source_target_pairs={{0,4},{4,8},{8,12},{12,0},{1,5},{5,9},{9,13},{13,1},{2,6},{6,10},{... | collective-permute-start | bytes 589832 | tf_op jit(solution)/shard_map/ppermute | solution.py:408
  10.1 15.5 %collective-permute-start.1 = (bf16[3,128,256]{2,1,0:T(8,128)(2,1)}, bf16[3,128,256]{2,1,0:T(8,128)(2,1)}, u32[]{:S(2)}, u32[]{:S(2)}) collective-permute-start(bf16[3,128,256]{2,1,0:T(8,128)(2,1)} %get-tuple-element.40), channel_id=1, source_target_pairs={{0,8},{4,12},{8,0},{12,4},{1,9},{5,13},{9,1},{13,5},{2,10},{6,14},... | collective-permute-start | bytes 589832 | tf_op jit(solution)/shard_map/ppermute | solution.py:408
  12.7 12.9 %collective-permute-start.2 = (bf16[3,128,256]{2,1,0:T(8,128)(2,1)}, bf16[3,128,256]{2,1,0:T(8,128)(2,1)}, u32[]{:S(2)}, u32[]{:S(2)}) collective-permute-start(bf16[3,128,256]{2,1,0:T(8,128)(2,1)} %get-tuple-element.39), channel_id=1, source_target_pairs={{0,12},{4,0},{8,4},{12,8},{1,13},{5,1},{9,5},{13,9},{2,14},{6,2},{... | collective-permute-start | bytes 589832 | tf_op jit(solution)/shard_map/ppermute | solution.py:408
  15.1 25.6 %collective-permute-start.10 = (f32[40,768]{1,0:T(8,128)S(1)}, f32[40,768]{1,0:T(8,128)}, u32[]{:S(2)}, u32[]{:S(2)}) collective-permute-start(f32[40,768]{1,0:T(8,128)S(1)} %maximum_maximum_fusion.refs_12_), channel_id=1, source_target_pairs={{0,2},{2,0},{1,3},{3,1},{4,6},{6,4},{5,7},{7,5},{8,10},{10,8},{9,1... | collective-permute-start | bytes 368648 | tf_op jit(solution)/shard_map/ppermute | solution.py:425
  27.1 23.4 %collective-permute-start.9 = (bf16[512,768]{1,0:T(8,128)(2,1)S(1)}, bf16[512,768]{1,0:T(8,128)(2,1)S(1)}, u32[]{:S(2)}, u32[]{:S(2)}) collective-permute-start(bf16[512,768]{1,0:T(8,128)(2,1)S(1)} %collective-permute-done.3.refs_10_), channel_id=1, source_target_pairs={{0,1},{1,0},{2,3},{3,2},{4,5},{5,4},{6,7},{7,6},{8,9},{9,8},{10,11... | collective-permute-start | bytes 2359304 | tf_op jit(solution)/shard_map/ppermute | solution.py:429
  27.2 23.3 %collective-permute-start.8 = (bf16[48,1536]{1,0:T(8,128)(2,1)S(1)}, bf16[48,1536]{1,0:T(8,128)(2,1)S(1)}, u32[]{:S(2)}, u32[]{:S(2)}) collective-permute-start(bf16[48,1536]{1,0:T(8,128)(2,1)S(1)} %pad_maximum_fusion.1), channel_id=1, source_target_pairs={{4,0},{8,4},{12,8},{5,1},{9,5},{13,9},{6,2},{10,6},{14,10},{7,3},{... | collective-permute-start | bytes 442376 | tf_op jit(solution)/shard_map/ppermute | solution.py:437
  34.1 9.3 %collective-permute-start.4 = (bf16[192,256]{1,0:T(8,128)(2,1)S(1)}, bf16[192,256]{1,0:T(8,128)(2,1)S(1)}, u32[]{:S(2)}, u32[]{:S(2)}) collective-permute-start(bf16[192,256]{1,0:T(8,128)(2,1)S(1)} %get-tuple-element.28), channel_id=1, source_target_pairs={{0,12},{4,0},{8,4},{12,8},{1,13},{5,1},{9,5},{13,9},{2,14},{6,2},{... | collective-permute-start | bytes 294920 | tf_op jit(solution)/shard_map/ppermute | solution.py:455
  39.4 11.1 %collective-permute-start.7 = (bf16[48,1536]{1,0:T(8,128)(2,1)S(1)}, bf16[48,1536]{1,0:T(8,128)(2,1)S(1)}, u32[]{:S(2)}, u32[]{:S(2)}) collective-permute-start(bf16[48,1536]{1,0:T(8,128)(2,1)S(1)} %pad_maximum_fusion), channel_id=1, source_target_pairs={{0,4},{4,8},{8,12},{1,5},{5,9},{9,13},{2,6},{6,10},{10,14},{3,7},{... | collective-permute-start | bytes 442376 | tf_op jit(solution)/shard_map/ppermute | solution.py:436
  40.7 9.8 %collective-permute-start.5 = (bf16[192,256]{1,0:T(8,128)(2,1)S(1)}, bf16[192,256]{1,0:T(8,128)(2,1)S(1)}, u32[]{:S(2)}, u32[]{:S(2)}) collective-permute-start(bf16[192,256]{1,0:T(8,128)(2,1)S(1)} %get-tuple-element.29), channel_id=1, source_target_pairs={{0,8},{4,12},{8,0},{12,4},{1,9},{5,13},{9,1},{13,5},{2,10},{6,14},... | collective-permute-start | bytes 294920 | tf_op jit(solution)/shard_map/ppermute | solution.py:455
  43.4 7.1 %collective-permute-start.6 = (bf16[192,256]{1,0:T(8,128)(2,1)S(1)}, bf16[192,256]{1,0:T(8,128)(2,1)S(1)}, u32[]{:S(2)}, u32[]{:S(2)}) collective-permute-start(bf16[192,256]{1,0:T(8,128)(2,1)S(1)} %get-tuple-element.30), channel_id=1, source_target_pairs={{0,4},{4,8},{8,12},{12,0},{1,5},{5,9},{9,13},{13,1},{2,6},{6,10},{... | collective-permute-start | bytes 294920 | tf_op jit(solution)/shard_map/ppermute | solution.py:455
  50.5 24.9 %copy-start.3 = (f32[31,768]{1,0:T(8,128)S(1)}, f32[31,768]{1,0:T(8,128)}, u32[]{:S(2)}) copy-start(f32[31,768]{1,0:T(8,128)} %param.16) | copy-start | bytes 285700
  61.1 4.1 %collective-permute-start.11 = (bf16[32,768]{1,0:T(8,128)(2,1)S(1)}, bf16[32,768]{1,0:T(8,128)(2,1)S(1)}, u32[]{:S(2)}, u32[]{:S(2)}) collective-permute-start(bf16[32,768]{1,0:T(8,128)(2,1)S(1)} %get-tuple-element.38), channel_id=1, source_target_pairs={{0,2},{2,0},{1,3},{3,1},{4,6},{6,4},{5,7},{7,5},{8,10},{10,8},{9,1... | collective-permute-start | bytes 147464 | tf_op jit(solution)/shard_map/ppermute | solution.py:491
  65.2 1.4 %collective-permute-start.12 = (f32[32,768]{1,0:T(8,128)S(1)}, f32[32,768]{1,0:T(8,128)S(1)}, u32[]{:S(2)}, u32[]{:S(2)}) collective-permute-start(f32[32,768]{1,0:T(8,128)S(1)} %convert_add_fusion), channel_id=1, source_target_pairs={{0,1},{1,0},{2,3},{3,2},{4,5},{5,4},{6,7},{7,6},{8,9},{9,8},{10,11... | collective-permute-start | bytes 294920 | tf_op jit(solution)/shard_map/ppermute | solution.py:492
  66.5 7.1 %collective-permute-start.13 = (bf16[32,768]{1,0:T(8,128)(2,1)S(1)}, bf16[32,768]{1,0:T(8,128)(2,1)S(1)}, u32[]{:S(2)}, u32[]{:S(2)}) collective-permute-start(bf16[32,768]{1,0:T(8,128)(2,1)S(1)} %add_convert_fusion), channel_id=1, source_target_pairs={{0,4},{4,8},{8,12},{12,0},{1,5},{5,9},{9,13},{13,1},{2,6},{6,10},{... | collective-permute-start | bytes 147464 | tf_op jit(solution)/shard_map/ppermute | solution.py:494
  68.8 6.1 %collective-permute-start.14 = (bf16[32,768]{1,0:T(8,128)(2,1)S(1)}, bf16[32,768]{1,0:T(8,128)(2,1)S(1)}, u32[]{:S(2)}, u32[]{:S(2)}) collective-permute-start(bf16[32,768]{1,0:T(8,128)(2,1)S(1)} %add_convert_fusion), channel_id=1, source_target_pairs={{0,8},{4,12},{8,0},{12,4},{1,9},{5,13},{9,1},{13,5},{2,10},{6,14},... | collective-permute-start | bytes 147464 | tf_op jit(solution)/shard_map/ppermute | solution.py:494
  70.8 4.6 %collective-permute-start.15 = (bf16[32,768]{1,0:T(8,128)(2,1)S(1)}, bf16[32,768]{1,0:T(8,128)(2,1)S(1)}, u32[]{:S(2)}, u32[]{:S(2)}) collective-permute-start(bf16[32,768]{1,0:T(8,128)(2,1)S(1)} %add_convert_fusion), channel_id=1, source_target_pairs={{0,12},{4,0},{8,4},{12,8},{1,13},{5,1},{9,5},{13,9},{2,14},{6,2},{... | collective-permute-start | bytes 147464 | tf_op jit(solution)/shard_map/ppermute | solution.py:494

commit v2 on v1

--- a/solution.py
+++ b/solution.py
@@ -15,6 +15,9 @@
 WIDE = 32
 NEAR = 16
 PARAM_ROWS = 40
+SHARE = 256
+QUERY_ROWS = 128
+CHUNKS = SHARE // LANES
 
 NEG_FILL = -1e30
 
@@ -184,30 +187,109 @@
         query_in.shape[0] == 1
         and mesh.shape["fsdp"] == 2
         and mesh.shape["dp"] == 2
-        and ctx_count > 1
-        and width % (ctx_count * LANES) == 0
-        and rows % LANES == 0
+        and ctx_count == 4
+        and width == ctx_count * SHARE
+        and rows == LANES
         and frames_in.shape[2] == 2 * out_weight.shape[1]
-        and out_weight.shape[1] % LANES == 0
-        and (ctx_count * rows) <= 1024
-    )
-
-
-def cyclic(count, step):
-    return [(i, (i + step) % count) for i in range(count)]
-
-
-def attend_kernel(count, rows, info_ref, *refs):
-    parts, outs = refs[:count], refs[count : 2 * count]
-    query_all, key_all, value_all, attended = refs[2 * count :]
-    place, valid_len = info_ref[0], info_ref[3]
+        and out_weight.shape[1] % SHARE == 0
+    )
+
+
+def facing(count, step):
+    return [(i, i ^ step) for i in range(count)]
+
+
+def pack_kernel(*refs):
+    (
+        query_ref, key_ref, value_ref, frames_ref, cotan_ref, weight_ref, taps_ref, bias_ref, gain_ref,
+        *outs,
+    ) = refs[: 9 + 3 * CHUNKS + 2]
+    whole, edges, taps, bias, gain, in_sems = refs[-6:]
+    *outs, edge, weight_out = outs
+    place, core = lax.axis_index("ctx"), lax.axis_index("dp")
+    rows = query_ref.shape[1]
+    depth = weight_out.shape[0] - 2 * PARAM_ROWS
+    arriving = []
+
+    def fetch(source, target):
+        arriving.append(pltpu.make_async_copy(source, target, in_sems.at[len(arriving)]))
+        arriving[-1].start()
+
+    per_input = rows // NEAR // 2
+    for which, source in enumerate((query_ref, key_ref, value_ref)):
+        for part in range(per_input):
+            span = slice(part * 2 * NEAR, (part + 1) * 2 * NEAR)
+            fetch(source.at[0, span, :], whole.at[which, span, :])
+    odd = lax.rem(place, 2)
+    for side in range(2):
+        high = odd if side else 1 - odd
+        wide = pl.multiple_of(high * (rows - WIDE), WIDE)
+        near = pl.multiple_of(high * (rows - NEAR), NEAR)
+        fetch(frames_ref.at[0, pl.ds(wide, WIDE), :], edges.at[side, 0:WIDE, :])
+        fetch(cotan_ref.at[0, pl.ds(near, NEAR), :], edges.at[side, WIDE : WIDE + NEAR, :])
+    for part in range(0, depth, 64):
+        first = pl.multiple_of(core * depth + part, 64)
+        fetch(weight_ref.at[pl.ds(first, 64), :], weight_out.at[part : part + 64, :])
+    for source, target in ((taps_ref, taps), (bias_ref, bias), (gain_ref, gain)):
+        fetch(source, target)
+    for which in range(3):
+        for part in range(per_input):
+            arriving[which * per_input + part].wait()
+        at = slice(which * rows, (which + 1) * rows)
+        for index, out in enumerate(outs):
+            first = (place ^ (index % 3 + 1)) * SHARE + index // 3 * LANES
+            out[at, :] = whole[which, :, pl.ds(pl.multiple_of(first, LANES), LANES)]
+    seen = 3 * per_input
+    for copy in arriving[seen : seen + 4]:
+        copy.wait()
+    for block in range(edges.shape[2] // LANES):
+        base = 3 * rows + block * (WIDE + NEAR)
+        outs[0][base : base + WIDE + NEAR, :] = edges[0, :, block * LANES : (block + 1) * LANES]
+    edge[...] = edges[1]
+    for copy in arriving[-3:]:
+        copy.wait()
+    params = parameters(taps, bias, gain)
+    rounded = params.astype(jnp.bfloat16)
+    weight_out[depth : depth + PARAM_ROWS, :] = rounded
+    weight_out[depth + PARAM_ROWS :, :] = (params - rounded.astype(jnp.float32)).astype(jnp.bfloat16)
+    for copy in arriving[seen + 4 : -3]:
+        copy.wait()
+
+
+def parameters(taps_ref, bias_ref, gain_ref):
+    half = taps_ref.shape[1]
+    return jnp.concatenate(
+        [
+            taps_ref[...],
+            bias_ref[...].reshape(1, half),
+            gain_ref[...].reshape(1, half),
+            jnp.zeros((PARAM_ROWS - TAPS - 2, half), jnp.float32),
+        ],
+        axis=0,
+    )
+
+
+def attend_kernel(chunk, length_ref, query_ref, key_ref, value_ref, *refs):
+    parts, outs = refs[:3], refs[3:7]
+    query_all, key_all, value_all, attended, sems = refs[7:]
+    place, valid_len = lax.axis_index("ctx"), length_ref[0]
     frames, width = query_all.shape
-    for step in range(count):
-        owner = lax.rem(place + count - step, count)
-        span = pl.ds(pl.multiple_of(owner * rows, rows), rows)
-        query_all[span, :] = parts[step][0]
-        key_all[span, :] = parts[step][1]
-        value_all[span, :] = parts[step][2]
+    rows = frames // 4
+    targets = (query_all, key_all, value_all)
+    mine = pl.ds(pl.multiple_of(place * rows, rows), rows)
+    heads = pl.ds(pl.multiple_of(place * SHARE + chunk * LANES, LANES), LANES)
+    copies = [
+        pltpu.make_async_copy(source.at[0, :, heads], target.at[mine, :], sems.at[which])
+        for which, (source, target) in enumerate(zip((query_ref, key_ref, value_ref), targets))
+    ]
+    for copy in copies:
+        copy.start()
+    for step, part in enumerate(parts, 1):
+        span = pl.ds(pl.multiple_of((place ^ step) * rows, rows), rows)
+        for which, target in enumerate(targets):
+            target[span, :] = part[which * rows : (which + 1) * rows, :]
+    for copy in copies:
+        copy.wait()
     attended[0:WIDE, :] = jnp.zeros((WIDE, width), attended.dtype)
     attended[WIDE + frames : 2 * WIDE + frames, :] = jnp.zeros((WIDE, width), attended.dtype)
     usable = lax.broadcasted_iota(jnp.int32, (1, frames), 1) < valid_len
@@ -215,14 +297,14 @@
     for pair in range(width // LANES):
         cols = slice(pair * LANES, (pair + 1) * LANES)
         keys, values = key_all[:, cols], value_all[:, cols]
-        own = [
+        heads = [
             (jnp.where(mine, keys, 0).astype(keys.dtype), jnp.where(mine, values, 0).astype(values.dtype))
             for mine in (lane < HD, lane >= HD)
         ]
-        for start in range(0, frames, rows):
-            queries = query_all[start : start + rows, cols]
-            total = jnp.zeros((rows, LANES), jnp.float32)
-            for key_head, value_head in own:
+        for start in range(0, frames, QUERY_ROWS):
+            queries = query_all[start : start + QUERY_ROWS, cols]
+            total = jnp.zeros((QUERY_ROWS, LANES), jnp.float32)
+            for key_head, value_head in heads:
                 scores = lax.dot_general(
                     queries, key_head, (((1,), (1,)), ((), ())), preferred_element_type=jnp.float32
                 ) * (1.0 / math.sqrt(HD))
@@ -235,9 +317,9 @@
                     )
                     / sums
                 )
-            attended[WIDE + start : WIDE + start + rows, cols] = total.astype(attended.dtype)
-    for step in range(count):
-        owner = lax.rem(place + count - step, count)
+            attended[WIDE + start : WIDE + start + QUERY_ROWS, cols] = total.astype(attended.dtype)
+    for step in range(4):
+        owner = place ^ step
         outs[step][...] = attended[pl.ds(pl.multiple_of(owner * rows, rows), rows + 2 * WIDE), :]
 
 
@@ -245,27 +327,42 @@
     return [[o for o in range(first, last + 1) if o % 8 == r] for r in range(8)]
 
 
-def module_kernel(count, *refs):
-    info_ref, *replies = refs[: 1 + count]
+def module_kernel(*refs):
+    count = 4
+    length_ref, *replies = refs[: 1 + count * CHUNKS]
     (
-        frames_ref, cotan_ref, below_ref, above_ref, w_own, w_near, w_far, par_own, par_other,
-        block_out, hidden_grad, sums_own, sums_other,
-        attended, params, normed, wide_grad, grad_hat, sums, partial, mean_one, mean_two,
-    ) = refs[1 + count :]
-    place, side, core, valid_len = info_ref[0], info_ref[1], info_ref[2], info_ref[3]
+        frames_ref, cotan_ref, beside_ref, edge_ref, w_own, w_near, w_far, taps_ref, bias_ref, gain_ref,
+        block_hbm, normed, wide_grad, params, inv_rows, sums_own, sums_other, par_mine,
+        edges, attended, sums, partial, block_out, out_sems,
+    ) = refs[1 + count * CHUNKS :]
+    place, side, core = lax.axis_index("ctx"), lax.axis_index("fsdp"), lax.axis_index("dp")
+    valid_len = length_ref[0]
     rows, features = frames_ref.shape
     half = features // 2
     tiles, half_tiles = features // LANES, half // LANES
     ext, near = rows + 2 * WIDE, rows + 2 * NEAR
-    depth = replies[0].shape[1]
-    per_part = w_near.shape[0] // depth
+    depth = SHARE
+    weight_rows = w_near.shape[0] - 2 * PARAM_ROWS
+    per_part = weight_rows // depth
+
+    even = 1 - lax.rem(place, 2)
+    for block in range(features // LANES):
+        base = 3 * rows + block * (WIDE + NEAR)
+        edges[even, :, block * LANES : (block + 1) * LANES] = beside_ref[base : base + WIDE + NEAR, :]
+    edges[1 - even] = edge_ref[...]
 
     def live(first, length):
         position = place * rows + first + lax.broadcasted_iota(jnp.int32, (length, 1), 0)
         return ((position >= 0) & (position < valid_len)).astype(jnp.float32)
 
     for step in range(count):
-        attended[lax.rem(place + step, count)] = replies[step][...]
+        for chunk in range(CHUNKS):
+            cols = slice(chunk * LANES, (chunk + 1) * LANES)
+            attended[place ^ step, :, cols] = replies[chunk * count + step][...]
+    par_own = parameters(taps_ref, bias_ref, gain_ref)
+    par_mine[...] = par_own
+    par_other = w_near[weight_rows : weight_rows + PARAM_ROWS, :].astype(jnp.float32)
+    par_other += w_near[weight_rows + PARAM_ROWS :, :].astype(jnp.float32)
     for tile in range(half_tiles):
         cols = slice(tile * LANES, (tile + 1) * LANES)
         for source, base in ((par_own, side * half_tiles), (par_other, (1 - side) * half_tiles)):
@@ -290,7 +387,7 @@
                     weight = source[inner * depth : (inner + 1) * depth, cols]
                 product += jnp.dot(attended[index], weight, preferred_element_type=jnp.float32)
             residual = jnp.concatenate(
-                [below_ref[0:WIDE, span], frames_ref[:, span], above_ref[0:WIDE, span]], axis=0
+                [edges[0, 0:WIDE, span], frames_ref[:, span], edges[1, 0:WIDE, span]], axis=0
             )
             hidden = (residual.astype(jnp.float32) + product).astype(jnp.bfloat16)
             block_out[:, span] = hidden[WIDE : WIDE + rows]
@@ -312,8 +409,7 @@
 
     live_near = live(-NEAR, near)
     live_rows = live(0, rows)
-    mean_one[...] = jnp.zeros_like(mean_one)
-    mean_two[...] = jnp.zeros_like(mean_two)
+    inv_rows[...] = jnp.broadcast_to(inv_scale[WIDE : WIDE + rows], inv_rows.shape)
 
     def one_tile(tile, carry):
         span = pl.ds(pl.multiple_of(tile * LANES, LANES), LANES)
@@ -328,11 +424,14 @@
         block_out[:, span] = (
             block_out[:, span].astype(jnp.float32) + live_rows * (pre_act * gate)[here]
         ).astype(block_out.dtype)
+        pltpu.make_async_copy(
+            block_out.at[:, span], block_hbm.at[:, span], out_sems.at[tile]
+        ).start()
         cotan = jnp.concatenate(
-            [below_ref[WIDE:, span], cotan_ref[:, span], above_ref[WIDE:, span]], axis=0
+            [edges[0, WIDE:, span], cotan_ref[:, span], edges[1, WIDE:, span]], axis=0
         ).astype(jnp.float32)
         grad_pre = cotan * live_near * gate * (1.0 + pre_act * (1.0 - gate))
-        wide_grad[0:near] = grad_pre
+        wide_grad[tile, 0:near] = grad_pre
         own_grad = grad_pre[here]
         first = WIDE - HALF
         for rest, offsets in enumerate(by_residue(first, first + TAPS - 1)):
@@ -345,9 +444,30 @@
                 )
         partial[TAPS] = jnp.sum(own_grad.reshape(rows // 8, 8, LANES), axis=0)
         sums[tile] = jnp.sum(partial[...], axis=1)
+        return carry
+
+    lax.fori_loop(0, tiles, one_tile, 0)
+    for tile in range(half_tiles):
+        cols = slice(tile * LANES, (tile + 1) * LANES)
+        sums_own[:, cols] = sums[side * half_tiles + tile].astype(sums_own.dtype)
+        sums_other[:, cols] = sums[(1 - side) * half_tiles + tile].astype(sums_other.dtype)
+    for tile in range(tiles):
+        cols = slice(tile * LANES, (tile + 1) * LANES)
+        pltpu.make_async_copy(block_out.at[:, cols], block_hbm.at[:, cols], out_sems.at[tile]).wait()
+
+
+def backward_kernel(length_ref, cotan_ref, normed, wide_grad, params, inv_rows, grad_hbm, grad_hat, mean_one, mean_two, hidden_grad, out_sems):
+    rows, features = cotan_ref.shape
+    tiles = features // LANES
+    position = lax.axis_index("ctx") * rows + lax.broadcasted_iota(jnp.int32, (rows, 1), 0)
+    live_rows = (position < length_ref[0]).astype(jnp.float32)
+    mean_one[...] = jnp.zeros_like(mean_one)
+    mean_two[...] = jnp.zeros_like(mean_two)
+
+    def one_tile(tile, carry):
         grad = jnp.zeros((rows, LANES), jnp.float32)
         for rest, offsets in enumerate(by_residue(1, TAPS)):
-            shifted = wide_grad[rest : rest + rows + 24]
+            shifted = wide_grad[tile, rest : rest + rows + 24]
             for offset in offsets:
                 at = offset - rest
                 tap = TAPS - offset
@@ -361,17 +481,26 @@
     lax.fori_loop(0, tiles, one_tile, 0)
     first_mean = jnp.sum(mean_one[...], axis=1, keepdims=True) * (1.0 / features)
     second_mean = jnp.sum(mean_two[...], axis=1, keepdims=True) * (1.0 / features)
-    inv_rows = inv_scale[WIDE : WIDE + rows]
     for tile in range(tiles):
         cols = slice(tile * LANES, (tile + 1) * LANES)
         inner = grad_hat[tile] - first_mean - normed[tile, WIDE : WIDE + rows] * second_mean
         hidden_grad[:, cols] = (
-            cotan_ref[:, cols].astype(jnp.float32) + inner * inv_rows
+            cotan_ref[:, cols].astype(jnp.float32) + inner * inv_rows[...]
         ).astype(hidden_grad.dtype)
-    for tile in range(half_tiles):
+        pltpu.make_async_copy(hidden_grad.at[:, cols], grad_hbm.at[:, cols], out_sems.at[tile]).start()
+    for tile in range(tiles):
         cols = slice(tile * LANES, (tile + 1) * LANES)
-        sums_own[:, cols] = sums[side * half_tiles + tile]
-        sums_other[:, cols] = sums[(1 - side) * half_tiles + tile].astype(sums_other.dtype)
+        pltpu.make_async_copy(hidden_grad.at[:, cols], grad_hbm.at[:, cols], out_sems.at[tile]).wait()
+
+
+def finish_kernel(factor, mine, one, two, three, params, kernel_out, bias_out, gain_out, terms):
+    place = lax.axis_index("ctx")
+    for step, source in enumerate((mine, one, two, three)):
+        terms[place ^ step] = source[...].astype(jnp.float32)
+    total = (((terms[0] + terms[1]) + terms[2]) + terms[3]) * factor
+    kernel_out[...] = total[:TAPS] * params[TAPS + 1 : TAPS + 2]
+    bias_out[...] = total[TAPS]
+    gain_out[...] = jnp.sum(total[:TAPS] * params[:TAPS], axis=0)
 
 
 def fast_shards(
@@ -389,118 +518,168 @@
     count = lax.axis_size("ctx")
     rows, width = query_in.shape[1], query_in.shape[2]
     features, half = frames_in.shape[2], out_weight.shape[1]
-    place, side, core = lax.axis_index("ctx"), lax.axis_index("fsdp"), lax.axis_index("dp")
-    info = jnp.stack([place, side, core, utt_lengths[0]]).astype(jnp.int32)
-    share = width // count
+    place = lax.axis_index("ctx")
     vmem = pl.BlockSpec(memory_space=pltpu.VMEM)
     smem = pl.BlockSpec(memory_space=pltpu.SMEM)
+    hbm = pl.BlockSpec(memory_space=pltpu.HBM)
     swap = [(0, 1), (1, 0)]
 
-    stacked = jnp.concatenate([query_in, key_in, value_in], axis=0)
-    pieces = [
-        lax.dynamic_slice_in_dim(stacked, lax.rem(place + step, count) * share, share, axis=2)
-        for step in range(count)
+    ends = (features // LANES) * (WIDE + NEAR)
+    sent = [
+        (3 * rows + ends, LANES),
+        *[(3 * rows, LANES)] * (3 * CHUNKS - 1),
+        (WIDE + NEAR, features),
+        (width // 2 + 2 * PARAM_ROWS, half),
     ]
-    out_weight_later, conv_kernel_later, _ = lax.optimization_barrier(
-        (out_weight, conv_kernel, pieces)
+    *pieces, edge, w_sent = pl.pallas_call(
+        pack_kernel,
+        name="pack",
+        out_shape=[jax.ShapeDtypeStruct(shape, jnp.bfloat16) for shape in sent],
+        in_specs=[hbm] * 9,
+        out_specs=[vmem] * len(sent),
+        scratch_shapes=[
+            pltpu.VMEM((3, rows, width), jnp.bfloat16),
+            pltpu.VMEM((2, WIDE + NEAR, features), jnp.bfloat16),
+            pltpu.VMEM((TAPS, half), jnp.float32),
+            pltpu.VMEM((half,), jnp.float32),
+            pltpu.VMEM((half,), jnp.float32),
+            pltpu.SemaphoreType.DMA((32,)),
+        ],
+        compiler_params=pltpu.CompilerParams(vmem_limit_bytes=32 << 20),
+    )(
+        *(
+            pltpu.with_memory_space_constraint(one, pltpu.HBM)
+            for one in (
+                query_in,
+                key_in,
+                value_in,
+                frames_in,
+                cotangent,
+                out_weight,
+                conv_kernel,
+                conv_bias,
+                ln_gain,
+            )
+        )
     )
     parts = [
-        piece if step == 0 else lax.ppermute(piece, "ctx", cyclic(count, step))
-        for step, piece in enumerate(pieces)
+        lax.ppermute(one, "ctx", facing(count, index % 3 + 1)) for index, one in enumerate(pieces)
     ]
-
-    depth = width // 2
-    w_near = lax.ppermute(
-        lax.dynamic_slice_in_dim(out_weight_later, core * depth, depth, axis=0), "fsdp", swap
-    )
-    par_own = jnp.concatenate(
-        [
-            conv_kernel_later,
-            conv_bias[None],
-            ln_gain[None],
-            jnp.zeros((PARAM_ROWS - TAPS - 2, half), jnp.float32),
-        ],
-        axis=0,
-    )
-    par_other = lax.ppermute(par_own, "fsdp", swap)
-    parts, w_near, frames_later, cotangent_later = lax.optimization_barrier(
-        (parts, w_near, frames_in, cotangent)
-    )
+    edge = lax.ppermute(edge, "ctx", [(1, 2), (2, 1)])
+    w_near = lax.ppermute(w_sent, "fsdp", swap)
+
+    replies = []
+    for chunk in range(CHUNKS):
+        ready = parts[3 * chunk : 3 * chunk + 3]
+        if chunk == CHUNKS - 1:
+            ready, edge, _ = lax.optimization_barrier((ready, edge, attended))
+        attended = pl.pallas_call(
+            functools.partial(attend_kernel, chunk),
+            name="attend",
+            out_shape=[jax.ShapeDtypeStruct((rows + 2 * WIDE, LANES), jnp.bfloat16)] * count,
+            in_specs=[smem] + [hbm] * 3 + [vmem] * 3,
+            out_specs=[vmem] * count,
+            scratch_shapes=[pltpu.VMEM((count * rows, LANES), jnp.bfloat16)] * 3
+            + [pltpu.VMEM((count * rows + 2 * WIDE, LANES), jnp.bfloat16)]
+            + [pltpu.SemaphoreType.DMA((3,))],
+            compiler_params=pltpu.CompilerParams(vmem_limit_bytes=40 << 20),
+            cost_estimate=pl.CostEstimate(flops=1, bytes_accessed=1, transcendentals=0),
+        )(utt_lengths, query_in, key_in, value_in, *ready)
+        replies += [
+            reply if step == 0 else lax.ppermute(reply, "ctx", facing(count, step))
+            for step, reply in enumerate(attended)
+        ]
+    _, w_near = lax.optimization_barrier((attended, w_near))
     w_far = lax.ppermute(w_near, "dp", swap)
-
     frames, cotan = frames_in[0], cotangent[0]
-    upward = jnp.concatenate(
-        [frames_later[0, rows - WIDE :], cotangent_later[0, rows - NEAR :]], axis=0
-    )
-    downward = jnp.concatenate([frames_later[0, :WIDE], cotangent_later[0, :NEAR]], axis=0)
-    below = lax.ppermute(upward, "ctx", [(i, i + 1) for i in range(count - 1)])
-    above = lax.ppermute(downward, "ctx", [(i + 1, i) for i in range(count - 1)])
-
-    replies = pl.pallas_call(
-        functools.partial(attend_kernel, count, rows),
-        name="attend",
-        out_shape=[jax.ShapeDtypeStruct((rows + 2 * WIDE, share), jnp.bfloat16)] * count,
-        in_specs=[smem] + [vmem] * count,
-        out_specs=[vmem] * count,
-        scratch_shapes=[pltpu.VMEM((count * rows, share), jnp.bfloat16)] * 3
-        + [pltpu.VMEM((count * rows + 2 * WIDE, share), jnp.bfloat16)],
-        compiler_params=pltpu.CompilerParams(vmem_limit_bytes=40 << 20),
-        cost_estimate=pl.CostEstimate(
-            flops=4 * share * (count * rows) ** 2,
-            bytes_accessed=2 * 4 * count * rows * share,
-            transcendentals=(share // HD) * (count * rows) ** 2,
-        ),
-    )(info, *parts)
-    replies = [
-        reply if step == 0 else lax.ppermute(reply, "ctx", cyclic(count, -step))
-        for step, reply in enumerate(replies)
-    ]
 
     ext, near = rows + 2 * WIDE, rows + 2 * NEAR
     tiles = features // LANES
-    block_out, hidden_grad, sums_own, sums_other = pl.pallas_call(
-        functools.partial(module_kernel, count),
+    block_out, normed, wide_grad, params, inv_rows, sums_own, sums_other, par_mine = pl.pallas_call(
+        module_kernel,
         name="conv_module",
         out_shape=[
             jax.ShapeDtypeStruct((rows, features), jnp.bfloat16),
-            jax.ShapeDtypeStruct((rows, features), jnp.bfloat16),
-            jax.ShapeDtypeStruct((TAPS + 1, half), jnp.float32),
+            jax.ShapeDtypeStruct((tiles, ext + 8, LANES), jnp.float32),
+            jax.ShapeDtypeStruct((tiles, near + 8, LANES), jnp.float32),
+            jax.ShapeDtypeStruct((tiles, PARAM_ROWS, LANES), jnp.float32),
+            jax.ShapeDtypeStruct((rows, LANES), jnp.float32),
             jax.ShapeDtypeStruct((TAPS + 1, half), jnp.bfloat16),
+            jax.ShapeDtypeStruct((TAPS + 1, half), jnp.bfloat16),
+            jax.ShapeDtypeStruct((PARAM_ROWS, half), jnp.float32),
         ],
-        in_specs=[smem] + [vmem] * (count + 9),
-        out_specs=[vmem] * 4,
+        in_specs=[smem] + [vmem] * (count * CHUNKS + 10),
+        out_specs=[hbm] + [vmem] * 7,
         scratch_shapes=[
-            pltpu.VMEM((count, ext, share), jnp.bfloat16),
-            pltpu.VMEM((tiles, PARAM_ROWS, LANES), jnp.float32),
-            pltpu.VMEM((tiles, ext + 8, LANES), jnp.float32),
-            pltpu.VMEM((near + 8, LANES), jnp.float32),
-            pltpu.VMEM((tiles, rows, LANES), jnp.float32),
+            pltpu.VMEM((2, WIDE + NEAR, features), jnp.bfloat16),
+            pltpu.VMEM((count, ext, SHARE), jnp.bfloat16),
             pltpu.VMEM((tiles, TAPS + 1, LANES), jnp.float32),
             pltpu.VMEM((TAPS + 1, 8, LANES), jnp.float32),
-            pltpu.VMEM((rows, LANES), jnp.float32),
-            pltpu.VMEM((rows, LANES), jnp.float32),
+            pltpu.VMEM((rows, features), jnp.bfloat16),
+            pltpu.SemaphoreType.DMA((tiles,)),
         ],
-        compiler_params=pltpu.CompilerParams(vmem_limit_bytes=40 << 20),
+        compiler_params=pltpu.CompilerParams(vmem_limit_bytes=32 << 20),
         cost_estimate=pl.CostEstimate(
-            flops=2 * ext * width * features + 6 * TAPS * rows * features,
+            flops=2 * ext * width * features + 4 * TAPS * rows * features,
             bytes_accessed=2 * width * features + 12 * rows * features,
             transcendentals=near * features,
         ),
-    )(info, *replies, frames, cotan, below, above, out_weight, w_near, w_far, par_own, par_other)
-
-    found = sums_own + lax.ppermute(sums_other, "fsdp", swap).astype(jnp.float32)
-    found = found + lax.ppermute(found, "dp", swap)
+    )(
+        utt_lengths,
+        *replies,
+        frames,
+        cotan,
+        parts[0],
+        edge,
+        out_weight,
+        w_near,
+        w_far,
+        conv_kernel,
+        conv_bias,
+        ln_gain,
+    )
+
+    pairs = [
+        lax.ppermute(sums_other, "fsdp", swap),
+        lax.ppermute(sums_other, ("fsdp", "dp"), [(0, 3), (3, 0), (1, 2), (2, 1)]),
+        lax.ppermute(sums_own, "dp", swap),
+    ]
+    hidden_grad = pl.pallas_call(
+        backward_kernel,
+        name="conv_backward",
+        out_shape=jax.ShapeDtypeStruct((rows, features), jnp.bfloat16),
+        in_specs=[smem] + [vmem] * 5,
+        out_specs=hbm,
+        scratch_shapes=[pltpu.VMEM((tiles, rows, LANES), jnp.float32)]
+        + [pltpu.VMEM((rows, LANES), jnp.float32)] * 2
+        + [pltpu.VMEM((rows, features), jnp.bfloat16), pltpu.SemaphoreType.DMA((tiles,))],
+        compiler_params=pltpu.CompilerParams(vmem_limit_bytes=32 << 20),
+        cost_estimate=pl.CostEstimate(
+            flops=2 * TAPS * rows * features,
+            bytes_accessed=12 * rows * features,
+            transcendentals=0,
+        ),
+    )(utt_lengths, cotan, normed, wide_grad, params, inv_rows)
+    pairs, hidden_grad = lax.optimization_barrier((pairs, hidden_grad))
+    across_x, diagonal, sibling = (one.astype(jnp.float32) for one in pairs)
+    found = (sums_own.astype(jnp.float32) + sibling) + (across_x + diagonal)
     found = found.astype(jnp.bfloat16)
-    arrived = [found] + [lax.ppermute(found, "ctx", cyclic(count, step)) for step in range(1, count)]
-    found = sum(
-        lax.select_n(lax.rem(place + count - block, count), *arrived).astype(jnp.float32)
-        for block in range(count)
-    )
+    arrived = [lax.ppermute(found, "ctx", facing(count, step)) for step in range(1, count)]
     factor = 1.0 / math.sqrt(lax.axis_size("fsdp") * lax.axis_size("dp") * rows * count)
-    found = found * factor
-    grad_kernel = found[:TAPS] * ln_gain
-    grad_gain = jnp.sum(found[:TAPS] * conv_kernel, axis=0)
-    return (block_out[None], hidden_grad[None], grad_kernel, found[TAPS], grad_gain)
+    grad_kernel, grad_bias, grad_gain = pl.pallas_call(
+        functools.partial(finish_kernel, factor),
+        name="finish",
+        out_shape=[
+            jax.ShapeDtypeStruct((TAPS, half), jnp.float32),
+            jax.ShapeDtypeStruct((half,), jnp.float32),
+            jax.ShapeDtypeStruct((half,), jnp.float32),
+        ],
+        in_specs=[vmem] * 5,
+        out_specs=[vmem] * 3,
+        scratch_shapes=[pltpu.VMEM((count, TAPS + 1, half), jnp.float32)],
+        compiler_params=pltpu.CompilerParams(vmem_limit_bytes=32 << 20),
+    )(found, *arrived, par_mine)
+    return (block_out[None], hidden_grad[None], grad_kernel, grad_bias, grad_gain)
 
 
 def solution(mesh):

time: 77.6 us -> 67.9 us (0.88)
  local copies, waits for them, and re-layouts: 5.57 us -> 0.05 us
  waiting for transfers between devices: 23.6 us -> 18.3 us
  Pallas kernels: 16 us -> 18.6 us
  other arithmetic: 2.4 us -> 0.03 us
  starting transfers between devices: 28.1 us -> 29.2 us
    ppermute x15 -> x20, waiting for transfers between devices: 23.6 us -> 18.3 us  [the longest x6 10.5 us: fast_shards(): lax.ppermute(one, 'ctx', facing(count, index % 3 + 1))]
    pallas_call x2 -> x6, Pallas kernels: 16 us -> 18.6 us  [the longest x1 7.81 us: fast_shards(): pl.pallas_call(module_kernel, name='conv_module', out_shape=[jax.ShapeDty...]
    unnamed x14 -> x18, local copies, waits for them, and re-layouts: 2.09 us -> 0.05 us
    dynamic_slice x2 -> x0, local copies, waits for them, and re-layouts: 1.8 us -> none  [the longest x1 0.94 us: fast_shards(): lax.dynamic_slice_in_dim(out_weight_later, core * depth, depth, axis=0)]
    reduce_sum x1 -> x0, other arithmetic: 1.25 us -> none  [fast_shards(): grad_gain = jnp.sum(found[:TAPS] * conv_kernel, axis=0)]
    ppermute x15 -> x20, starting transfers between devices: 28.1 us -> 29.2 us  [the longest x6 9.86 us: fast_shards(): lax.ppermute(reply, 'ctx', facing(count, step))]
    concatenate x2 -> x0, local copies, waits for them, and re-layouts: 1.04 us -> none  [the longest x1 0.97 us: fast_shards(): stacked = jnp.concatenate([query_in, key_in, value_in], axis=0)]
    concatenate x3 -> x0, other arithmetic: 0.99 us -> none  [the longest x1 0.97 us: fast_shards(): jnp.concatenate([conv_kernel_later, conv_bias[None], ln_gain[None], jnp.z...]
  transfers between devices with their start and end apart: 16 -> 21, of which waited for: 8 -> 8; matrix products, arithmetic and copies ran while one was open for 2% -> 0% of each run, Pallas kernels for 7% -> 12%
where the time goes in v2:
time: 67.9 us; the launch traced here: 67.8 us
  starting transfers between devices  29.2 us (43%)
  Pallas kernels  18.6 us (27%)
  waiting for transfers between devices  18.3 us (27%)
  between operations  1.54 us (2%)
    ppermute x6, waiting for transfers between devices, fast_shards(): lax.ppermute(one, 'ctx', facing(count, index % 3 + 1))  10.5 us
    ppermute x6, starting transfers between devices, fast_shards(): lax.ppermute(reply, 'ctx', facing(count, step))  9.86 us
    ppermute x6, starting transfers between devices, fast_shards(): lax.ppermute(one, 'ctx', facing(count, index % 3 + 1))  9.27 us
    pallas_call x1, Pallas kernels, fast_shards(): pl.pallas_call(module_kernel, name='conv_module', out_shape=[jax.ShapeDty...  7.81 us
    pallas_call x2, Pallas kernels, fast_shards(): pl.pallas_call(functools.partial(attend_kernel, chunk), name='attend', ou...  4.7 us
    ppermute x6, waiting for transfers between devices, fast_shards(): lax.ppermute(reply, 'ctx', facing(count, step))  4.49 us
    ppermute x3, starting transfers between devices, fast_shards(): lax.ppermute(found, 'ctx', facing(count, step))  4.45 us
    pallas_call x1, Pallas kernels, fast_shards(): pl.pallas_call(backward_kernel, name='conv_backward', out_shape=jax.Shape...  3.44 us
  transfers between devices with their start and end apart: 21, of which 8 were waited for; matrix products, arithmetic and copies ran while one was open for 0% of the time, Pallas kernels for 12%

profile of v2, /device:TPU:0, one launch (start us, length us, event | category | flops | bytes accessed | tf_op | source)
XLA Modules:
  0.0 67.8 jit_solution(13014391756346403970)
XLA Ops:
  0.7 2.0 %pack.1 = (bf16[960,128]{1,0:T(8,128)(2,1)S(1)}, bf16[384,128]{1,0:T(8,128)(2,1)S(1)}, bf16[384,128]{1,0:T(8,128)(2,1)S(1)}, bf16[384,128]{1,0:T(8,128)(2,1)S(1)...) custom-call(bf16[1,128,1024]{2,1,0:T(8,128)(2,1)} %query_ref.3, ...), custom_call_target="tpu_custom_call" | custom-call | tf_op jit(solution)/shard_map/pack/pallas_call | solution.py:534
  2.7 3.0 %collective-permute-start.13 = (bf16[592,768]{1,0:T(8,128)(2,1)S(1)}, bf16[592,768]{1,0:T(8,128)(2,1)S(1)}, u32[]{:S(2)}, u32[]{:S(2)}) collective-permute-start(bf16[592,768]{1,0:T(8,128)(2,1)S(1)} %get-tuple-element.60), channel_id=1, source_target_pairs={{0,2},{2,0},{1,3},{3,1},{4,6},{6,4},{5,7},{7,5},{8,10},{10,8},{9,1... | collective-permute-start | bytes 2727944 | tf_op jit(solution)/shard_map/ppermute | solution.py:569
  5.7 1.6 %collective-permute-start = (bf16[960,128]{1,0:T(8,128)(2,1)S(1)}, bf16[960,128]{1,0:T(8,128)(2,1)S(1)}, u32[]{:S(2)}, u32[]{:S(2)}) collective-permute-start(bf16[960,128]{1,0:T(8,128)(2,1)S(1)} %get-tuple-element.41), channel_id=1, source_target_pairs={{0,4},{4,0},{8,12},{12,8},{1,5},{5,1},{9,13},{13,9},{2,6},{6,2},{1... | collective-permute-start | bytes 737288 | tf_op jit(solution)/shard_map/ppermute | solution.py:566
  7.3 2.6 %collective-permute-start.1 = (bf16[384,128]{1,0:T(8,128)(2,1)S(1)}, bf16[384,128]{1,0:T(8,128)(2,1)S(1)}, u32[]{:S(2)}, u32[]{:S(2)}) collective-permute-start(bf16[384,128]{1,0:T(8,128)(2,1)S(1)} %get-tuple-element.42), channel_id=1, source_target_pairs={{0,8},{4,12},{8,0},{12,4},{1,9},{5,13},{9,1},{13,5},{2,10},{6,14},... | collective-permute-start | bytes 294920 | tf_op jit(solution)/shard_map/ppermute | solution.py:566
  9.9 0.2 collective-permute-start.2
  10.1 0.7 collective-permute-start.9
  10.8 4.7 %collective-permute-done.1.refs_1_ = bf16[384,128]{1,0:T(8,128)(2,1)S(1)} collective-permute-done((bf16[384,128]{1,0:T(8,128)(2,1)S(1)}, bf16[384,128]{1,0:T(8,128)(2,1)S(1)}, u32[]{:S(2)}, u32[]{:S(2)}) %collective-permute-start.1) | collective-permute-done | bytes 98336 | tf_op jit(solution)/shard_map/ppermute | solution.py:566
  15.4 3.7 %collective-permute-start.6 = (bf16[384,128]{1,0:T(8,128)(2,1)S(1)}, bf16[384,128]{1,0:T(8,128)(2,1)S(1)}, u32[]{:S(2)}, u32[]{:S(2)}) collective-permute-start(bf16[384,128]{1,0:T(8,128)(2,1)S(1)} %get-tuple-element.48), channel_id=1, source_target_pairs={{0,4},{4,0},{8,12},{12,8},{1,5},{5,1},{9,13},{13,9},{2,6},{6,2},{1... | collective-permute-start | bytes 294920 | tf_op jit(solution)/shard_map/ppermute | solution.py:566
  19.1 1.6 %collective-permute-done.2.refs_2_ = bf16[384,128]{1,0:T(8,128)(2,1)S(1)} collective-permute-done((bf16[384,128]{1,0:T(8,128)(2,1)S(1)}, bf16[384,128]{1,0:T(8,128)(2,1)S(1)}, u32[]{:S(2)}, u32[]{:S(2)}) %collective-permute-start.2) | collective-permute-done | bytes 98336 | tf_op jit(solution)/shard_map/ppermute | solution.py:566
  20.7 0.7 collective-permute-start.7
  21.4 0.5 collective-permute-start.8
  22.6 2.4 %attend.2 = (bf16[192,128]{1,0:T(8,128)(2,1)S(1)}, bf16[192,128]{1,0:T(8,128)(2,1)S(1)}, bf16[192,128]{1,0:T(8,128)(2,1)S(1)}, bf16[192,128]{1,0:T(8,128)(2,1)S(1)}) custom-call(s32[1]{0:T(128)S(6)} %copy.15.length_ref.refs_0_, bf16[1,128,1024]{2,1,0:T(8,128)(2,1)S(1)} %copy-done.2, bf16[1,128,1024]{2,1,0:T(8,128)(2,1)S(1)} %copy-done.3, ...), custom_call_target="tpu_custom_call" | custom-call | flops 1 | bytes 1 | tf_op jit(solution)/shard_map/attend/pallas_call | solution.py:576
  25.0 4.3 %collective-permute-done.7.refs_1_ = bf16[384,128]{1,0:T(8,128)(2,1)S(1)} collective-permute-done((bf16[384,128]{1,0:T(8,128)(2,1)S(1)}, bf16[384,128]{1,0:T(8,128)(2,1)S(1)}, u32[]{:S(2)}, u32[]{:S(2)}) %collective-permute-start.7) | collective-permute-done | bytes 98336 | tf_op jit(solution)/shard_map/ppermute | solution.py:566
  29.2 2.3 %attend.3 = (bf16[192,128]{1,0:T(8,128)(2,1)S(1)}, bf16[192,128]{1,0:T(8,128)(2,1)S(1)}, bf16[192,128]{1,0:T(8,128)(2,1)S(1)}, bf16[192,128]{1,0:T(8,128)(2,1)S(1)}) custom-call(s32[1]{0:T(128)S(6)} %copy.15.length_ref.refs_0_, bf16[1,128,1024]{2,1,0:T(8,128)(2,1)S(1)} %copy-done.2, bf16[1,128,1024]{2,1,0:T(8,128)(2,1)S(1)} %copy-done.3, ...), custom_call_target="tpu_custom_call" | custom-call | flops 1 | bytes 1 | tf_op jit(solution)/shard_map/attend/pallas_call | solution.py:576
  31.7 1.7 %collective-permute-start.10 = (bf16[192,128]{1,0:T(8,128)(2,1)S(1)}, bf16[192,128]{1,0:T(8,128)(2,1)S(1)}, u32[]{:S(2)}, u32[]{:S(2)}) collective-permute-start(bf16[192,128]{1,0:T(8,128)(2,1)S(1)} %get-tuple-element.56), channel_id=1, source_target_pairs={{0,4},{4,0},{8,12},{12,8},{1,5},{5,1},{9,13},{13,9},{2,6},{6,2},{1... | collective-permute-start | bytes 147464 | tf_op jit(solution)/shard_map/ppermute | solution.py:589
  33.4 1.2 %collective-permute-start.11 = (bf16[192,128]{1,0:T(8,128)(2,1)S(1)}, bf16[192,128]{1,0:T(8,128)(2,1)S(1)}, u32[]{:S(2)}, u32[]{:S(2)}) collective-permute-start(bf16[192,128]{1,0:T(8,128)(2,1)S(1)} %get-tuple-element.57), channel_id=1, source_target_pairs={{0,8},{4,12},{8,0},{12,4},{1,9},{5,13},{9,1},{13,5},{2,10},{6,14},... | collective-permute-start | bytes 147464 | tf_op jit(solution)/shard_map/ppermute | solution.py:589
  34.6 1.5 %collective-permute-start.12 = (bf16[192,128]{1,0:T(8,128)(2,1)S(1)}, bf16[192,128]{1,0:T(8,128)(2,1)S(1)}, u32[]{:S(2)}, u32[]{:S(2)}) collective-permute-start(bf16[192,128]{1,0:T(8,128)(2,1)S(1)} %get-tuple-element.58), channel_id=1, source_target_pairs={{0,12},{4,8},{8,4},{12,0},{1,13},{5,9},{9,5},{13,1},{2,14},{6,10},... | collective-permute-start | bytes 147464 | tf_op jit(solution)/shard_map/ppermute | solution.py:589
  36.1 0.7 %collective-permute-start.3 = (bf16[192,128]{1,0:T(8,128)(2,1)S(1)}, bf16[192,128]{1,0:T(8,128)(2,1)S(1)}, u32[]{:S(2)}, u32[]{:S(2)}) collective-permute-start(bf16[192,128]{1,0:T(8,128)(2,1)S(1)} %get-tuple-element.45), channel_id=1, source_target_pairs={{0,4},{4,0},{8,12},{12,8},{1,5},{5,1},{9,13},{13,9},{2,6},{6,2},{1... | collective-permute-start | bytes 147464 | tf_op jit(solution)/shard_map/ppermute | solution.py:589
  36.9 2.1 %collective-permute-start.4 = (bf16[192,128]{1,0:T(8,128)(2,1)S(1)}, bf16[192,128]{1,0:T(8,128)(2,1)S(1)}, u32[]{:S(2)}, u32[]{:S(2)}) collective-permute-start(bf16[192,128]{1,0:T(8,128)(2,1)S(1)} %get-tuple-element.46), channel_id=1, source_target_pairs={{0,8},{4,12},{8,0},{12,4},{1,9},{5,13},{9,1},{13,5},{2,10},{6,14},... | collective-permute-start | bytes 147464 | tf_op jit(solution)/shard_map/ppermute | solution.py:589
  39.0 1.1 %collective-permute-done.11.refs_7_ = bf16[192,128]{1,0:T(8,128)(2,1)S(1)} collective-permute-done((bf16[192,128]{1,0:T(8,128)(2,1)S(1)}, bf16[192,128]{1,0:T(8,128)(2,1)S(1)}, u32[]{:S(2)}, u32[]{:S(2)}) %collective-permute-start.11) | collective-permute-done | bytes 49184 | tf_op jit(solution)/shard_map/ppermute | solution.py:589
  40.1 2.5 %collective-permute-start.5 = (bf16[192,128]{1,0:T(8,128)(2,1)S(1)}, bf16[192,128]{1,0:T(8,128)(2,1)S(1)}, u32[]{:S(2)}, u32[]{:S(2)}) collective-permute-start(bf16[192,128]{1,0:T(8,128)(2,1)S(1)} %get-tuple-element.47), channel_id=1, source_target_pairs={{0,12},{4,8},{8,4},{12,0},{1,13},{5,9},{9,5},{13,1},{2,14},{6,10},... | collective-permute-start | bytes 147464 | tf_op jit(solution)/shard_map/ppermute | solution.py:589
  42.7 1.6 %collective-permute-done.4.refs_3_ = bf16[192,128]{1,0:T(8,128)(2,1)S(1)} collective-permute-done((bf16[192,128]{1,0:T(8,128)(2,1)S(1)}, bf16[192,128]{1,0:T(8,128)(2,1)S(1)}, u32[]{:S(2)}, u32[]{:S(2)}) %collective-permute-start.4) | collective-permute-done | bytes 49184 | tf_op jit(solution)/shard_map/ppermute | solution.py:589
  44.3 1.8 %collective-permute-done.5.refs_4_ = bf16[192,128]{1,0:T(8,128)(2,1)S(1)} collective-permute-done((bf16[192,128]{1,0:T(8,128)(2,1)S(1)}, bf16[192,128]{1,0:T(8,128)(2,1)S(1)}, u32[]{:S(2)}, u32[]{:S(2)}) %collective-permute-start.5) | collective-permute-done | bytes 49184 | tf_op jit(solution)/shard_map/ppermute | solution.py:589
  46.1 7.8 %conv_module.1 = (bf16[128,1536]{1,0:T(8,128)(2,1)}, f32[12,200,128]{2,1,0:T(8,128)S(1)}, f32[12,168,128]{2,1,0:T(8,128)S(1)}, f32[12,40,128]{2,1,0:T(8,128)S(1)...) custom-call(s32[1]{0:T(128)S(6)} %copy.15.length_ref.refs_0_, ...), custom_call_target="tpu_custom_call" | custom-call | flops 628359168 | bytes 5505024 | tf_op jit(solution)/shard_map/conv_module/pallas_call | solution.py:598
  54.0 0.6 collective-permute-start.15
  54.6 1.3 %collective-permute-start.17 = (bf16[32,768]{1,0:T(8,128)(2,1)S(1)}, bf16[32,768]{1,0:T(8,128)(2,1)S(1)}, u32[]{:S(2)}, u32[]{:S(2)}) collective-permute-start(bf16[32,768]{1,0:T(8,128)(2,1)S(1)} %get-tuple-element.64), channel_id=1, source_target_pairs={{0,1},{1,0},{2,3},{3,2},{4,5},{5,4},{6,7},{7,6},{8,9},{9,8},{10,11... | collective-permute-start | bytes 147464 | tf_op jit(solution)/shard_map/ppermute | solution.py:645
  55.8 3.4 %conv_backward.1 = bf16[128,1536]{1,0:T(8,128)(2,1)} custom-call(s32[1]{0:T(128)S(6)} %copy.15.length_ref.refs_0_, bf16[128,1536]{1,0:T(8,128)(2,1)S(1)} %bitcast.5, f32[12,200,128]{2,1,0:T(8,128)S(1)} %get-tuple-element.65.normed, f32[12,168,128]{2,1,0:T(8,128)S(1)} %get-tuple-element.66.wide_grad, f32[12,40,128]{2,1,0:T(8,128)S(1)} %get-tuple-element.67.params, ...), custom_call_target="tpu_custom_call" | custom-call | flops 12189696 | bytes 2359296 | tf_op jit(solution)/shard_map/conv_backward/pallas_call | solution.py:647
  59.3 2.6 %collective-permute-start.20 = (bf16[32,768]{1,0:T(8,128)(2,1)S(1)}, bf16[32,768]{1,0:T(8,128)(2,1)S(1)}, u32[]{:S(2)}, u32[]{:S(2)}) collective-permute-start(bf16[32,768]{1,0:T(8,128)(2,1)S(1)} %add_convert_fusion.mine), channel_id=1, source_target_pairs={{0,12},{4,8},{8,4},{12,0},{1,13},{5,9},{9,5},{13,1},{2,14},{6,10},... | collective-permute-start | bytes 147464 | tf_op jit(solution)/shard_map/ppermute | solution.py:667
  61.9 1.9 %collective-permute-start.18 = (bf16[32,768]{1,0:T(8,128)(2,1)S(1)}, bf16[32,768]{1,0:T(8,128)(2,1)S(1)}, u32[]{:S(2)}, u32[]{:S(2)}) collective-permute-start(bf16[32,768]{1,0:T(8,128)(2,1)S(1)} %add_convert_fusion.mine), channel_id=1, source_target_pairs={{0,4},{4,0},{8,12},{12,8},{1,5},{5,1},{9,13},{13,9},{2,6},{6,2},{1... | collective-permute-start | bytes 147464 | tf_op jit(solution)/shard_map/ppermute | solution.py:667
  63.8 1.6 %collective-permute-done.20.three = bf16[32,768]{1,0:T(8,128)(2,1)S(1)} collective-permute-done((bf16[32,768]{1,0:T(8,128)(2,1)S(1)}, bf16[32,768]{1,0:T(8,128)(2,1)S(1)}, u32[]{:S(2)}, u32[]{:S(2)}) %collective-permute-start.20) | collective-permute-done | bytes 49184 | tf_op jit(solution)/shard_map/ppermute | solution.py:667
  65.4 1.6 %collective-permute-done.19.two = bf16[32,768]{1,0:T(8,128)(2,1)S(1)} collective-permute-done((bf16[32,768]{1,0:T(8,128)(2,1)S(1)}, bf16[32,768]{1,0:T(8,128)(2,1)S(1)}, u32[]{:S(2)}, u32[]{:S(2)}) %collective-permute-start.19) | collective-permute-done | bytes 49184 | tf_op jit(solution)/shard_map/ppermute | solution.py:667
  67.0 0.7 %finish.1 = (f32[31,768]{1,0:T(8,128)}, f32[768]{0:T(1024)}, f32[768]{0:T(1024)}) custom-call(bf16[32,768]{1,0:T(8,128)(2,1)S(1)} %add_convert_fusion.mine, bf16[32,768]{1,0:T(8,128)(2,1)S(1)} %collective-permute-done.18.one, bf16[32,768]{1,0:T(8,128)(2,1)S(1)} %collective-permute-done.19.two, bf16[32,768]{1,0:T(8,128)(2,1)S(1)} %collective-permute-done.20.three, ...), custom_call_target="tpu_custom_call" | custom-call | tf_op jit(solution)/shard_map/finish/pallas_call | solution.py:669
  (35 shorter events, 0.3 us)
Async XLA Ops:
  0.6 21.9 %copy-start.4 = (bf16[1,128,1024]{2,1,0:T(8,128)(2,1)S(1)}, bf16[1,128,1024]{2,1,0:T(8,128)(2,1)}, u32[]{:S(2)}) copy-start(bf16[1,128,1024]{2,1,0:T(8,128)(2,1)} %value_ref.3) | copy-start | bytes 786436
  0.6 21.9 %copy-start.3 = (bf16[1,128,1024]{2,1,0:T(8,128)(2,1)S(1)}, bf16[1,128,1024]{2,1,0:T(8,128)(2,1)}, u32[]{:S(2)}) copy-start(bf16[1,128,1024]{2,1,0:T(8,128)(2,1)} %key_ref.3) | copy-start | bytes 786436
  0.7 21.9 %copy-start.2 = (bf16[1,128,1024]{2,1,0:T(8,128)(2,1)S(1)}, bf16[1,128,1024]{2,1,0:T(8,128)(2,1)}, u32[]{:S(2)}) copy-start(bf16[1,128,1024]{2,1,0:T(8,128)(2,1)} %query_ref.3) | copy-start | bytes 786436
  0.7 45.4 %copy-start.5 = (bf16[1,128,1536]{2,1,0:T(8,128)(2,1)S(1)}, bf16[1,128,1536]{2,1,0:T(8,128)(2,1)}, u32[]{:S(2)}) copy-start(bf16[1,128,1536]{2,1,0:T(8,128)(2,1)} %refs_3_.1) | copy-start | bytes 1179652
  2.6 43.4 %copy-start = (bf16[1024,768]{1,0:T(8,128)(2,1)S(1)}, bf16[1024,768]{1,0:T(8,128)(2,1)}, u32[]{:S(2)}) copy-start(bf16[1024,768]{1,0:T(8,128)(2,1)} %refs_13_.1) | copy-start | bytes 4718596
  2.7 43.4 %copy-start.1 = (bf16[1,128,1536]{2,1,0:T(8,128)(2,1)S(1)}, bf16[1,128,1536]{2,1,0:T(8,128)(2,1)}, u32[]{:S(2)}) copy-start(bf16[1,128,1536]{2,1,0:T(8,128)(2,1)} %refs_4_.1) | copy-start | bytes 1179652
  2.7 43.4 %copy-start.6 = (f32[31,768]{1,0:T(8,128)S(1)}, f32[31,768]{1,0:T(8,128)}, u32[]{:S(2)}) copy-start(f32[31,768]{1,0:T(8,128)} %refs_16_.1) | copy-start | bytes 285700
  2.7 43.4 %copy-start.7 = (f32[768]{0:T(1024)S(1)}, f32[768]{0:T(1024)}, u32[]{:S(2)}) copy-start(f32[768]{0:T(1024)} %refs_17_.1) | copy-start | bytes 9220
  2.7 43.4 %copy-start.8 = (f32[768]{0:T(1024)S(1)}, f32[768]{0:T(1024)}, u32[]{:S(2)}) copy-start(f32[768]{0:T(1024)} %refs_18_.1) | copy-start | bytes 9220
  2.7 28.9 %collective-permute-start.13 = (bf16[592,768]{1,0:T(8,128)(2,1)S(1)}, bf16[592,768]{1,0:T(8,128)(2,1)S(1)}, u32[]{:S(2)}, u32[]{:S(2)}) collective-permute-start(bf16[592,768]{1,0:T(8,128)(2,1)S(1)} %get-tuple-element.60), channel_id=1, source_target_pairs={{0,2},{2,0},{1,3},{3,1},{4,6},{6,4},{5,7},{7,5},{8,10},{10,8},{9,1... | collective-permute-start | bytes 2727944 | tf_op jit(solution)/shard_map/ppermute | solution.py:569
  5.7 15.7 %collective-permute-start = (bf16[960,128]{1,0:T(8,128)(2,1)S(1)}, bf16[960,128]{1,0:T(8,128)(2,1)S(1)}, u32[]{:S(2)}, u32[]{:S(2)}) collective-permute-start(bf16[960,128]{1,0:T(8,128)(2,1)S(1)} %get-tuple-element.41), channel_id=1, source_target_pairs={{0,4},{4,0},{8,12},{12,8},{1,5},{5,1},{9,13},{13,9},{2,6},{6,2},{1... | collective-permute-start | bytes 737288 | tf_op jit(solution)/shard_map/ppermute | solution.py:566
  7.3 8.1 %collective-permute-start.1 = (bf16[384,128]{1,0:T(8,128)(2,1)S(1)}, bf16[384,128]{1,0:T(8,128)(2,1)S(1)}, u32[]{:S(2)}, u32[]{:S(2)}) collective-permute-start(bf16[384,128]{1,0:T(8,128)(2,1)S(1)} %get-tuple-element.42), channel_id=1, source_target_pairs={{0,8},{4,12},{8,0},{12,4},{1,9},{5,13},{9,1},{13,5},{2,10},{6,14},... | collective-permute-start | bytes 294920 | tf_op jit(solution)/shard_map/ppermute | solution.py:566
  9.9 10.8 %collective-permute-start.2 = (bf16[384,128]{1,0:T(8,128)(2,1)S(1)}, bf16[384,128]{1,0:T(8,128)(2,1)S(1)}, u32[]{:S(2)}, u32[]{:S(2)}) collective-permute-start(bf16[384,128]{1,0:T(8,128)(2,1)S(1)} %get-tuple-element.43), channel_id=1, source_target_pairs={{0,12},{4,8},{8,4},{12,0},{1,13},{5,9},{9,5},{13,1},{2,14},{6,10},... | collective-permute-start | bytes 294920 | tf_op jit(solution)/shard_map/ppermute | solution.py:566
  10.1 19.1 %collective-permute-start.9 = (bf16[48,1536]{1,0:T(8,128)(2,1)S(1)}, bf16[48,1536]{1,0:T(8,128)(2,1)S(1)}, u32[]{:S(2)}, u32[]{:S(2)}) collective-permute-start(bf16[48,1536]{1,0:T(8,128)(2,1)S(1)} %get-tuple-element.51), channel_id=1, source_target_pairs={{4,8},{8,4},{5,9},{9,5},{6,10},{10,6},{7,11},{11,7},{20,24},{24,20... | collective-permute-start | bytes 442376 | tf_op jit(solution)/shard_map/ppermute | solution.py:568
  15.4 9.5 %collective-permute-start.6 = (bf16[384,128]{1,0:T(8,128)(2,1)S(1)}, bf16[384,128]{1,0:T(8,128)(2,1)S(1)}, u32[]{:S(2)}, u32[]{:S(2)}) collective-permute-start(bf16[384,128]{1,0:T(8,128)(2,1)S(1)} %get-tuple-element.48), channel_id=1, source_target_pairs={{0,4},{4,0},{8,12},{12,8},{1,5},{5,1},{9,13},{13,9},{2,6},{6,2},{1... | collective-permute-start | bytes 294920 | tf_op jit(solution)/shard_map/ppermute | solution.py:566
  20.7 8.5 %collective-permute-start.7 = (bf16[384,128]{1,0:T(8,128)(2,1)S(1)}, bf16[384,128]{1,0:T(8,128)(2,1)S(1)}, u32[]{:S(2)}, u32[]{:S(2)}) collective-permute-start(bf16[384,128]{1,0:T(8,128)(2,1)S(1)} %get-tuple-element.49), channel_id=1, source_target_pairs={{0,8},{4,12},{8,0},{12,4},{1,9},{5,13},{9,1},{13,5},{2,10},{6,14},... | collective-permute-start | bytes 294920 | tf_op jit(solution)/shard_map/ppermute | solution.py:566
  21.4 7.9 %collective-permute-start.8 = (bf16[384,128]{1,0:T(8,128)(2,1)S(1)}, bf16[384,128]{1,0:T(8,128)(2,1)S(1)}, u32[]{:S(2)}, u32[]{:S(2)}) collective-permute-start(bf16[384,128]{1,0:T(8,128)(2,1)S(1)} %get-tuple-element.50), channel_id=1, source_target_pairs={{0,12},{4,8},{8,4},{12,0},{1,13},{5,9},{9,5},{13,1},{2,14},{6,10},... | collective-permute-start | bytes 294920 | tf_op jit(solution)/shard_map/ppermute | solution.py:566
  31.6 14.4 %collective-permute-start.14 = (bf16[592,768]{1,0:T(8,128)(2,1)S(1)}, bf16[592,768]{1,0:T(8,128)(2,1)S(1)}, u32[]{:S(2)}, u32[]{:S(2)}) collective-permute-start(bf16[592,768]{1,0:T(8,128)(2,1)S(1)} %collective-permute-done.13.refs_14_), channel_id=1, source_target_pairs={{0,1},{1,0},{2,3},{3,2},{4,5},{5,4},{6,7},{7,6},{8,9},{9,8},{10,11... | collective-permute-start | bytes 2727944 | tf_op jit(solution)/shard_map/ppermute | solution.py:593
  31.7 5.2 %collective-permute-start.10 = (bf16[192,128]{1,0:T(8,128)(2,1)S(1)}, bf16[192,128]{1,0:T(8,128)(2,1)S(1)}, u32[]{:S(2)}, u32[]{:S(2)}) collective-permute-start(bf16[192,128]{1,0:T(8,128)(2,1)S(1)} %get-tuple-element.56), channel_id=1, source_target_pairs={{0,4},{4,0},{8,12},{12,8},{1,5},{5,1},{9,13},{13,9},{2,6},{6,2},{1... | collective-permute-start | bytes 147464 | tf_op jit(solution)/shard_map/ppermute | solution.py:589
  33.4 6.8 %collective-permute-start.11 = (bf16[192,128]{1,0:T(8,128)(2,1)S(1)}, bf16[192,128]{1,0:T(8,128)(2,1)S(1)}, u32[]{:S(2)}, u32[]{:S(2)}) collective-permute-start(bf16[192,128]{1,0:T(8,128)(2,1)S(1)} %get-tuple-element.57), channel_id=1, source_target_pairs={{0,8},{4,12},{8,0},{12,4},{1,9},{5,13},{9,1},{13,5},{2,10},{6,14},... | collective-permute-start | bytes 147464 | tf_op jit(solution)/shard_map/ppermute | solution.py:589
  34.6 8.0 %collective-permute-start.12 = (bf16[192,128]{1,0:T(8,128)(2,1)S(1)}, bf16[192,128]{1,0:T(8,128)(2,1)S(1)}, u32[]{:S(2)}, u32[]{:S(2)}) collective-permute-start(bf16[192,128]{1,0:T(8,128)(2,1)S(1)} %get-tuple-element.58), channel_id=1, source_target_pairs={{0,12},{4,8},{8,4},{12,0},{1,13},{5,9},{9,5},{13,1},{2,14},{6,10},... | collective-permute-start | bytes 147464 | tf_op jit(solution)/shard_map/ppermute | solution.py:589
  36.1 6.5 %collective-permute-start.3 = (bf16[192,128]{1,0:T(8,128)(2,1)S(1)}, bf16[192,128]{1,0:T(8,128)(2,1)S(1)}, u32[]{:S(2)}, u32[]{:S(2)}) collective-permute-start(bf16[192,128]{1,0:T(8,128)(2,1)S(1)} %get-tuple-element.45), channel_id=1, source_target_pairs={{0,4},{4,0},{8,12},{12,8},{1,5},{5,1},{9,13},{13,9},{2,6},{6,2},{1... | collective-permute-start | bytes 147464 | tf_op jit(solution)/shard_map/ppermute | solution.py:589
  36.9 7.4 %collective-permute-start.4 = (bf16[192,128]{1,0:T(8,128)(2,1)S(1)}, bf16[192,128]{1,0:T(8,128)(2,1)S(1)}, u32[]{:S(2)}, u32[]{:S(2)}) collective-permute-start(bf16[192,128]{1,0:T(8,128)(2,1)S(1)} %get-tuple-element.46), channel_id=1, source_target_pairs={{0,8},{4,12},{8,0},{12,4},{1,9},{5,13},{9,1},{13,5},{2,10},{6,14},... | collective-permute-start | bytes 147464 | tf_op jit(solution)/shard_map/ppermute | solution.py:589
  40.1 5.9 %collective-permute-start.5 = (bf16[192,128]{1,0:T(8,128)(2,1)S(1)}, bf16[192,128]{1,0:T(8,128)(2,1)S(1)}, u32[]{:S(2)}, u32[]{:S(2)}) collective-permute-start(bf16[192,128]{1,0:T(8,128)(2,1)S(1)} %get-tuple-element.47), channel_id=1, source_target_pairs={{0,12},{4,8},{8,4},{12,0},{1,13},{5,9},{9,5},{13,1},{2,14},{6,10},... | collective-permute-start | bytes 147464 | tf_op jit(solution)/shard_map/ppermute | solution.py:589
  53.9 5.4 %collective-permute-start.16 = (bf16[32,768]{1,0:T(8,128)(2,1)S(1)}, bf16[32,768]{1,0:T(8,128)(2,1)S(1)}, u32[]{:S(2)}, u32[]{:S(2)}) collective-permute-start(bf16[32,768]{1,0:T(8,128)(2,1)S(1)} %get-tuple-element.63), channel_id=1, source_target_pairs={{0,3},{3,0},{1,2},{2,1},{4,7},{7,4},{5,6},{6,5},{8,11},{11,8},{9,1... | collective-permute-start | bytes 147464 | tf_op jit(solution)/shard_map/ppermute | solution.py:644
  54.0 5.3 %collective-permute-start.15 = (bf16[32,768]{1,0:T(8,128)(2,1)S(1)}, bf16[32,768]{1,0:T(8,128)(2,1)S(1)}, u32[]{:S(2)}, u32[]{:S(2)}) collective-permute-start(bf16[32,768]{1,0:T(8,128)(2,1)S(1)} %get-tuple-element.63), channel_id=1, source_target_pairs={{0,2},{2,0},{1,3},{3,1},{4,6},{6,4},{5,7},{7,5},{8,10},{10,8},{9,1... | collective-permute-start | bytes 147464 | tf_op jit(solution)/shard_map/ppermute | solution.py:643
  54.6 4.7 %collective-permute-start.17 = (bf16[32,768]{1,0:T(8,128)(2,1)S(1)}, bf16[32,768]{1,0:T(8,128)(2,1)S(1)}, u32[]{:S(2)}, u32[]{:S(2)}) collective-permute-start(bf16[32,768]{1,0:T(8,128)(2,1)S(1)} %get-tuple-element.64), channel_id=1, source_target_pairs={{0,1},{1,0},{2,3},{3,2},{4,5},{5,4},{6,7},{7,6},{8,9},{9,8},{10,11... | collective-permute-start | bytes 147464 | tf_op jit(solution)/shard_map/ppermute | solution.py:645
  59.3 6.1 %collective-permute-start.20 = (bf16[32,768]{1,0:T(8,128)(2,1)S(1)}, bf16[32,768]{1,0:T(8,128)(2,1)S(1)}, u32[]{:S(2)}, u32[]{:S(2)}) collective-permute-start(bf16[32,768]{1,0:T(8,128)(2,1)S(1)} %add_convert_fusion.mine), channel_id=1, source_target_pairs={{0,12},{4,8},{8,4},{12,0},{1,13},{5,9},{9,5},{13,1},{2,14},{6,10},... | collective-permute-start | bytes 147464 | tf_op jit(solution)/shard_map/ppermute | solution.py:667
  61.9 5.1 %collective-permute-start.19 = (bf16[32,768]{1,0:T(8,128)(2,1)S(1)}, bf16[32,768]{1,0:T(8,128)(2,1)S(1)}, u32[]{:S(2)}, u32[]{:S(2)}) collective-permute-start(bf16[32,768]{1,0:T(8,128)(2,1)S(1)} %add_convert_fusion.mine), channel_id=1, source_target_pairs={{0,8},{4,12},{8,0},{12,4},{1,9},{5,13},{9,1},{13,5},{2,10},{6,14},... | collective-permute-start | bytes 147464 | tf_op jit(solution)/shard_map/ppermute | solution.py:667
  61.9 5.1 %collective-permute-start.18 = (bf16[32,768]{1,0:T(8,128)(2,1)S(1)}, bf16[32,768]{1,0:T(8,128)(2,1)S(1)}, u32[]{:S(2)}, u32[]{:S(2)}) collective-permute-start(bf16[32,768]{1,0:T(8,128)(2,1)S(1)} %add_convert_fusion.mine), channel_id=1, source_target_pairs={{0,4},{4,0},{8,12},{12,8},{1,5},{5,1},{9,13},{13,9},{2,6},{6,2},{1... | collective-permute-start | bytes 147464 | tf_op jit(solution)/shard_map/ppermute | solution.py:667

commit v3 on v2

--- a/solution.py
+++ b/solution.py
@@ -199,11 +199,14 @@
     return [(i, i ^ step) for i in range(count)]
 
 
+PIECES = [(1, 0)] + [(step, chunk) for chunk in range(CHUNKS) for step in (2, 3)]
+
+
 def pack_kernel(*refs):
     (
         query_ref, key_ref, value_ref, frames_ref, cotan_ref, weight_ref, taps_ref, bias_ref, gain_ref,
         *outs,
-    ) = refs[: 9 + 3 * CHUNKS + 2]
+    ) = refs[: 9 + len(PIECES) + 2]
     whole, edges, taps, bias, gain, in_sems = refs[-6:]
     *outs, edge, weight_out = outs
     place, core = lax.axis_index("ctx"), lax.axis_index("dp")
@@ -236,15 +239,16 @@
         for part in range(per_input):
             arriving[which * per_input + part].wait()
         at = slice(which * rows, (which + 1) * rows)
-        for index, out in enumerate(outs):
-            first = (place ^ (index % 3 + 1)) * SHARE + index // 3 * LANES
-            out[at, :] = whole[which, :, pl.ds(pl.multiple_of(first, LANES), LANES)]
+        for out, (step, chunk) in zip(outs, PIECES):
+            first = (place ^ step) * SHARE + chunk * LANES
+            size = out.shape[1]
+            out[at, :] = whole[which, :, pl.ds(pl.multiple_of(first, LANES), size)]
     seen = 3 * per_input
     for copy in arriving[seen : seen + 4]:
         copy.wait()
-    for block in range(edges.shape[2] // LANES):
+    for block in range(edges.shape[2] // SHARE):
         base = 3 * rows + block * (WIDE + NEAR)
-        outs[0][base : base + WIDE + NEAR, :] = edges[0, :, block * LANES : (block + 1) * LANES]
+        outs[0][base : base + WIDE + NEAR, :] = edges[0, :, block * SHARE : (block + 1) * SHARE]
     edge[...] = edges[1]
     for copy in arriving[-3:]:
         copy.wait()
@@ -270,8 +274,10 @@
 
 
 def attend_kernel(chunk, length_ref, query_ref, key_ref, value_ref, *refs):
-    parts, outs = refs[:3], refs[3:7]
-    query_all, key_all, value_all, attended, sems = refs[7:]
+    parts, refs = refs[:3], refs[3:]
+    before, refs = refs[:chunk], refs[chunk:]
+    outs = refs[:4]
+    query_all, key_all, value_all, attended, sems = refs[4:]
     place, valid_len = lax.axis_index("ctx"), length_ref[0]
     frames, width = query_all.shape
     rows = frames // 4
@@ -287,7 +293,8 @@
     for step, part in enumerate(parts, 1):
         span = pl.ds(pl.multiple_of((place ^ step) * rows, rows), rows)
         for which, target in enumerate(targets):
-            target[span, :] = part[which * rows : (which + 1) * rows, :]
+            cols = slice(chunk * LANES, (chunk + 1) * LANES) if step == 1 else slice(None)
+            target[span, :] = part[which * rows : (which + 1) * rows, cols]
     for copy in copies:
         copy.wait()
     attended[0:WIDE, :] = jnp.zeros((WIDE, width), attended.dtype)
@@ -320,7 +327,12 @@
             attended[WIDE + start : WIDE + start + QUERY_ROWS, cols] = total.astype(attended.dtype)
     for step in range(4):
         owner = place ^ step
-        outs[step][...] = attended[pl.ds(pl.multiple_of(owner * rows, rows), rows + 2 * WIDE), :]
+        found = attended[pl.ds(pl.multiple_of(owner * rows, rows), rows + 2 * WIDE), :]
+        if step == 1 and chunk:
+            outs[step][:, :LANES] = before[0][...]
+            outs[step][:, LANES:] = found
+        else:
+            outs[step][...] = found
 
 
 def by_residue(first, last):
@@ -329,12 +341,12 @@
 
 def module_kernel(*refs):
     count = 4
-    length_ref, *replies = refs[: 1 + count * CHUNKS]
+    length_ref, *replies = refs[: 1 + count * CHUNKS - 1]
     (
         frames_ref, cotan_ref, beside_ref, edge_ref, w_own, w_near, w_far, taps_ref, bias_ref, gain_ref,
         block_hbm, normed, wide_grad, params, inv_rows, sums_own, sums_other, par_mine,
         edges, attended, sums, partial, block_out, out_sems,
-    ) = refs[1 + count * CHUNKS :]
+    ) = refs[count * CHUNKS :]
     place, side, core = lax.axis_index("ctx"), lax.axis_index("fsdp"), lax.axis_index("dp")
     valid_len = length_ref[0]
     rows, features = frames_ref.shape
@@ -346,9 +358,9 @@
     per_part = weight_rows // depth
 
     even = 1 - lax.rem(place, 2)
-    for block in range(features // LANES):
+    for block in range(features // SHARE):
         base = 3 * rows + block * (WIDE + NEAR)
-        edges[even, :, block * LANES : (block + 1) * LANES] = beside_ref[base : base + WIDE + NEAR, :]
+        edges[even, :, block * SHARE : (block + 1) * SHARE] = beside_ref[base : base + WIDE + NEAR, :]
     edges[1 - even] = edge_ref[...]
 
     def live(first, length):
@@ -356,9 +368,12 @@
         return ((position >= 0) & (position < valid_len)).astype(jnp.float32)
 
     for step in range(count):
+        if step == 1:
+            attended[place ^ step] = replies[1][...]
+            continue
         for chunk in range(CHUNKS):
             cols = slice(chunk * LANES, (chunk + 1) * LANES)
-            attended[place ^ step, :, cols] = replies[chunk * count + step][...]
+            attended[place ^ step, :, cols] = replies[(0, 4)[chunk] + (step - chunk if step else 0)][...]
     par_own = parameters(taps_ref, bias_ref, gain_ref)
     par_mine[...] = par_own
     par_other = w_near[weight_rows : weight_rows + PARAM_ROWS, :].astype(jnp.float32)
@@ -524,10 +539,10 @@
     hbm = pl.BlockSpec(memory_space=pltpu.HBM)
     swap = [(0, 1), (1, 0)]
 
-    ends = (features // LANES) * (WIDE + NEAR)
+    ends = (features // SHARE) * (WIDE + NEAR)
     sent = [
-        (3 * rows + ends, LANES),
-        *[(3 * rows, LANES)] * (3 * CHUNKS - 1),
+        (3 * rows + ends, SHARE),
+        *[(3 * rows, LANES)] * (len(PIECES) - 1),
         (WIDE + NEAR, features),
         (width // 2 + 2 * PARAM_ROWS, half),
     ]
@@ -563,32 +578,42 @@
         )
     )
     parts = [
-        lax.ppermute(one, "ctx", facing(count, index % 3 + 1)) for index, one in enumerate(pieces)
+        lax.ppermute(one, "ctx", facing(count, step)) for one, (step, _) in zip(pieces, PIECES)
     ]
     edge = lax.ppermute(edge, "ctx", [(1, 2), (2, 1)])
     w_near = lax.ppermute(w_sent, "fsdp", swap)
 
-    replies = []
+    replies, attended = [], []
     for chunk in range(CHUNKS):
-        ready = parts[3 * chunk : 3 * chunk + 3]
-        if chunk == CHUNKS - 1:
-            ready, edge, _ = lax.optimization_barrier((ready, edge, attended))
+        ready = [parts[0], *parts[2 * chunk + 1 : 2 * chunk + 3]]
+        before = []
+        if chunk:
+            before = [attended[1]]
+            ready, edge = lax.optimization_barrier((ready, edge))
         attended = pl.pallas_call(
             functools.partial(attend_kernel, chunk),
             name="attend",
-            out_shape=[jax.ShapeDtypeStruct((rows + 2 * WIDE, LANES), jnp.bfloat16)] * count,
-            in_specs=[smem] + [hbm] * 3 + [vmem] * 3,
+            out_shape=[
+                jax.ShapeDtypeStruct(
+                    (rows + 2 * WIDE, SHARE if chunk and step == 1 else LANES), jnp.bfloat16
+                )
+                for step in range(count)
+            ],
+            in_specs=[smem] + [hbm] * 3 + [vmem] * (3 + len(before)),
             out_specs=[vmem] * count,
             scratch_shapes=[pltpu.VMEM((count * rows, LANES), jnp.bfloat16)] * 3
             + [pltpu.VMEM((count * rows + 2 * WIDE, LANES), jnp.bfloat16)]
             + [pltpu.SemaphoreType.DMA((3,))],
             compiler_params=pltpu.CompilerParams(vmem_limit_bytes=40 << 20),
             cost_estimate=pl.CostEstimate(flops=1, bytes_accessed=1, transcendentals=0),
-        )(utt_lengths, query_in, key_in, value_in, *ready)
+        )(utt_lengths, query_in, key_in, value_in, *ready, *before)
         replies += [
-            reply if step == 0 else lax.ppermute(reply, "ctx", facing(count, step))
+            lax.ppermute(reply, "ctx", facing(count, step))
+            if step > 1 or (step == 1 and chunk)
+            else reply
             for step, reply in enumerate(attended)
         ]
+    replies = [replies[0], replies[5], replies[2], replies[3], replies[4], *replies[6:]]
     _, w_near = lax.optimization_barrier((attended, w_near))
     w_far = lax.ppermute(w_near, "dp", swap)
     frames, cotan = frames_in[0], cotangent[0]
@@ -608,7 +633,7 @@
             jax.ShapeDtypeStruct((TAPS + 1, half), jnp.bfloat16),
             jax.ShapeDtypeStruct((PARAM_ROWS, half), jnp.float32),
         ],
-        in_specs=[smem] + [vmem] * (count * CHUNKS + 10),
+        in_specs=[smem] + [vmem] * (count * CHUNKS + 9),
         out_specs=[hbm] + [vmem] * 7,
         scratch_shapes=[
             pltpu.VMEM((2, WIDE + NEAR, features), jnp.bfloat16),

time: 67.9 us -> 66.5 us (0.979)
  starting transfers between devices: 29.2 us -> 27.9 us
    ppermute x6 -> x5, starting transfers between devices: 9.86 us -> 8.33 us  [fast_shards(): lax.ppermute(reply, 'ctx', facing(count, step))]
    ppermute x6 -> x5, waiting for transfers between devices: 10.5 us -> 9.54 us  [fast_shards(): lax.ppermute(one, 'ctx', facing(count, step))]
    ppermute x6 -> x5, waiting for transfers between devices: 4.49 us -> 5.16 us  [fast_shards(): lax.ppermute(reply, 'ctx', facing(count, step))]
    ppermute x6 -> x5, starting transfers between devices: 9.27 us -> 9.46 us  [fast_shards(): lax.ppermute(one, 'ctx', facing(count, step))]
  transfers between devices with their start and end apart: 21 -> 19, of which waited for: 8 -> 7; matrix products, arithmetic and copies ran while one was open for 0% -> 0% of each run, Pallas kernels for 12% -> 12%
where the time goes in v3:
time: 66.5 us; the launch traced here: 66.3 us
  starting transfers between devices  27.9 us (42%)
  Pallas kernels  18.6 us (28%)
  waiting for transfers between devices  18.1 us (27%)
  between operations  1.55 us (2%)
    ppermute x5, waiting for transfers between devices, fast_shards(): lax.ppermute(one, 'ctx', facing(count, step))  9.54 us
    ppermute x5, starting transfers between devices, fast_shards(): lax.ppermute(one, 'ctx', facing(count, step))  9.46 us
    ppermute x5, starting transfers between devices, fast_shards(): lax.ppermute(reply, 'ctx', facing(count, step))  8.33 us
    pallas_call x1, Pallas kernels, fast_shards(): pl.pallas_call(module_kernel, name='conv_module', out_shape=[jax.ShapeDty...  7.8 us
    ppermute x5, waiting for transfers between devices, fast_shards(): lax.ppermute(reply, 'ctx', facing(count, step))  5.16 us
    pallas_call x2, Pallas kernels, fast_shards(): pl.pallas_call(functools.partial(attend_kernel, chunk), name='attend', ou...  4.74 us
    ppermute x3, starting transfers between devices, fast_shards(): lax.ppermute(found, 'ctx', facing(count, step))  4.45 us
    pallas_call x1, Pallas kernels, fast_shards(): pl.pallas_call(backward_kernel, name='conv_backward', out_shape=jax.Shape...  3.44 us
  transfers between devices with their start and end apart: 19, of which 7 were waited for; matrix products, arithmetic and copies ran while one was open for 0% of the time, Pallas kernels for 12%

profile of v3, /device:TPU:0, one launch (start us, length us, event | category | flops | bytes accessed | tf_op | source)
XLA Modules:
  0.0 66.3 jit_solution(6549807606246751474)
XLA Ops:
  0.7 1.9 %pack.1 = (bf16[672,256]{1,0:T(8,128)(2,1)S(1)}, bf16[384,128]{1,0:T(8,128)(2,1)S(1)}, bf16[384,128]{1,0:T(8,128)(2,1)S(1)}, bf16[384,128]{1,0:T(8,128)(2,1)S(1)...) custom-call(bf16[1,128,1024]{2,1,0:T(8,128)(2,1)} %query_ref.3, ...), custom_call_target="tpu_custom_call" | custom-call | tf_op jit(solution)/shard_map/pack/pallas_call | solution.py:549
  2.7 3.0 %collective-permute-start.11 = (bf16[592,768]{1,0:T(8,128)(2,1)S(1)}, bf16[592,768]{1,0:T(8,128)(2,1)S(1)}, u32[]{:S(2)}, u32[]{:S(2)}) collective-permute-start(bf16[592,768]{1,0:T(8,128)(2,1)S(1)} %get-tuple-element.58), channel_id=1, source_target_pairs={{0,2},{2,0},{1,3},{3,1},{4,6},{6,4},{5,7},{7,5},{8,10},{10,8},{9,1... | collective-permute-start | bytes 2727944 | tf_op jit(solution)/shard_map/ppermute | solution.py:584
  5.7 1.6 %collective-permute-start = (bf16[672,256]{1,0:T(8,128)(2,1)S(1)}, bf16[672,256]{1,0:T(8,128)(2,1)S(1)}, u32[]{:S(2)}, u32[]{:S(2)}) collective-permute-start(bf16[672,256]{1,0:T(8,128)(2,1)S(1)} %get-tuple-element.40), channel_id=1, source_target_pairs={{0,4},{4,0},{8,12},{12,8},{1,5},{5,1},{9,13},{13,9},{2,6},{6,2},{1... | collective-permute-start | bytes 1032200 | tf_op jit(solution)/shard_map/ppermute | solution.py:581
  7.3 2.6 %collective-permute-start.1 = (bf16[384,128]{1,0:T(8,128)(2,1)S(1)}, bf16[384,128]{1,0:T(8,128)(2,1)S(1)}, u32[]{:S(2)}, u32[]{:S(2)}) collective-permute-start(bf16[384,128]{1,0:T(8,128)(2,1)S(1)} %get-tuple-element.41), channel_id=1, source_target_pairs={{0,8},{4,12},{8,0},{12,4},{1,9},{5,13},{9,1},{13,5},{2,10},{6,14},... | collective-permute-start | bytes 294920 | tf_op jit(solution)/shard_map/ppermute | solution.py:581
  9.9 0.2 collective-permute-start.2
  10.1 0.7 collective-permute-start.5
  10.7 6.8 %collective-permute-done.1.refs_1_ = bf16[384,128]{1,0:T(8,128)(2,1)S(1)} collective-permute-done((bf16[384,128]{1,0:T(8,128)(2,1)S(1)}, bf16[384,128]{1,0:T(8,128)(2,1)S(1)}, u32[]{:S(2)}, u32[]{:S(2)}) %collective-permute-start.1) | collective-permute-done | bytes 98336 | tf_op jit(solution)/shard_map/ppermute | solution.py:581
  17.5 3.4 %collective-permute-start.3 = (bf16[384,128]{1,0:T(8,128)(2,1)S(1)}, bf16[384,128]{1,0:T(8,128)(2,1)S(1)}, u32[]{:S(2)}, u32[]{:S(2)}) collective-permute-start(bf16[384,128]{1,0:T(8,128)(2,1)S(1)} %get-tuple-element.44), channel_id=1, source_target_pairs={{0,8},{4,12},{8,0},{12,4},{1,9},{5,13},{9,1},{13,5},{2,10},{6,14},... | collective-permute-start | bytes 294920 | tf_op jit(solution)/shard_map/ppermute | solution.py:581
  21.0 0.8 %collective-permute-done.2.refs_2_ = bf16[384,128]{1,0:T(8,128)(2,1)S(1)} collective-permute-done((bf16[384,128]{1,0:T(8,128)(2,1)S(1)}, bf16[384,128]{1,0:T(8,128)(2,1)S(1)}, u32[]{:S(2)}, u32[]{:S(2)}) %collective-permute-start.2) | collective-permute-done | bytes 98336 | tf_op jit(solution)/shard_map/ppermute | solution.py:581
  21.8 1.6 %collective-permute-start.4 = (bf16[384,128]{1,0:T(8,128)(2,1)S(1)}, bf16[384,128]{1,0:T(8,128)(2,1)S(1)}, u32[]{:S(2)}, u32[]{:S(2)}) collective-permute-start(bf16[384,128]{1,0:T(8,128)(2,1)S(1)} %get-tuple-element.45), channel_id=1, source_target_pairs={{0,12},{4,8},{8,4},{12,0},{1,13},{5,9},{9,5},{13,1},{2,14},{6,10},... | collective-permute-start | bytes 294920 | tf_op jit(solution)/shard_map/ppermute | solution.py:581
  24.1 2.4 %attend.2 = (bf16[192,128]{1,0:T(8,128)(2,1)S(1)}, bf16[192,128]{1,0:T(8,128)(2,1)S(1)}, bf16[192,128]{1,0:T(8,128)(2,1)S(1)}, bf16[192,128]{1,0:T(8,128)(2,1)S(1)}) custom-call(s32[1]{0:T(128)S(6)} %copy.15.length_ref.refs_0_, bf16[1,128,1024]{2,1,0:T(8,128)(2,1)S(1)} %copy-done.2, bf16[1,128,1024]{2,1,0:T(8,128)(2,1)S(1)} %copy-done.3, ...), custom_call_target="tpu_custom_call" | custom-call | flops 1 | bytes 1 | tf_op jit(solution)/shard_map/attend/pallas_call | solution.py:593
  26.5 1.9 %collective-permute-done.3.refs_1_ = bf16[384,128]{1,0:T(8,128)(2,1)S(1)} collective-permute-done((bf16[384,128]{1,0:T(8,128)(2,1)S(1)}, bf16[384,128]{1,0:T(8,128)(2,1)S(1)}, u32[]{:S(2)}, u32[]{:S(2)}) %collective-permute-start.3) | collective-permute-done | bytes 98336 | tf_op jit(solution)/shard_map/ppermute | solution.py:581
  28.4 2.4 %attend.3 = (bf16[192,128]{1,0:T(8,128)(2,1)S(1)}, bf16[192,256]{1,0:T(8,128)(2,1)S(1)}, bf16[192,128]{1,0:T(8,128)(2,1)S(1)}, bf16[192,128]{1,0:T(8,128)(2,1)S(1)}) custom-call(s32[1]{0:T(128)S(6)} %copy.15.length_ref.refs_0_, bf16[1,128,1024]{2,1,0:T(8,128)(2,1)S(1)} %copy-done.2, bf16[1,128,1024]{2,1,0:T(8,128)(2,1)S(1)} %copy-done.3, ...), custom_call_target="tpu_custom_call" | custom-call | flops 1 | bytes 1 | tf_op jit(solution)/shard_map/attend/pallas_call | solution.py:593
  30.8 0.1 collective-permute-start.12
  30.9 3.3 %collective-permute-start.9 = (bf16[192,128]{1,0:T(8,128)(2,1)S(1)}, bf16[192,128]{1,0:T(8,128)(2,1)S(1)}, u32[]{:S(2)}, u32[]{:S(2)}) collective-permute-start(bf16[192,128]{1,0:T(8,128)(2,1)S(1)} %get-tuple-element.55), channel_id=1, source_target_pairs={{0,8},{4,12},{8,0},{12,4},{1,9},{5,13},{9,1},{13,5},{2,10},{6,14},... | collective-permute-start | bytes 147464 | tf_op jit(solution)/shard_map/ppermute | solution.py:611
  34.2 0.3 collective-permute-start.6
  34.5 1.3 %collective-permute-start.10 = (bf16[192,128]{1,0:T(8,128)(2,1)S(1)}, bf16[192,128]{1,0:T(8,128)(2,1)S(1)}, u32[]{:S(2)}, u32[]{:S(2)}) collective-permute-start(bf16[192,128]{1,0:T(8,128)(2,1)S(1)} %get-tuple-element.56), channel_id=1, source_target_pairs={{0,12},{4,8},{8,4},{12,0},{1,13},{5,9},{9,5},{13,1},{2,14},{6,10},... | collective-permute-start | bytes 147464 | tf_op jit(solution)/shard_map/ppermute | solution.py:611
  35.8 1.9 %collective-permute-start.7 = (bf16[192,128]{1,0:T(8,128)(2,1)S(1)}, bf16[192,128]{1,0:T(8,128)(2,1)S(1)}, u32[]{:S(2)}, u32[]{:S(2)}) collective-permute-start(bf16[192,128]{1,0:T(8,128)(2,1)S(1)} %get-tuple-element.52), channel_id=1, source_target_pairs={{0,8},{4,12},{8,0},{12,4},{1,9},{5,13},{9,1},{13,5},{2,10},{6,14},... | collective-permute-start | bytes 147464 | tf_op jit(solution)/shard_map/ppermute | solution.py:611
  37.7 1.6 %collective-permute-start.8 = (bf16[192,128]{1,0:T(8,128)(2,1)S(1)}, bf16[192,128]{1,0:T(8,128)(2,1)S(1)}, u32[]{:S(2)}, u32[]{:S(2)}) collective-permute-start(bf16[192,128]{1,0:T(8,128)(2,1)S(1)} %get-tuple-element.53), channel_id=1, source_target_pairs={{0,12},{4,8},{8,4},{12,0},{1,13},{5,9},{9,5},{13,1},{2,14},{6,10},... | collective-permute-start | bytes 147464 | tf_op jit(solution)/shard_map/ppermute | solution.py:611
  39.2 2.3 %collective-permute-done.10.refs_7_ = bf16[192,128]{1,0:T(8,128)(2,1)S(1)} collective-permute-done((bf16[192,128]{1,0:T(8,128)(2,1)S(1)}, bf16[192,128]{1,0:T(8,128)(2,1)S(1)}, u32[]{:S(2)}, u32[]{:S(2)}) %collective-permute-start.10) | collective-permute-done | bytes 49184 | tf_op jit(solution)/shard_map/ppermute | solution.py:611
  41.5 2.9 %collective-permute-done.7.refs_3_ = bf16[192,128]{1,0:T(8,128)(2,1)S(1)} collective-permute-done((bf16[192,128]{1,0:T(8,128)(2,1)S(1)}, bf16[192,128]{1,0:T(8,128)(2,1)S(1)}, u32[]{:S(2)}, u32[]{:S(2)}) %collective-permute-start.7) | collective-permute-done | bytes 49184 | tf_op jit(solution)/shard_map/ppermute | solution.py:611
  44.5 7.8 %conv_module.1 = (bf16[128,1536]{1,0:T(8,128)(2,1)}, f32[12,200,128]{2,1,0:T(8,128)S(1)}, f32[12,168,128]{2,1,0:T(8,128)S(1)}, f32[12,40,128]{2,1,0:T(8,128)S(1)...) custom-call(s32[1]{0:T(128)S(6)} %copy.15.length_ref.refs_0_, ...), custom_call_target="tpu_custom_call" | custom-call | flops 628359168 | bytes 5505024 | tf_op jit(solution)/shard_map/conv_module/pallas_call | solution.py:623
  52.3 0.1 collective-permute-start.14
  52.4 0.6 collective-permute-start.13
  53.0 1.2 %collective-permute-start.15 = (bf16[32,768]{1,0:T(8,128)(2,1)S(1)}, bf16[32,768]{1,0:T(8,128)(2,1)S(1)}, u32[]{:S(2)}, u32[]{:S(2)}) collective-permute-start(bf16[32,768]{1,0:T(8,128)(2,1)S(1)} %get-tuple-element.62), channel_id=1, source_target_pairs={{0,1},{1,0},{2,3},{3,2},{4,5},{5,4},{6,7},{7,6},{8,9},{9,8},{10,11... | collective-permute-start | bytes 147464 | tf_op jit(solution)/shard_map/ppermute | solution.py:670
  54.2 3.4 %conv_backward.1 = bf16[128,1536]{1,0:T(8,128)(2,1)} custom-call(s32[1]{0:T(128)S(6)} %copy.15.length_ref.refs_0_, bf16[128,1536]{1,0:T(8,128)(2,1)S(1)} %bitcast.5, f32[12,200,128]{2,1,0:T(8,128)S(1)} %get-tuple-element.63.normed, f32[12,168,128]{2,1,0:T(8,128)S(1)} %get-tuple-element.64.wide_grad, f32[12,40,128]{2,1,0:T(8,128)S(1)} %get-tuple-element.65.params, ...), custom_call_target="tpu_custom_call" | custom-call | flops 12189696 | bytes 2359296 | tf_op jit(solution)/shard_map/conv_backward/pallas_call | solution.py:672
  57.7 1.8 %collective-permute-start.18 = (bf16[32,768]{1,0:T(8,128)(2,1)S(1)}, bf16[32,768]{1,0:T(8,128)(2,1)S(1)}, u32[]{:S(2)}, u32[]{:S(2)}) collective-permute-start(bf16[32,768]{1,0:T(8,128)(2,1)S(1)} %add_convert_fusion.mine), channel_id=1, source_target_pairs={{0,12},{4,8},{8,4},{12,0},{1,13},{5,9},{9,5},{13,1},{2,14},{6,10},... | collective-permute-start | bytes 147464 | tf_op jit(solution)/shard_map/ppermute | solution.py:692
  59.5 0.8 %collective-permute-start.17 = (bf16[32,768]{1,0:T(8,128)(2,1)S(1)}, bf16[32,768]{1,0:T(8,128)(2,1)S(1)}, u32[]{:S(2)}, u32[]{:S(2)}) collective-permute-start(bf16[32,768]{1,0:T(8,128)(2,1)S(1)} %add_convert_fusion.mine), channel_id=1, source_target_pairs={{0,8},{4,12},{8,0},{12,4},{1,9},{5,13},{9,1},{13,5},{2,10},{6,14},... | collective-permute-start | bytes 147464 | tf_op jit(solution)/shard_map/ppermute | solution.py:692
  60.3 1.8 %collective-permute-start.16 = (bf16[32,768]{1,0:T(8,128)(2,1)S(1)}, bf16[32,768]{1,0:T(8,128)(2,1)S(1)}, u32[]{:S(2)}, u32[]{:S(2)}) collective-permute-start(bf16[32,768]{1,0:T(8,128)(2,1)S(1)} %add_convert_fusion.mine), channel_id=1, source_target_pairs={{0,4},{4,0},{8,12},{12,8},{1,5},{5,1},{9,13},{13,9},{2,6},{6,2},{1... | collective-permute-start | bytes 147464 | tf_op jit(solution)/shard_map/ppermute | solution.py:692
  62.2 1.7 %collective-permute-done.18.three = bf16[32,768]{1,0:T(8,128)(2,1)S(1)} collective-permute-done((bf16[32,768]{1,0:T(8,128)(2,1)S(1)}, bf16[32,768]{1,0:T(8,128)(2,1)S(1)}, u32[]{:S(2)}, u32[]{:S(2)}) %collective-permute-start.18) | collective-permute-done | bytes 49184 | tf_op jit(solution)/shard_map/ppermute | solution.py:692
  63.9 1.7 %collective-permute-done.17.two = bf16[32,768]{1,0:T(8,128)(2,1)S(1)} collective-permute-done((bf16[32,768]{1,0:T(8,128)(2,1)S(1)}, bf16[32,768]{1,0:T(8,128)(2,1)S(1)}, u32[]{:S(2)}, u32[]{:S(2)}) %collective-permute-start.17) | collective-permute-done | bytes 49184 | tf_op jit(solution)/shard_map/ppermute | solution.py:692
  65.6 0.7 %finish.1 = (f32[31,768]{1,0:T(8,128)}, f32[768]{0:T(1024)}, f32[768]{0:T(1024)}) custom-call(bf16[32,768]{1,0:T(8,128)(2,1)S(1)} %add_convert_fusion.mine, bf16[32,768]{1,0:T(8,128)(2,1)S(1)} %collective-permute-done.16.one, bf16[32,768]{1,0:T(8,128)(2,1)S(1)} %collective-permute-done.17.two, bf16[32,768]{1,0:T(8,128)(2,1)S(1)} %collective-permute-done.18.three, ...), custom_call_target="tpu_custom_call" | custom-call | tf_op jit(solution)/shard_map/finish/pallas_call | solution.py:694
  (31 shorter events, 0.1 us)
Async XLA Ops:
  0.6 23.5 %copy-start.4 = (bf16[1,128,1024]{2,1,0:T(8,128)(2,1)S(1)}, bf16[1,128,1024]{2,1,0:T(8,128)(2,1)}, u32[]{:S(2)}) copy-start(bf16[1,128,1024]{2,1,0:T(8,128)(2,1)} %value_ref.3) | copy-start | bytes 786436
  0.6 23.5 %copy-start.3 = (bf16[1,128,1024]{2,1,0:T(8,128)(2,1)S(1)}, bf16[1,128,1024]{2,1,0:T(8,128)(2,1)}, u32[]{:S(2)}) copy-start(bf16[1,128,1024]{2,1,0:T(8,128)(2,1)} %key_ref.3) | copy-start | bytes 786436
  0.7 23.5 %copy-start.2 = (bf16[1,128,1024]{2,1,0:T(8,128)(2,1)S(1)}, bf16[1,128,1024]{2,1,0:T(8,128)(2,1)}, u32[]{:S(2)}) copy-start(bf16[1,128,1024]{2,1,0:T(8,128)(2,1)} %query_ref.3) | copy-start | bytes 786436
  2.6 41.8 %copy-start = (bf16[1024,768]{1,0:T(8,128)(2,1)S(1)}, bf16[1024,768]{1,0:T(8,128)(2,1)}, u32[]{:S(2)}) copy-start(bf16[1024,768]{1,0:T(8,128)(2,1)} %refs_12_.1) | copy-start | bytes 4718596
  2.6 41.8 %copy-start.1 = (bf16[1,128,1536]{2,1,0:T(8,128)(2,1)S(1)}, bf16[1,128,1536]{2,1,0:T(8,128)(2,1)}, u32[]{:S(2)}) copy-start(bf16[1,128,1536]{2,1,0:T(8,128)(2,1)} %refs_4_.1) | copy-start | bytes 1179652
  2.6 41.8 %copy-start.5 = (bf16[1,128,1536]{2,1,0:T(8,128)(2,1)S(1)}, bf16[1,128,1536]{2,1,0:T(8,128)(2,1)}, u32[]{:S(2)}) copy-start(bf16[1,128,1536]{2,1,0:T(8,128)(2,1)} %refs_3_.1) | copy-start | bytes 1179652
  2.7 41.8 %copy-start.6 = (f32[31,768]{1,0:T(8,128)S(1)}, f32[31,768]{1,0:T(8,128)}, u32[]{:S(2)}) copy-start(f32[31,768]{1,0:T(8,128)} %refs_15_.1) | copy-start | bytes 285700
  2.7 41.8 %copy-start.7 = (f32[768]{0:T(1024)S(1)}, f32[768]{0:T(1024)}, u32[]{:S(2)}) copy-start(f32[768]{0:T(1024)} %refs_16_.1) | copy-start | bytes 9220
  2.7 41.8 %copy-start.8 = (f32[768]{0:T(1024)S(1)}, f32[768]{0:T(1024)}, u32[]{:S(2)}) copy-start(f32[768]{0:T(1024)} %refs_17_.1) | copy-start | bytes 9220
  2.7 28.1 %collective-permute-start.11 = (bf16[592,768]{1,0:T(8,128)(2,1)S(1)}, bf16[592,768]{1,0:T(8,128)(2,1)S(1)}, u32[]{:S(2)}, u32[]{:S(2)}) collective-permute-start(bf16[592,768]{1,0:T(8,128)(2,1)S(1)} %get-tuple-element.58), channel_id=1, source_target_pairs={{0,2},{2,0},{1,3},{3,1},{4,6},{6,4},{5,7},{7,5},{8,10},{10,8},{9,1... | collective-permute-start | bytes 2727944 | tf_op jit(solution)/shard_map/ppermute | solution.py:584
  5.7 18.4 %collective-permute-start = (bf16[672,256]{1,0:T(8,128)(2,1)S(1)}, bf16[672,256]{1,0:T(8,128)(2,1)S(1)}, u32[]{:S(2)}, u32[]{:S(2)}) collective-permute-start(bf16[672,256]{1,0:T(8,128)(2,1)S(1)} %get-tuple-element.40), channel_id=1, source_target_pairs={{0,4},{4,0},{8,12},{12,8},{1,5},{5,1},{9,13},{13,9},{2,6},{6,2},{1... | collective-permute-start | bytes 1032200 | tf_op jit(solution)/shard_map/ppermute | solution.py:581
  7.3 10.2 %collective-permute-start.1 = (bf16[384,128]{1,0:T(8,128)(2,1)S(1)}, bf16[384,128]{1,0:T(8,128)(2,1)S(1)}, u32[]{:S(2)}, u32[]{:S(2)}) collective-permute-start(bf16[384,128]{1,0:T(8,128)(2,1)S(1)} %get-tuple-element.41), channel_id=1, source_target_pairs={{0,8},{4,12},{8,0},{12,4},{1,9},{5,13},{9,1},{13,5},{2,10},{6,14},... | collective-permute-start | bytes 294920 | tf_op jit(solution)/shard_map/ppermute | solution.py:581
  9.9 11.9 %collective-permute-start.2 = (bf16[384,128]{1,0:T(8,128)(2,1)S(1)}, bf16[384,128]{1,0:T(8,128)(2,1)S(1)}, u32[]{:S(2)}, u32[]{:S(2)}) collective-permute-start(bf16[384,128]{1,0:T(8,128)(2,1)S(1)} %get-tuple-element.42), channel_id=1, source_target_pairs={{0,12},{4,8},{8,4},{12,0},{1,13},{5,9},{9,5},{13,1},{2,14},{6,10},... | collective-permute-start | bytes 294920 | tf_op jit(solution)/shard_map/ppermute | solution.py:581
  10.1 18.4 %collective-permute-start.5 = (bf16[48,1536]{1,0:T(8,128)(2,1)S(1)}, bf16[48,1536]{1,0:T(8,128)(2,1)S(1)}, u32[]{:S(2)}, u32[]{:S(2)}) collective-permute-start(bf16[48,1536]{1,0:T(8,128)(2,1)S(1)} %get-tuple-element.46), channel_id=1, source_target_pairs={{4,8},{8,4},{5,9},{9,5},{6,10},{10,6},{7,11},{11,7},{20,24},{24,20... | collective-permute-start | bytes 442376 | tf_op jit(solution)/shard_map/ppermute | solution.py:583
  17.5 10.9 %collective-permute-start.3 = (bf16[384,128]{1,0:T(8,128)(2,1)S(1)}, bf16[384,128]{1,0:T(8,128)(2,1)S(1)}, u32[]{:S(2)}, u32[]{:S(2)}) collective-permute-start(bf16[384,128]{1,0:T(8,128)(2,1)S(1)} %get-tuple-element.44), channel_id=1, source_target_pairs={{0,8},{4,12},{8,0},{12,4},{1,9},{5,13},{9,1},{13,5},{2,10},{6,14},... | collective-permute-start | bytes 294920 | tf_op jit(solution)/shard_map/ppermute | solution.py:581
  21.8 6.6 %collective-permute-start.4 = (bf16[384,128]{1,0:T(8,128)(2,1)S(1)}, bf16[384,128]{1,0:T(8,128)(2,1)S(1)}, u32[]{:S(2)}, u32[]{:S(2)}) collective-permute-start(bf16[384,128]{1,0:T(8,128)(2,1)S(1)} %get-tuple-element.45), channel_id=1, source_target_pairs={{0,12},{4,8},{8,4},{12,0},{1,13},{5,9},{9,5},{13,1},{2,14},{6,10},... | collective-permute-start | bytes 294920 | tf_op jit(solution)/shard_map/ppermute | solution.py:581
  30.8 13.6 %collective-permute-start.12 = (bf16[592,768]{1,0:T(8,128)(2,1)S(1)}, bf16[592,768]{1,0:T(8,128)(2,1)S(1)}, u32[]{:S(2)}, u32[]{:S(2)}) collective-permute-start(bf16[592,768]{1,0:T(8,128)(2,1)S(1)} %collective-permute-done.11.refs_13_), channel_id=1, source_target_pairs={{0,1},{1,0},{2,3},{3,2},{4,5},{5,4},{6,7},{7,6},{8,9},{9,8},{10,11... | collective-permute-start | bytes 2727944 | tf_op jit(solution)/shard_map/ppermute | solution.py:618
  30.9 6.8 %collective-permute-start.9 = (bf16[192,128]{1,0:T(8,128)(2,1)S(1)}, bf16[192,128]{1,0:T(8,128)(2,1)S(1)}, u32[]{:S(2)}, u32[]{:S(2)}) collective-permute-start(bf16[192,128]{1,0:T(8,128)(2,1)S(1)} %get-tuple-element.55), channel_id=1, source_target_pairs={{0,8},{4,12},{8,0},{12,4},{1,9},{5,13},{9,1},{13,5},{2,10},{6,14},... | collective-permute-start | bytes 147464 | tf_op jit(solution)/shard_map/ppermute | solution.py:611
  34.2 10.2 %collective-permute-start.6 = (bf16[192,256]{1,0:T(8,128)(2,1)S(1)}, bf16[192,256]{1,0:T(8,128)(2,1)S(1)}, u32[]{:S(2)}, u32[]{:S(2)}) collective-permute-start(bf16[192,256]{1,0:T(8,128)(2,1)S(1)} %get-tuple-element.51), channel_id=1, source_target_pairs={{0,4},{4,0},{8,12},{12,8},{1,5},{5,1},{9,13},{13,9},{2,6},{6,2},{1... | collective-permute-start | bytes 294920 | tf_op jit(solution)/shard_map/ppermute | solution.py:611
  34.5 7.0 %collective-permute-start.10 = (bf16[192,128]{1,0:T(8,128)(2,1)S(1)}, bf16[192,128]{1,0:T(8,128)(2,1)S(1)}, u32[]{:S(2)}, u32[]{:S(2)}) collective-permute-start(bf16[192,128]{1,0:T(8,128)(2,1)S(1)} %get-tuple-element.56), channel_id=1, source_target_pairs={{0,12},{4,8},{8,4},{12,0},{1,13},{5,9},{9,5},{13,1},{2,14},{6,10},... | collective-permute-start | bytes 147464 | tf_op jit(solution)/shard_map/ppermute | solution.py:611
  35.8 8.6 %collective-permute-start.7 = (bf16[192,128]{1,0:T(8,128)(2,1)S(1)}, bf16[192,128]{1,0:T(8,128)(2,1)S(1)}, u32[]{:S(2)}, u32[]{:S(2)}) collective-permute-start(bf16[192,128]{1,0:T(8,128)(2,1)S(1)} %get-tuple-element.52), channel_id=1, source_target_pairs={{0,8},{4,12},{8,0},{12,4},{1,9},{5,13},{9,1},{13,5},{2,10},{6,14},... | collective-permute-start | bytes 147464 | tf_op jit(solution)/shard_map/ppermute | solution.py:611
  37.7 6.7 %collective-permute-start.8 = (bf16[192,128]{1,0:T(8,128)(2,1)S(1)}, bf16[192,128]{1,0:T(8,128)(2,1)S(1)}, u32[]{:S(2)}, u32[]{:S(2)}) collective-permute-start(bf16[192,128]{1,0:T(8,128)(2,1)S(1)} %get-tuple-element.53), channel_id=1, source_target_pairs={{0,12},{4,8},{8,4},{12,0},{1,13},{5,9},{9,5},{13,1},{2,14},{6,10},... | collective-permute-start | bytes 147464 | tf_op jit(solution)/shard_map/ppermute | solution.py:611
  52.3 5.4 %collective-permute-start.14 = (bf16[32,768]{1,0:T(8,128)(2,1)S(1)}, bf16[32,768]{1,0:T(8,128)(2,1)S(1)}, u32[]{:S(2)}, u32[]{:S(2)}) collective-permute-start(bf16[32,768]{1,0:T(8,128)(2,1)S(1)} %get-tuple-element.61), channel_id=1, source_target_pairs={{0,3},{3,0},{1,2},{2,1},{4,7},{7,4},{5,6},{6,5},{8,11},{11,8},{9,1... | collective-permute-start | bytes 147464 | tf_op jit(solution)/shard_map/ppermute | solution.py:669
  52.4 5.3 %collective-permute-start.13 = (bf16[32,768]{1,0:T(8,128)(2,1)S(1)}, bf16[32,768]{1,0:T(8,128)(2,1)S(1)}, u32[]{:S(2)}, u32[]{:S(2)}) collective-permute-start(bf16[32,768]{1,0:T(8,128)(2,1)S(1)} %get-tuple-element.61), channel_id=1, source_target_pairs={{0,2},{2,0},{1,3},{3,1},{4,6},{6,4},{5,7},{7,5},{8,10},{10,8},{9,1... | collective-permute-start | bytes 147464 | tf_op jit(solution)/shard_map/ppermute | solution.py:668
  53.0 4.7 %collective-permute-start.15 = (bf16[32,768]{1,0:T(8,128)(2,1)S(1)}, bf16[32,768]{1,0:T(8,128)(2,1)S(1)}, u32[]{:S(2)}, u32[]{:S(2)}) collective-permute-start(bf16[32,768]{1,0:T(8,128)(2,1)S(1)} %get-tuple-element.62), channel_id=1, source_target_pairs={{0,1},{1,0},{2,3},{3,2},{4,5},{5,4},{6,7},{7,6},{8,9},{9,8},{10,11... | collective-permute-start | bytes 147464 | tf_op jit(solution)/shard_map/ppermute | solution.py:670
  57.7 6.1 %collective-permute-start.18 = (bf16[32,768]{1,0:T(8,128)(2,1)S(1)}, bf16[32,768]{1,0:T(8,128)(2,1)S(1)}, u32[]{:S(2)}, u32[]{:S(2)}) collective-permute-start(bf16[32,768]{1,0:T(8,128)(2,1)S(1)} %add_convert_fusion.mine), channel_id=1, source_target_pairs={{0,12},{4,8},{8,4},{12,0},{1,13},{5,9},{9,5},{13,1},{2,14},{6,10},... | collective-permute-start | bytes 147464 | tf_op jit(solution)/shard_map/ppermute | solution.py:692
  59.5 6.0 %collective-permute-start.17 = (bf16[32,768]{1,0:T(8,128)(2,1)S(1)}, bf16[32,768]{1,0:T(8,128)(2,1)S(1)}, u32[]{:S(2)}, u32[]{:S(2)}) collective-permute-start(bf16[32,768]{1,0:T(8,128)(2,1)S(1)} %add_convert_fusion.mine), channel_id=1, source_target_pairs={{0,8},{4,12},{8,0},{12,4},{1,9},{5,13},{9,1},{13,5},{2,10},{6,14},... | collective-permute-start | bytes 147464 | tf_op jit(solution)/shard_map/ppermute | solution.py:692
  60.3 5.2 %collective-permute-start.16 = (bf16[32,768]{1,0:T(8,128)(2,1)S(1)}, bf16[32,768]{1,0:T(8,128)(2,1)S(1)}, u32[]{:S(2)}, u32[]{:S(2)}) collective-permute-start(bf16[32,768]{1,0:T(8,128)(2,1)S(1)} %add_convert_fusion.mine), channel_id=1, source_target_pairs={{0,4},{4,0},{8,12},{12,8},{1,5},{5,1},{9,13},{13,9},{2,6},{6,2},{1... | collective-permute-start | bytes 147464 | tf_op jit(solution)/shard_map/ppermute | solution.py:692

commit v4 on v3

--- a/solution.py
+++ b/solution.py
@@ -275,7 +275,7 @@
 
 def attend_kernel(chunk, length_ref, query_ref, key_ref, value_ref, *refs):
     parts, refs = refs[:3], refs[3:]
-    before, refs = refs[:chunk], refs[chunk:]
+    before, refs = refs[: 4 * chunk], refs[4 * chunk :]
     outs = refs[:4]
     query_all, key_all, value_all, attended, sems = refs[4:]
     place, valid_len = lax.axis_index("ctx"), length_ref[0]
@@ -328,8 +328,8 @@
     for step in range(4):
         owner = place ^ step
         found = attended[pl.ds(pl.multiple_of(owner * rows, rows), rows + 2 * WIDE), :]
-        if step == 1 and chunk:
-            outs[step][:, :LANES] = before[0][...]
+        if chunk:
+            outs[step][:, :LANES] = before[step][...]
             outs[step][:, LANES:] = found
         else:
             outs[step][...] = found
@@ -339,72 +339,77 @@
     return [[o for o in range(first, last + 1) if o % 8 == r] for r in range(8)]
 
 
-def module_kernel(*refs):
-    count = 4
-    length_ref, *replies = refs[: 1 + count * CHUNKS - 1]
+def live_at(length_ref, rows, first, length):
+    position = lax.axis_index("ctx") * rows + first + lax.broadcasted_iota(jnp.int32, (length, 1), 0)
+    return ((position >= 0) & (position < length_ref[0])).astype(jnp.float32)
+
+
+def weight_block(w_own, w_near, w_far, part, tile, mine):
+    cols = slice(tile * LANES, (tile + 1) * LANES)
+    if mine:
+        return w_own[pl.ds(pl.multiple_of(part * SHARE, SHARE), SHARE), cols]
+    per_part = (w_near.shape[0] - 2 * PARAM_ROWS) // SHARE
+    rows = pl.ds(pl.multiple_of(lax.rem(part, per_part) * SHARE, SHARE), SHARE)
+    near = lax.div(part, per_part) == lax.axis_index("dp")
+    return jnp.where(near, w_near[rows, cols], w_far[rows, cols])
+
+
+def prepare_kernel(*refs):
     (
-        frames_ref, cotan_ref, beside_ref, edge_ref, w_own, w_near, w_far, taps_ref, bias_ref, gain_ref,
-        block_hbm, normed, wide_grad, params, inv_rows, sums_own, sums_other, par_mine,
-        edges, attended, sums, partial, block_out, out_sems,
-    ) = refs[count * CHUNKS :]
-    place, side, core = lax.axis_index("ctx"), lax.axis_index("fsdp"), lax.axis_index("dp")
-    valid_len = length_ref[0]
+        length_ref, own_ref, frames_ref, cotan_ref, beside_ref, edge_ref, w_own, w_near, w_far,
+        taps_ref, bias_ref, gain_ref, base, cotan_live, params, par_mine, edges,
+    ) = refs
+    place, side = lax.axis_index("ctx"), lax.axis_index("fsdp")
     rows, features = frames_ref.shape
-    half = features // 2
-    tiles, half_tiles = features // LANES, half // LANES
-    ext, near = rows + 2 * WIDE, rows + 2 * NEAR
-    depth = SHARE
+    half_tiles = features // 2 // LANES
     weight_rows = w_near.shape[0] - 2 * PARAM_ROWS
-    per_part = weight_rows // depth
-
     even = 1 - lax.rem(place, 2)
     for block in range(features // SHARE):
-        base = 3 * rows + block * (WIDE + NEAR)
-        edges[even, :, block * SHARE : (block + 1) * SHARE] = beside_ref[base : base + WIDE + NEAR, :]
+        first = 3 * rows + block * (WIDE + NEAR)
+        edges[even, :, block * SHARE : (block + 1) * SHARE] = beside_ref[first : first + WIDE + NEAR, :]
     edges[1 - even] = edge_ref[...]
-
-    def live(first, length):
-        position = place * rows + first + lax.broadcasted_iota(jnp.int32, (length, 1), 0)
-        return ((position >= 0) & (position < valid_len)).astype(jnp.float32)
-
-    for step in range(count):
-        if step == 1:
-            attended[place ^ step] = replies[1][...]
-            continue
-        for chunk in range(CHUNKS):
-            cols = slice(chunk * LANES, (chunk + 1) * LANES)
-            attended[place ^ step, :, cols] = replies[(0, 4)[chunk] + (step - chunk if step else 0)][...]
     par_own = parameters(taps_ref, bias_ref, gain_ref)
     par_mine[...] = par_own
     par_other = w_near[weight_rows : weight_rows + PARAM_ROWS, :].astype(jnp.float32)
     par_other += w_near[weight_rows + PARAM_ROWS :, :].astype(jnp.float32)
+    live_near = live_at(length_ref, rows, -NEAR, rows + 2 * NEAR)
+    own = own_ref[...]
+    row = lax.broadcasted_iota(jnp.int32, (PARAM_ROWS, 1), 0)
     for tile in range(half_tiles):
         cols = slice(tile * LANES, (tile + 1) * LANES)
-        for source, base in ((par_own, side * half_tiles), (par_other, (1 - side) * half_tiles)):
+        for mine, source in ((True, par_own), (False, par_other)):
+            at = (side if mine else 1 - side) * half_tiles + tile
             values = source[:, cols]
-            gain = values[TAPS + 1 : TAPS + 2]
-            row = lax.broadcasted_iota(jnp.int32, (PARAM_ROWS, 1), 0)
-            params[base + tile] = jnp.where(row < TAPS, values * gain, values)
-
+            params[at] = jnp.where(row < TAPS, values * values[TAPS + 1 : TAPS + 2], values)
+            span = pl.ds(pl.multiple_of(at * LANES, LANES), LANES)
+            weight = weight_block(w_own, w_near, w_far, place, tile, mine)
+            base[at] = jnp.dot(own, weight, preferred_element_type=jnp.float32) + jnp.concatenate(
+                [edges[0, 0:WIDE, span], frames_ref[:, span], edges[1, 0:WIDE, span]], axis=0
+            ).astype(jnp.float32)
+            cotan_live[at] = live_near * jnp.concatenate(
+                [edges[0, WIDE:, span], cotan_ref[:, span], edges[1, WIDE:, span]], axis=0
+            ).astype(jnp.float32)
+
+
+def module_kernel(*refs):
+    (
+        length_ref, reply_one, reply_two, reply_three, base, cotan_live, params, w_own, w_near, w_far,
+        block_hbm, normed, wide_grad, inv_rows, sums_own, sums_other,
+        sums, partial, block_out, out_sems,
+    ) = refs
+    place, side = lax.axis_index("ctx"), lax.axis_index("fsdp")
+    tiles, ext = base.shape[:2]
+    rows, features = ext - 2 * WIDE, tiles * LANES
+    half_tiles, near = tiles // 2, rows + 2 * NEAR
     for tile in range(half_tiles):
-        cols = slice(tile * LANES, (tile + 1) * LANES)
         for mine in (True, False):
             at = (side if mine else 1 - side) * half_tiles + tile
             span = pl.ds(pl.multiple_of(at * LANES, LANES), LANES)
-            product = jnp.zeros((ext, LANES), jnp.float32)
-            for part in range(count):
-                if mine:
-                    index, weight = part, w_own[part * depth : (part + 1) * depth, cols]
-                else:
-                    inner = part % per_part
-                    source = w_near if part < per_part else w_far
-                    index = (core if part < per_part else 1 - core) * per_part + inner
-                    weight = source[inner * depth : (inner + 1) * depth, cols]
-                product += jnp.dot(attended[index], weight, preferred_element_type=jnp.float32)
-            residual = jnp.concatenate(
-                [edges[0, 0:WIDE, span], frames_ref[:, span], edges[1, 0:WIDE, span]], axis=0
-            )
-            hidden = (residual.astype(jnp.float32) + product).astype(jnp.bfloat16)
+            product = base[at]
+            for step, reply in enumerate((reply_one, reply_two, reply_three), 1):
+                weight = weight_block(w_own, w_near, w_far, place ^ step, tile, mine)
+                product += jnp.dot(reply[...], weight, preferred_element_type=jnp.float32)
+            hidden = product.astype(jnp.bfloat16)
             block_out[:, span] = hidden[WIDE : WIDE + rows]
             normed[at, 0:ext] = hidden.astype(jnp.float32)
 
@@ -418,12 +423,11 @@
         total += centered * centered
     variance = jnp.sum(total, axis=1, keepdims=True) * (1.0 / features)
     inv_scale = lax.rsqrt(variance + 1e-05)
-    scale = inv_scale * live(-WIDE, ext)
+    scale = inv_scale * live_at(length_ref, rows, -WIDE, ext)
     for tile in range(tiles):
         normed[tile, 0:ext] = (normed[tile, 0:ext] - average) * scale
 
-    live_near = live(-NEAR, near)
-    live_rows = live(0, rows)
+    live_rows = live_at(length_ref, rows, 0, rows)
     inv_rows[...] = jnp.broadcast_to(inv_scale[WIDE : WIDE + rows], inv_rows.shape)
 
     def one_tile(tile, carry):
@@ -442,10 +446,7 @@
         pltpu.make_async_copy(
             block_out.at[:, span], block_hbm.at[:, span], out_sems.at[tile]
         ).start()
-        cotan = jnp.concatenate(
-            [edges[0, WIDE:, span], cotan_ref[:, span], edges[1, WIDE:, span]], axis=0
-        ).astype(jnp.float32)
-        grad_pre = cotan * live_near * gate * (1.0 + pre_act * (1.0 - gate))
+        grad_pre = cotan_live[tile] * gate * (1.0 + pre_act * (1.0 - gate))
         wide_grad[tile, 0:near] = grad_pre
         own_grad = grad_pre[here]
         first = WIDE - HALF
@@ -471,11 +472,9 @@
         pltpu.make_async_copy(block_out.at[:, cols], block_hbm.at[:, cols], out_sems.at[tile]).wait()
 
 
-def backward_kernel(length_ref, cotan_ref, normed, wide_grad, params, inv_rows, grad_hbm, grad_hat, mean_one, mean_two, hidden_grad, out_sems):
-    rows, features = cotan_ref.shape
-    tiles = features // LANES
-    position = lax.axis_index("ctx") * rows + lax.broadcasted_iota(jnp.int32, (rows, 1), 0)
-    live_rows = (position < length_ref[0]).astype(jnp.float32)
+def backward_kernel(length_ref, normed, wide_grad, params, grad_hat, means, mean_one, mean_two):
+    tiles, rows = grad_hat.shape[:2]
+    live_rows = live_at(length_ref, rows, 0, rows)
     mean_one[...] = jnp.zeros_like(mean_one)
     mean_two[...] = jnp.zeros_like(mean_two)
 
@@ -494,18 +493,26 @@
         return carry
 
     lax.fori_loop(0, tiles, one_tile, 0)
-    first_mean = jnp.sum(mean_one[...], axis=1, keepdims=True) * (1.0 / features)
-    second_mean = jnp.sum(mean_two[...], axis=1, keepdims=True) * (1.0 / features)
+    for index, total in enumerate((mean_one, mean_two)):
+        mean = jnp.sum(total[...], axis=1, keepdims=True) * (1.0 / (tiles * LANES))
+        means[index] = jnp.broadcast_to(mean, (rows, LANES))
+
+
+def hidden_grad_kernel(cotan_ref, normed, inv_rows, grad_hat, means, grad_hbm, hidden_grad, out_sems):
+    tiles, rows = grad_hat.shape[:2]
+    copies = []
     for tile in range(tiles):
         cols = slice(tile * LANES, (tile + 1) * LANES)
-        inner = grad_hat[tile] - first_mean - normed[tile, WIDE : WIDE + rows] * second_mean
+        inner = grad_hat[tile] - means[0] - normed[tile, WIDE : WIDE + rows] * means[1]
         hidden_grad[:, cols] = (
             cotan_ref[:, cols].astype(jnp.float32) + inner * inv_rows[...]
         ).astype(hidden_grad.dtype)
-        pltpu.make_async_copy(hidden_grad.at[:, cols], grad_hbm.at[:, cols], out_sems.at[tile]).start()
-    for tile in range(tiles):
-        cols = slice(tile * LANES, (tile + 1) * LANES)
-        pltpu.make_async_copy(hidden_grad.at[:, cols], grad_hbm.at[:, cols], out_sems.at[tile]).wait()
+        copies.append(
+            pltpu.make_async_copy(hidden_grad.at[:, cols], grad_hbm.at[:, cols], out_sems.at[tile])
+        )
+        copies[-1].start()
+    for copy in copies:
+        copy.wait()
 
 
 def finish_kernel(factor, mine, one, two, three, params, kernel_out, bias_out, gain_out, terms):
@@ -583,22 +590,20 @@
     edge = lax.ppermute(edge, "ctx", [(1, 2), (2, 1)])
     w_near = lax.ppermute(w_sent, "fsdp", swap)
 
-    replies, attended = [], []
+    attended = []
     for chunk in range(CHUNKS):
         ready = [parts[0], *parts[2 * chunk + 1 : 2 * chunk + 3]]
         before = []
         if chunk:
-            before = [attended[1]]
+            before = attended
             ready, edge = lax.optimization_barrier((ready, edge))
         attended = pl.pallas_call(
             functools.partial(attend_kernel, chunk),
             name="attend",
             out_shape=[
-                jax.ShapeDtypeStruct(
-                    (rows + 2 * WIDE, SHARE if chunk and step == 1 else LANES), jnp.bfloat16
-                )
-                for step in range(count)
-            ],
+                jax.ShapeDtypeStruct((rows + 2 * WIDE, (chunk + 1) * LANES), jnp.bfloat16)
+            ]
+            * count,
             in_specs=[smem] + [hbm] * 3 + [vmem] * (3 + len(before)),
             out_specs=[vmem] * count,
             scratch_shapes=[pltpu.VMEM((count * rows, LANES), jnp.bfloat16)] * 3
@@ -607,37 +612,60 @@
             compiler_params=pltpu.CompilerParams(vmem_limit_bytes=40 << 20),
             cost_estimate=pl.CostEstimate(flops=1, bytes_accessed=1, transcendentals=0),
         )(utt_lengths, query_in, key_in, value_in, *ready, *before)
-        replies += [
-            lax.ppermute(reply, "ctx", facing(count, step))
-            if step > 1 or (step == 1 and chunk)
-            else reply
-            for step, reply in enumerate(attended)
-        ]
-    replies = [replies[0], replies[5], replies[2], replies[3], replies[4], *replies[6:]]
+    own, *replies = [
+        reply if step == 0 else lax.ppermute(reply, "ctx", facing(count, step))
+        for step, reply in enumerate(attended)
+    ]
     _, w_near = lax.optimization_barrier((attended, w_near))
     w_far = lax.ppermute(w_near, "dp", swap)
     frames, cotan = frames_in[0], cotangent[0]
 
     ext, near = rows + 2 * WIDE, rows + 2 * NEAR
     tiles = features // LANES
-    block_out, normed, wide_grad, params, inv_rows, sums_own, sums_other, par_mine = pl.pallas_call(
+    base, cotan_live, params, par_mine = pl.pallas_call(
+        prepare_kernel,
+        name="prepare",
+        out_shape=[
+            jax.ShapeDtypeStruct((tiles, ext, LANES), jnp.float32),
+            jax.ShapeDtypeStruct((tiles, near, LANES), jnp.float32),
+            jax.ShapeDtypeStruct((tiles, PARAM_ROWS, LANES), jnp.float32),
+            jax.ShapeDtypeStruct((PARAM_ROWS, half), jnp.float32),
+        ],
+        in_specs=[smem] + [vmem] * 11,
+        out_specs=[vmem] * 4,
+        scratch_shapes=[pltpu.VMEM((2, WIDE + NEAR, features), jnp.bfloat16)],
+        compiler_params=pltpu.CompilerParams(vmem_limit_bytes=32 << 20),
+        cost_estimate=pl.CostEstimate(
+            flops=2 * ext * SHARE * features, bytes_accessed=8 * rows * features, transcendentals=0
+        ),
+    )(
+        utt_lengths,
+        own,
+        frames,
+        cotan,
+        parts[0],
+        edge,
+        out_weight,
+        w_near,
+        w_far,
+        conv_kernel,
+        conv_bias,
+        ln_gain,
+    )
+    block_out, normed, wide_grad, inv_rows, sums_own, sums_other = pl.pallas_call(
         module_kernel,
         name="conv_module",
         out_shape=[
             jax.ShapeDtypeStruct((rows, features), jnp.bfloat16),
             jax.ShapeDtypeStruct((tiles, ext + 8, LANES), jnp.float32),
             jax.ShapeDtypeStruct((tiles, near + 8, LANES), jnp.float32),
-            jax.ShapeDtypeStruct((tiles, PARAM_ROWS, LANES), jnp.float32),
             jax.ShapeDtypeStruct((rows, LANES), jnp.float32),
             jax.ShapeDtypeStruct((TAPS + 1, half), jnp.bfloat16),
             jax.ShapeDtypeStruct((TAPS + 1, half), jnp.bfloat16),
-            jax.ShapeDtypeStruct((PARAM_ROWS, half), jnp.float32),
         ],
-        in_specs=[smem] + [vmem] * (count * CHUNKS + 9),
-        out_specs=[hbm] + [vmem] * 7,
+        in_specs=[smem] + [vmem] * 9,
+        out_specs=[hbm] + [vmem] * 5,
         scratch_shapes=[
-            pltpu.VMEM((2, WIDE + NEAR, features), jnp.bfloat16),
-            pltpu.VMEM((count, ext, SHARE), jnp.bfloat16),
             pltpu.VMEM((tiles, TAPS + 1, LANES), jnp.float32),
             pltpu.VMEM((TAPS + 1, 8, LANES), jnp.float32),
             pltpu.VMEM((rows, features), jnp.bfloat16),
@@ -652,16 +680,12 @@
     )(
         utt_lengths,
         *replies,
-        frames,
-        cotan,
-        parts[0],
-        edge,
+        base,
+        cotan_live,
+        params,
         out_weight,
         w_near,
         w_far,
-        conv_kernel,
-        conv_bias,
-        ln_gain,
     )
 
     pairs = [
@@ -669,27 +693,44 @@
         lax.ppermute(sums_other, ("fsdp", "dp"), [(0, 3), (3, 0), (1, 2), (2, 1)]),
         lax.ppermute(sums_own, "dp", swap),
     ]
-    hidden_grad = pl.pallas_call(
+    grad_hat, means = pl.pallas_call(
         backward_kernel,
         name="conv_backward",
-        out_shape=jax.ShapeDtypeStruct((rows, features), jnp.bfloat16),
-        in_specs=[smem] + [vmem] * 5,
-        out_specs=hbm,
-        scratch_shapes=[pltpu.VMEM((tiles, rows, LANES), jnp.float32)]
-        + [pltpu.VMEM((rows, LANES), jnp.float32)] * 2
-        + [pltpu.VMEM((rows, features), jnp.bfloat16), pltpu.SemaphoreType.DMA((tiles,))],
+        out_shape=[
+            jax.ShapeDtypeStruct((tiles, rows, LANES), jnp.float32),
+            jax.ShapeDtypeStruct((2, rows, LANES), jnp.float32),
+        ],
+        in_specs=[smem] + [vmem] * 3,
+        out_specs=[vmem] * 2,
+        scratch_shapes=[pltpu.VMEM((rows, LANES), jnp.float32)] * 2,
         compiler_params=pltpu.CompilerParams(vmem_limit_bytes=32 << 20),
         cost_estimate=pl.CostEstimate(
             flops=2 * TAPS * rows * features,
             bytes_accessed=12 * rows * features,
             transcendentals=0,
         ),
-    )(utt_lengths, cotan, normed, wide_grad, params, inv_rows)
-    pairs, hidden_grad = lax.optimization_barrier((pairs, hidden_grad))
+    )(utt_lengths, normed, wide_grad, params)
+    pairs, grad_hat = lax.optimization_barrier((pairs, grad_hat))
     across_x, diagonal, sibling = (one.astype(jnp.float32) for one in pairs)
     found = (sums_own.astype(jnp.float32) + sibling) + (across_x + diagonal)
     found = found.astype(jnp.bfloat16)
     arrived = [lax.ppermute(found, "ctx", facing(count, step)) for step in range(1, count)]
+    hidden_grad = pl.pallas_call(
+        hidden_grad_kernel,
+        name="hidden_grad",
+        out_shape=jax.ShapeDtypeStruct((rows, features), jnp.bfloat16),
+        in_specs=[vmem] * 5,
+        out_specs=hbm,
+        scratch_shapes=[
+            pltpu.VMEM((rows, features), jnp.bfloat16),
+            pltpu.SemaphoreType.DMA((tiles,)),
+        ],
+        compiler_params=pltpu.CompilerParams(vmem_limit_bytes=32 << 20),
+        cost_estimate=pl.CostEstimate(
+            flops=6 * rows * features, bytes_accessed=12 * rows * features, transcendentals=0
+        ),
+    )(cotan, normed, inv_rows, grad_hat, means)
+    arrived, hidden_grad = lax.optimization_barrier((arrived, hidden_grad))
     factor = 1.0 / math.sqrt(lax.axis_size("fsdp") * lax.axis_size("dp") * rows * count)
     grad_kernel, grad_bias, grad_gain = pl.pallas_call(
         functools.partial(finish_kernel, factor),

time: 66.5 us -> 65.5 us (0.985)
  starting transfers between devices: 27.9 us -> 24.8 us
  waiting for transfers between devices: 18.1 us -> 20.3 us
    ppermute x5 -> x3, starting transfers between devices: 8.33 us -> 4.92 us  [fast_shards(): lax.ppermute(reply, 'ctx', facing(count, step))]
    ppermute x5 -> x3, waiting for transfers between devices: 5.16 us -> 7.74 us  [fast_shards(): lax.ppermute(reply, 'ctx', facing(count, step))]
    ppermute x1, starting transfers between devices: 1.24 us -> 0.07 us  [fast_shards(): lax.ppermute(sums_own, 'dp', swap)]
    ppermute x1, starting transfers between devices: 0.61 us -> 1.47 us  [fast_shards(): lax.ppermute(sums_other, 'fsdp', swap)]
    ppermute x3, waiting for transfers between devices: 3.38 us -> 2.53 us  [fast_shards(): lax.ppermute(found, 'ctx', facing(count, step))]
    pallas_call x1 -> x3, Pallas kernels: 3.44 us -> 3.81 us  [the longest x1 2.39 us: fast_shards(): pl.pallas_call(backward_kernel, name='conv_backward', out_shape=[jax.Shap...]
  transfers between devices with their start and end apart: 19 -> 17, of which waited for: 7 -> 8; matrix products, arithmetic and copies ran while one was open for 0% -> 0% of each run, Pallas kernels for 12% -> 13%
where the time goes in v4:
time: 65.5 us; the launch traced here: 65.3 us
  starting transfers between devices  24.8 us (38%)
  waiting for transfers between devices  20.3 us (31%)
  Pallas kernels  18.6 us (28%)
  between operations  1.54 us (2%)
    ppermute x5, waiting for transfers between devices, fast_shards(): lax.ppermute(one, 'ctx', facing(count, step))  9.47 us
    ppermute x5, starting transfers between devices, fast_shards(): lax.ppermute(one, 'ctx', facing(count, step))  9.46 us
    ppermute x3, waiting for transfers between devices, fast_shards(): lax.ppermute(reply, 'ctx', facing(count, step))  7.74 us
    pallas_call x1, Pallas kernels, fast_shards(): pl.pallas_call(module_kernel, name='conv_module', out_shape=[jax.ShapeDty...  7.35 us
    ppermute x3, starting transfers between devices, fast_shards(): lax.ppermute(reply, 'ctx', facing(count, step))  4.92 us
    pallas_call x2, Pallas kernels, fast_shards(): pl.pallas_call(functools.partial(attend_kernel, chunk), name='attend', ou...  4.77 us
    ppermute x3, starting transfers between devices, fast_shards(): lax.ppermute(found, 'ctx', facing(count, step))  4.45 us
    ppermute x1, starting transfers between devices, fast_shards(): w_near = lax.ppermute(w_sent, 'fsdp', swap)  3 us
  transfers between devices with their start and end apart: 17, of which 8 were waited for; matrix products, arithmetic and copies ran while one was open for 0% of the time, Pallas kernels for 13%

profile of v4, /device:TPU:0, one launch (start us, length us, event | category | flops | bytes accessed | tf_op | source)
XLA Modules:
  0.0 65.3 jit_solution(16842350733236746864)
XLA Ops:
  0.7 1.9 %pack.1 = (bf16[672,256]{1,0:T(8,128)(2,1)S(1)}, bf16[384,128]{1,0:T(8,128)(2,1)S(1)}, bf16[384,128]{1,0:T(8,128)(2,1)S(1)}, bf16[384,128]{1,0:T(8,128)(2,1)S(1)...) custom-call(bf16[1,128,1024]{2,1,0:T(8,128)(2,1)} %query_ref.3, ...), custom_call_target="tpu_custom_call" | custom-call | tf_op jit(solution)/shard_map/pack/pallas_call | solution.py:556
  2.6 3.0 %collective-permute-start.9 = (bf16[592,768]{1,0:T(8,128)(2,1)S(1)}, bf16[592,768]{1,0:T(8,128)(2,1)S(1)}, u32[]{:S(2)}, u32[]{:S(2)}) collective-permute-start(bf16[592,768]{1,0:T(8,128)(2,1)S(1)} %get-tuple-element.66), channel_id=1, source_target_pairs={{0,2},{2,0},{1,3},{3,1},{4,6},{6,4},{5,7},{7,5},{8,10},{10,8},{9,1... | collective-permute-start | bytes 2727944 | tf_op jit(solution)/shard_map/ppermute | solution.py:591
  5.6 1.6 %collective-permute-start = (bf16[672,256]{1,0:T(8,128)(2,1)S(1)}, bf16[672,256]{1,0:T(8,128)(2,1)S(1)}, u32[]{:S(2)}, u32[]{:S(2)}) collective-permute-start(bf16[672,256]{1,0:T(8,128)(2,1)S(1)} %get-tuple-element.48), channel_id=1, source_target_pairs={{0,4},{4,0},{8,12},{12,8},{1,5},{5,1},{9,13},{13,9},{2,6},{6,2},{1... | collective-permute-start | bytes 1032200 | tf_op jit(solution)/shard_map/ppermute | solution.py:588
  7.2 2.6 %collective-permute-start.4 = (bf16[384,128]{1,0:T(8,128)(2,1)S(1)}, bf16[384,128]{1,0:T(8,128)(2,1)S(1)}, u32[]{:S(2)}, u32[]{:S(2)}) collective-permute-start(bf16[384,128]{1,0:T(8,128)(2,1)S(1)} %get-tuple-element.55), channel_id=1, source_target_pairs={{0,8},{4,12},{8,0},{12,4},{1,9},{5,13},{9,1},{13,5},{2,10},{6,14},... | collective-permute-start | bytes 294920 | tf_op jit(solution)/shard_map/ppermute | solution.py:588
  9.8 0.2 collective-permute-start.5
  10.0 0.7 %collective-permute-start.3 = (bf16[48,1536]{1,0:T(8,128)(2,1)S(1)}, bf16[48,1536]{1,0:T(8,128)(2,1)S(1)}, u32[]{:S(2)}, u32[]{:S(2)}) collective-permute-start(bf16[48,1536]{1,0:T(8,128)(2,1)S(1)} %get-tuple-element.51), channel_id=1, source_target_pairs={{4,8},{8,4},{5,9},{9,5},{6,10},{10,6},{7,11},{11,7},{20,24},{24,20... | collective-permute-start | bytes 442376 | tf_op jit(solution)/shard_map/ppermute | solution.py:590
  10.7 6.8 %collective-permute-done.4.refs_1_ = bf16[384,128]{1,0:T(8,128)(2,1)S(1)} collective-permute-done((bf16[384,128]{1,0:T(8,128)(2,1)S(1)}, bf16[384,128]{1,0:T(8,128)(2,1)S(1)}, u32[]{:S(2)}, u32[]{:S(2)}) %collective-permute-start.4) | collective-permute-done | bytes 98336 | tf_op jit(solution)/shard_map/ppermute | solution.py:588
  17.4 3.4 %collective-permute-start.1 = (bf16[384,128]{1,0:T(8,128)(2,1)S(1)}, bf16[384,128]{1,0:T(8,128)(2,1)S(1)}, u32[]{:S(2)}, u32[]{:S(2)}) collective-permute-start(bf16[384,128]{1,0:T(8,128)(2,1)S(1)} %get-tuple-element.49), channel_id=1, source_target_pairs={{0,8},{4,12},{8,0},{12,4},{1,9},{5,13},{9,1},{13,5},{2,10},{6,14},... | collective-permute-start | bytes 294920 | tf_op jit(solution)/shard_map/ppermute | solution.py:588
  20.9 0.8 %collective-permute-done.5.refs_2_ = bf16[384,128]{1,0:T(8,128)(2,1)S(1)} collective-permute-done((bf16[384,128]{1,0:T(8,128)(2,1)S(1)}, bf16[384,128]{1,0:T(8,128)(2,1)S(1)}, u32[]{:S(2)}, u32[]{:S(2)}) %collective-permute-start.5) | collective-permute-done | bytes 98336 | tf_op jit(solution)/shard_map/ppermute | solution.py:588
  21.7 1.6 %collective-permute-start.2 = (bf16[384,128]{1,0:T(8,128)(2,1)S(1)}, bf16[384,128]{1,0:T(8,128)(2,1)S(1)}, u32[]{:S(2)}, u32[]{:S(2)}) collective-permute-start(bf16[384,128]{1,0:T(8,128)(2,1)S(1)} %get-tuple-element.50), channel_id=1, source_target_pairs={{0,12},{4,8},{8,4},{12,0},{1,13},{5,9},{9,5},{13,1},{2,14},{6,10},... | collective-permute-start | bytes 294920 | tf_op jit(solution)/shard_map/ppermute | solution.py:588
  24.1 2.4 %attend.2 = (bf16[192,128]{1,0:T(8,128)(2,1)S(1)}, bf16[192,128]{1,0:T(8,128)(2,1)S(1)}, bf16[192,128]{1,0:T(8,128)(2,1)S(1)}, bf16[192,128]{1,0:T(8,128)(2,1)S(1)}) custom-call(s32[1]{0:T(128)S(6)} %copy.15.length_ref.refs_0_, bf16[1,128,1024]{2,1,0:T(8,128)(2,1)S(1)} %copy-done.2, bf16[1,128,1024]{2,1,0:T(8,128)(2,1)S(1)} %copy-done.3, ...), custom_call_target="tpu_custom_call" | custom-call | flops 1 | bytes 1 | tf_op jit(solution)/shard_map/attend/pallas_call | solution.py:600
  26.5 1.9 %collective-permute-done.1.refs_1_ = bf16[384,128]{1,0:T(8,128)(2,1)S(1)} collective-permute-done((bf16[384,128]{1,0:T(8,128)(2,1)S(1)}, bf16[384,128]{1,0:T(8,128)(2,1)S(1)}, u32[]{:S(2)}, u32[]{:S(2)}) %collective-permute-start.1) | collective-permute-done | bytes 98336 | tf_op jit(solution)/shard_map/ppermute | solution.py:588
  28.4 2.4 %attend.3 = (bf16[192,256]{1,0:T(8,128)(2,1)S(1)}, bf16[192,256]{1,0:T(8,128)(2,1)S(1)}, bf16[192,256]{1,0:T(8,128)(2,1)S(1)}, bf16[192,256]{1,0:T(8,128)(2,1)S(1)}) custom-call(s32[1]{0:T(128)S(6)} %copy.15.length_ref.refs_0_, bf16[1,128,1024]{2,1,0:T(8,128)(2,1)S(1)} %copy-done.2, bf16[1,128,1024]{2,1,0:T(8,128)(2,1)S(1)} %copy-done.3, ...), custom_call_target="tpu_custom_call" | custom-call | flops 1 | bytes 1 | tf_op jit(solution)/shard_map/attend/pallas_call | solution.py:600
  30.9 2.5 %collective-permute-start.6 = (bf16[192,256]{1,0:T(8,128)(2,1)S(1)}, bf16[192,256]{1,0:T(8,128)(2,1)S(1)}, u32[]{:S(2)}, u32[]{:S(2)}) collective-permute-start(bf16[192,256]{1,0:T(8,128)(2,1)S(1)} %get-tuple-element.61), channel_id=1, source_target_pairs={{0,4},{4,0},{8,12},{12,8},{1,5},{5,1},{9,13},{13,9},{2,6},{6,2},{1... | collective-permute-start | bytes 294920 | tf_op jit(solution)/shard_map/ppermute | solution.py:616
  33.4 1.1 %collective-permute-start.7 = (bf16[192,256]{1,0:T(8,128)(2,1)S(1)}, bf16[192,256]{1,0:T(8,128)(2,1)S(1)}, u32[]{:S(2)}, u32[]{:S(2)}) collective-permute-start(bf16[192,256]{1,0:T(8,128)(2,1)S(1)} %get-tuple-element.62), channel_id=1, source_target_pairs={{0,8},{4,12},{8,0},{12,4},{1,9},{5,13},{9,1},{13,5},{2,10},{6,14},... | collective-permute-start | bytes 294920 | tf_op jit(solution)/shard_map/ppermute | solution.py:616
  34.4 1.3 %collective-permute-start.8 = (bf16[192,256]{1,0:T(8,128)(2,1)S(1)}, bf16[192,256]{1,0:T(8,128)(2,1)S(1)}, u32[]{:S(2)}, u32[]{:S(2)}) collective-permute-start(bf16[192,256]{1,0:T(8,128)(2,1)S(1)} %get-tuple-element.63), channel_id=1, source_target_pairs={{0,12},{4,8},{8,4},{12,0},{1,13},{5,9},{9,5},{13,1},{2,14},{6,10},... | collective-permute-start | bytes 294920 | tf_op jit(solution)/shard_map/ppermute | solution.py:616
  35.8 0.5 prepare.1
  36.4 0.4 collective-permute-done.6.refs_1_
  36.7 7.4 %collective-permute-done.7.refs_2_ = bf16[192,256]{1,0:T(8,128)(2,1)S(1)} collective-permute-done((bf16[192,256]{1,0:T(8,128)(2,1)S(1)}, bf16[192,256]{1,0:T(8,128)(2,1)S(1)}, u32[]{:S(2)}, u32[]{:S(2)}) %collective-permute-start.7) | collective-permute-done | bytes 98336 | tf_op jit(solution)/shard_map/ppermute | solution.py:616
  44.1 7.3 %conv_module.1 = (bf16[128,1536]{1,0:T(8,128)(2,1)}, f32[12,200,128]{2,1,0:T(8,128)S(1)}, f32[12,168,128]{2,1,0:T(8,128)S(1)}, f32[128,128]{1,0:T(8,128)S(1)}, b...) custom-call(s32[1]{0:T(128)S(6)} %copy.15.length_ref.refs_0_, ...), custom_call_target="tpu_custom_call" | custom-call | flops 628359168 | bytes 5505024 | tf_op jit(solution)/shard_map/conv_module/pallas_call | solution.py:655
  51.5 0.1 collective-permute-start.13
  51.5 0.7 %collective-permute-start.12 = (bf16[32,768]{1,0:T(8,128)(2,1)S(1)}, bf16[32,768]{1,0:T(8,128)(2,1)S(1)}, u32[]{:S(2)}, u32[]{:S(2)}) collective-permute-start(bf16[32,768]{1,0:T(8,128)(2,1)S(1)} %get-tuple-element.73), channel_id=1, source_target_pairs={{0,3},{3,0},{1,2},{2,1},{4,7},{7,4},{5,6},{6,5},{8,11},{11,8},{9,1... | collective-permute-start | bytes 147464 | tf_op jit(solution)/shard_map/ppermute | solution.py:693
  52.2 1.5 %collective-permute-start.11 = (bf16[32,768]{1,0:T(8,128)(2,1)S(1)}, bf16[32,768]{1,0:T(8,128)(2,1)S(1)}, u32[]{:S(2)}, u32[]{:S(2)}) collective-permute-start(bf16[32,768]{1,0:T(8,128)(2,1)S(1)} %get-tuple-element.73), channel_id=1, source_target_pairs={{0,2},{2,0},{1,3},{3,1},{4,6},{6,4},{5,7},{7,5},{8,10},{10,8},{9,1... | collective-permute-start | bytes 147464 | tf_op jit(solution)/shard_map/ppermute | solution.py:692
  53.7 2.4 %conv_backward.1 = (f32[12,128,128]{2,1,0:T(8,128)S(1)}, f32[2,128,128]{2,1,0:T(8,128)S(1)}) custom-call(s32[1]{0:T(128)S(6)} %copy.15.length_ref.refs_0_, f32[12,200,128]{2,1,0:T(8,128)S(1)} %get-tuple-element.74.normed, f32[12,168,128]{2,1,0:T(8,128)S(1)} %get-tuple-element.75.wide_grad, f32[12,40,128]{2,1,0:T(8,128)S(1)} %get-tuple-element.70.refs_6_.params), custom_call_target="tpu_custom_call" | custom-call | flops 12189696 | bytes 2359296 | tf_op jit(solution)/shard_map/conv_backward/pallas_call | solution.py:696
  56.1 0.6 collective-permute-done.11
  56.7 2.2 %collective-permute-start.16 = (bf16[32,768]{1,0:T(8,128)(2,1)S(1)}, bf16[32,768]{1,0:T(8,128)(2,1)S(1)}, u32[]{:S(2)}, u32[]{:S(2)}) collective-permute-start(bf16[32,768]{1,0:T(8,128)(2,1)S(1)} %add_convert_fusion.mine), channel_id=1, source_target_pairs={{0,12},{4,8},{8,4},{12,0},{1,13},{5,9},{9,5},{13,1},{2,14},{6,10},... | collective-permute-start | bytes 147464 | tf_op jit(solution)/shard_map/ppermute | solution.py:717
  59.0 1.2 %collective-permute-start.15 = (bf16[32,768]{1,0:T(8,128)(2,1)S(1)}, bf16[32,768]{1,0:T(8,128)(2,1)S(1)}, u32[]{:S(2)}, u32[]{:S(2)}) collective-permute-start(bf16[32,768]{1,0:T(8,128)(2,1)S(1)} %add_convert_fusion.mine), channel_id=1, source_target_pairs={{0,8},{4,12},{8,0},{12,4},{1,9},{5,13},{9,1},{13,5},{2,10},{6,14},... | collective-permute-start | bytes 147464 | tf_op jit(solution)/shard_map/ppermute | solution.py:717
  60.2 1.0 %collective-permute-start.14 = (bf16[32,768]{1,0:T(8,128)(2,1)S(1)}, bf16[32,768]{1,0:T(8,128)(2,1)S(1)}, u32[]{:S(2)}, u32[]{:S(2)}) collective-permute-start(bf16[32,768]{1,0:T(8,128)(2,1)S(1)} %add_convert_fusion.mine), channel_id=1, source_target_pairs={{0,4},{4,0},{8,12},{12,8},{1,5},{5,1},{9,13},{13,9},{2,6},{6,2},{1... | collective-permute-start | bytes 147464 | tf_op jit(solution)/shard_map/ppermute | solution.py:717
  61.2 0.9 %hidden_grad.1 = bf16[128,1536]{1,0:T(8,128)(2,1)} custom-call(bf16[128,1536]{1,0:T(8,128)(2,1)S(1)} %bitcast.5, f32[12,200,128]{2,1,0:T(8,128)S(1)} %get-tuple-element.74.normed, f32[128,128]{1,0:T(8,128)S(1)} %get-tuple-element.80.inv_rows, f32[12,128,128]{2,1,0:T(8,128)S(1)} %get-tuple-element.81.grad_hat, f32[2,128,128]{2,1,0:T(8,128)S(1)} %get-tuple-element.82.means), custom_call_target="tpu_custom_call" | custom-call | flops 1179648 | bytes 2359296 | tf_op jit(solution)/shard_map/hidden_grad/pallas_call | solution.py:718
  62.1 1.1 %collective-permute-done.16.three = bf16[32,768]{1,0:T(8,128)(2,1)S(1)} collective-permute-done((bf16[32,768]{1,0:T(8,128)(2,1)S(1)}, bf16[32,768]{1,0:T(8,128)(2,1)S(1)}, u32[]{:S(2)}, u32[]{:S(2)}) %collective-permute-start.16) | collective-permute-done | bytes 49184 | tf_op jit(solution)/shard_map/ppermute | solution.py:717
  63.2 1.4 %collective-permute-done.15.two = bf16[32,768]{1,0:T(8,128)(2,1)S(1)} collective-permute-done((bf16[32,768]{1,0:T(8,128)(2,1)S(1)}, bf16[32,768]{1,0:T(8,128)(2,1)S(1)}, u32[]{:S(2)}, u32[]{:S(2)}) %collective-permute-start.15) | collective-permute-done | bytes 49184 | tf_op jit(solution)/shard_map/ppermute | solution.py:717
  64.6 0.7 %finish.1 = (f32[31,768]{1,0:T(8,128)}, f32[768]{0:T(1024)}, f32[768]{0:T(1024)}) custom-call(bf16[32,768]{1,0:T(8,128)(2,1)S(1)} %add_convert_fusion.mine, bf16[32,768]{1,0:T(8,128)(2,1)S(1)} %collective-permute-done.14.one, bf16[32,768]{1,0:T(8,128)(2,1)S(1)} %collective-permute-done.15.two, bf16[32,768]{1,0:T(8,128)(2,1)S(1)} %collective-permute-done.16.three, ...), custom_call_target="tpu_custom_call" | custom-call | tf_op jit(solution)/shard_map/finish/pallas_call | solution.py:735
  (29 shorter events, 0.2 us)
Async XLA Ops:
  0.6 23.5 %copy-start.4 = (bf16[1,128,1024]{2,1,0:T(8,128)(2,1)S(1)}, bf16[1,128,1024]{2,1,0:T(8,128)(2,1)}, u32[]{:S(2)}) copy-start(bf16[1,128,1024]{2,1,0:T(8,128)(2,1)} %value_ref.3) | copy-start | bytes 786436
  0.6 23.5 %copy-start.3 = (bf16[1,128,1024]{2,1,0:T(8,128)(2,1)S(1)}, bf16[1,128,1024]{2,1,0:T(8,128)(2,1)}, u32[]{:S(2)}) copy-start(bf16[1,128,1024]{2,1,0:T(8,128)(2,1)} %key_ref.3) | copy-start | bytes 786436
  0.7 23.5 %copy-start.2 = (bf16[1,128,1024]{2,1,0:T(8,128)(2,1)S(1)}, bf16[1,128,1024]{2,1,0:T(8,128)(2,1)}, u32[]{:S(2)}) copy-start(bf16[1,128,1024]{2,1,0:T(8,128)(2,1)} %query_ref.3) | copy-start | bytes 786436
  2.6 28.2 %collective-permute-start.9 = (bf16[592,768]{1,0:T(8,128)(2,1)S(1)}, bf16[592,768]{1,0:T(8,128)(2,1)S(1)}, u32[]{:S(2)}, u32[]{:S(2)}) collective-permute-start(bf16[592,768]{1,0:T(8,128)(2,1)S(1)} %get-tuple-element.66), channel_id=1, source_target_pairs={{0,2},{2,0},{1,3},{3,1},{4,6},{6,4},{5,7},{7,5},{8,10},{10,8},{9,1... | collective-permute-start | bytes 2727944 | tf_op jit(solution)/shard_map/ppermute | solution.py:591
  5.6 18.5 %collective-permute-start = (bf16[672,256]{1,0:T(8,128)(2,1)S(1)}, bf16[672,256]{1,0:T(8,128)(2,1)S(1)}, u32[]{:S(2)}, u32[]{:S(2)}) collective-permute-start(bf16[672,256]{1,0:T(8,128)(2,1)S(1)} %get-tuple-element.48), channel_id=1, source_target_pairs={{0,4},{4,0},{8,12},{12,8},{1,5},{5,1},{9,13},{13,9},{2,6},{6,2},{1... | collective-permute-start | bytes 1032200 | tf_op jit(solution)/shard_map/ppermute | solution.py:588
  7.2 10.2 %collective-permute-start.4 = (bf16[384,128]{1,0:T(8,128)(2,1)S(1)}, bf16[384,128]{1,0:T(8,128)(2,1)S(1)}, u32[]{:S(2)}, u32[]{:S(2)}) collective-permute-start(bf16[384,128]{1,0:T(8,128)(2,1)S(1)} %get-tuple-element.55), channel_id=1, source_target_pairs={{0,8},{4,12},{8,0},{12,4},{1,9},{5,13},{9,1},{13,5},{2,10},{6,14},... | collective-permute-start | bytes 294920 | tf_op jit(solution)/shard_map/ppermute | solution.py:588
  9.8 11.9 %collective-permute-start.5 = (bf16[384,128]{1,0:T(8,128)(2,1)S(1)}, bf16[384,128]{1,0:T(8,128)(2,1)S(1)}, u32[]{:S(2)}, u32[]{:S(2)}) collective-permute-start(bf16[384,128]{1,0:T(8,128)(2,1)S(1)} %get-tuple-element.56), channel_id=1, source_target_pairs={{0,12},{4,8},{8,4},{12,0},{1,13},{5,9},{9,5},{13,1},{2,14},{6,10},... | collective-permute-start | bytes 294920 | tf_op jit(solution)/shard_map/ppermute | solution.py:588
  10.0 18.4 %collective-permute-start.3 = (bf16[48,1536]{1,0:T(8,128)(2,1)S(1)}, bf16[48,1536]{1,0:T(8,128)(2,1)S(1)}, u32[]{:S(2)}, u32[]{:S(2)}) collective-permute-start(bf16[48,1536]{1,0:T(8,128)(2,1)S(1)} %get-tuple-element.51), channel_id=1, source_target_pairs={{4,8},{8,4},{5,9},{9,5},{6,10},{10,6},{7,11},{11,7},{20,24},{24,20... | collective-permute-start | bytes 442376 | tf_op jit(solution)/shard_map/ppermute | solution.py:590
  17.4 10.9 %collective-permute-start.1 = (bf16[384,128]{1,0:T(8,128)(2,1)S(1)}, bf16[384,128]{1,0:T(8,128)(2,1)S(1)}, u32[]{:S(2)}, u32[]{:S(2)}) collective-permute-start(bf16[384,128]{1,0:T(8,128)(2,1)S(1)} %get-tuple-element.49), channel_id=1, source_target_pairs={{0,8},{4,12},{8,0},{12,4},{1,9},{5,13},{9,1},{13,5},{2,10},{6,14},... | collective-permute-start | bytes 294920 | tf_op jit(solution)/shard_map/ppermute | solution.py:588
  21.7 6.6 %collective-permute-start.2 = (bf16[384,128]{1,0:T(8,128)(2,1)S(1)}, bf16[384,128]{1,0:T(8,128)(2,1)S(1)}, u32[]{:S(2)}, u32[]{:S(2)}) collective-permute-start(bf16[384,128]{1,0:T(8,128)(2,1)S(1)} %get-tuple-element.50), channel_id=1, source_target_pairs={{0,12},{4,8},{8,4},{12,0},{1,13},{5,9},{9,5},{13,1},{2,14},{6,10},... | collective-permute-start | bytes 294920 | tf_op jit(solution)/shard_map/ppermute | solution.py:588
  24.0 11.8 %copy-start = (bf16[1024,768]{1,0:T(8,128)(2,1)S(1)}, bf16[1024,768]{1,0:T(8,128)(2,1)}, u32[]{:S(2)}) copy-start(bf16[1024,768]{1,0:T(8,128)(2,1)} %refs_7_.3) | copy-start | bytes 4718596
  24.0 11.8 %copy-start.1 = (bf16[1,128,1536]{2,1,0:T(8,128)(2,1)S(1)}, bf16[1,128,1536]{2,1,0:T(8,128)(2,1)}, u32[]{:S(2)}) copy-start(bf16[1,128,1536]{2,1,0:T(8,128)(2,1)} %refs_4_.1) | copy-start | bytes 1179652
  24.0 11.8 %copy-start.5 = (bf16[1,128,1536]{2,1,0:T(8,128)(2,1)S(1)}, bf16[1,128,1536]{2,1,0:T(8,128)(2,1)}, u32[]{:S(2)}) copy-start(bf16[1,128,1536]{2,1,0:T(8,128)(2,1)} %refs_3_.1) | copy-start | bytes 1179652
  24.0 11.8 %copy-start.6 = (f32[31,768]{1,0:T(8,128)S(1)}, f32[31,768]{1,0:T(8,128)}, u32[]{:S(2)}) copy-start(f32[31,768]{1,0:T(8,128)} %refs_9_.1) | copy-start | bytes 285700
  24.1 11.8 %copy-start.7 = (f32[768]{0:T(1024)S(1)}, f32[768]{0:T(1024)}, u32[]{:S(2)}) copy-start(f32[768]{0:T(1024)} %refs_10_.1) | copy-start | bytes 9220
  24.1 11.8 %copy-start.8 = (f32[768]{0:T(1024)S(1)}, f32[768]{0:T(1024)}, u32[]{:S(2)}) copy-start(f32[768]{0:T(1024)} %refs_11_.1) | copy-start | bytes 9220
  30.8 5.0 %collective-permute-start.10 = (bf16[592,768]{1,0:T(8,128)(2,1)S(1)}, bf16[592,768]{1,0:T(8,128)(2,1)S(1)}, u32[]{:S(2)}, u32[]{:S(2)}) collective-permute-start(bf16[592,768]{1,0:T(8,128)(2,1)S(1)} %collective-permute-done.9.refs_7_.refs_8_), channel_id=1, source_target_pairs={{0,1},{1,0},{2,3},{3,2},{4,5},{5,4},{6,7},{7,6},{8,9},{9,8},{10,11... | collective-permute-start | bytes 2727944 | tf_op jit(solution)/shard_map/ppermute | solution.py:620
  30.9 5.9 %collective-permute-start.6 = (bf16[192,256]{1,0:T(8,128)(2,1)S(1)}, bf16[192,256]{1,0:T(8,128)(2,1)S(1)}, u32[]{:S(2)}, u32[]{:S(2)}) collective-permute-start(bf16[192,256]{1,0:T(8,128)(2,1)S(1)} %get-tuple-element.61), channel_id=1, source_target_pairs={{0,4},{4,0},{8,12},{12,8},{1,5},{5,1},{9,13},{13,9},{2,6},{6,2},{1... | collective-permute-start | bytes 294920 | tf_op jit(solution)/shard_map/ppermute | solution.py:616
  33.4 10.8 %collective-permute-start.7 = (bf16[192,256]{1,0:T(8,128)(2,1)S(1)}, bf16[192,256]{1,0:T(8,128)(2,1)S(1)}, u32[]{:S(2)}, u32[]{:S(2)}) collective-permute-start(bf16[192,256]{1,0:T(8,128)(2,1)S(1)} %get-tuple-element.62), channel_id=1, source_target_pairs={{0,8},{4,12},{8,0},{12,4},{1,9},{5,13},{9,1},{13,5},{2,10},{6,14},... | collective-permute-start | bytes 294920 | tf_op jit(solution)/shard_map/ppermute | solution.py:616
  34.4 9.7 %collective-permute-start.8 = (bf16[192,256]{1,0:T(8,128)(2,1)S(1)}, bf16[192,256]{1,0:T(8,128)(2,1)S(1)}, u32[]{:S(2)}, u32[]{:S(2)}) collective-permute-start(bf16[192,256]{1,0:T(8,128)(2,1)S(1)} %get-tuple-element.63), channel_id=1, source_target_pairs={{0,12},{4,8},{8,4},{12,0},{1,13},{5,9},{9,5},{13,1},{2,14},{6,10},... | collective-permute-start | bytes 294920 | tf_op jit(solution)/shard_map/ppermute | solution.py:616
  51.5 4.6 %collective-permute-start.13 = (bf16[32,768]{1,0:T(8,128)(2,1)S(1)}, bf16[32,768]{1,0:T(8,128)(2,1)S(1)}, u32[]{:S(2)}, u32[]{:S(2)}) collective-permute-start(bf16[32,768]{1,0:T(8,128)(2,1)S(1)} %get-tuple-element.72), channel_id=1, source_target_pairs={{0,1},{1,0},{2,3},{3,2},{4,5},{5,4},{6,7},{7,6},{8,9},{9,8},{10,11... | collective-permute-start | bytes 147464 | tf_op jit(solution)/shard_map/ppermute | solution.py:694
  51.5 4.6 %collective-permute-start.12 = (bf16[32,768]{1,0:T(8,128)(2,1)S(1)}, bf16[32,768]{1,0:T(8,128)(2,1)S(1)}, u32[]{:S(2)}, u32[]{:S(2)}) collective-permute-start(bf16[32,768]{1,0:T(8,128)(2,1)S(1)} %get-tuple-element.73), channel_id=1, source_target_pairs={{0,3},{3,0},{1,2},{2,1},{4,7},{7,4},{5,6},{6,5},{8,11},{11,8},{9,1... | collective-permute-start | bytes 147464 | tf_op jit(solution)/shard_map/ppermute | solution.py:693
  52.2 4.5 %collective-permute-start.11 = (bf16[32,768]{1,0:T(8,128)(2,1)S(1)}, bf16[32,768]{1,0:T(8,128)(2,1)S(1)}, u32[]{:S(2)}, u32[]{:S(2)}) collective-permute-start(bf16[32,768]{1,0:T(8,128)(2,1)S(1)} %get-tuple-element.73), channel_id=1, source_target_pairs={{0,2},{2,0},{1,3},{3,1},{4,6},{6,4},{5,7},{7,5},{8,10},{10,8},{9,1... | collective-permute-start | bytes 147464 | tf_op jit(solution)/shard_map/ppermute | solution.py:692
  56.7 6.5 %collective-permute-start.16 = (bf16[32,768]{1,0:T(8,128)(2,1)S(1)}, bf16[32,768]{1,0:T(8,128)(2,1)S(1)}, u32[]{:S(2)}, u32[]{:S(2)}) collective-permute-start(bf16[32,768]{1,0:T(8,128)(2,1)S(1)} %add_convert_fusion.mine), channel_id=1, source_target_pairs={{0,12},{4,8},{8,4},{12,0},{1,13},{5,9},{9,5},{13,1},{2,14},{6,10},... | collective-permute-start | bytes 147464 | tf_op jit(solution)/shard_map/ppermute | solution.py:717
  59.0 5.7 %collective-permute-start.15 = (bf16[32,768]{1,0:T(8,128)(2,1)S(1)}, bf16[32,768]{1,0:T(8,128)(2,1)S(1)}, u32[]{:S(2)}, u32[]{:S(2)}) collective-permute-start(bf16[32,768]{1,0:T(8,128)(2,1)S(1)} %add_convert_fusion.mine), channel_id=1, source_target_pairs={{0,8},{4,12},{8,0},{12,4},{1,9},{5,13},{9,1},{13,5},{2,10},{6,14},... | collective-permute-start | bytes 147464 | tf_op jit(solution)/shard_map/ppermute | solution.py:717
  60.2 4.5 %collective-permute-start.14 = (bf16[32,768]{1,0:T(8,128)(2,1)S(1)}, bf16[32,768]{1,0:T(8,128)(2,1)S(1)}, u32[]{:S(2)}, u32[]{:S(2)}) collective-permute-start(bf16[32,768]{1,0:T(8,128)(2,1)S(1)} %add_convert_fusion.mine), channel_id=1, source_target_pairs={{0,4},{4,0},{8,12},{12,8},{1,5},{5,1},{9,13},{13,9},{2,6},{6,2},{1... | collective-permute-start | bytes 147464 | tf_op jit(solution)/shard_map/ppermute | solution.py:717

commit v5 on v4

--- a/solution.py
+++ b/solution.py
@@ -462,7 +462,7 @@
         sums[tile] = jnp.sum(partial[...], axis=1)
         return carry
 
-    lax.fori_loop(0, tiles, one_tile, 0)
+    lax.fori_loop(0, tiles, one_tile, 0, unroll=2)
     for tile in range(half_tiles):
         cols = slice(tile * LANES, (tile + 1) * LANES)
         sums_own[:, cols] = sums[side * half_tiles + tile].astype(sums_own.dtype)
@@ -492,7 +492,7 @@
         mean_two[...] += grad * normed[tile, WIDE : WIDE + rows]
         return carry
 
-    lax.fori_loop(0, tiles, one_tile, 0)
+    lax.fori_loop(0, tiles, one_tile, 0, unroll=2)
     for index, total in enumerate((mean_one, mean_two)):
         mean = jnp.sum(total[...], axis=1, keepdims=True) * (1.0 / (tiles * LANES))
         means[index] = jnp.broadcast_to(mean, (rows, LANES))

time: 65.5 us -> 64.9 us (level)
  Pallas kernels: 18.6 us -> 17.6 us
where the time goes in v5:
time: 64.9 us; the launch traced here: 64.7 us
  starting transfers between devices  24.8 us (38%)
  waiting for transfers between devices  20.8 us (32%)
  Pallas kernels  17.6 us (27%)
  between operations  1.54 us (2%)
    ppermute x5, waiting for transfers between devices, fast_shards(): lax.ppermute(one, 'ctx', facing(count, step))  9.47 us
    ppermute x5, starting transfers between devices, fast_shards(): lax.ppermute(one, 'ctx', facing(count, step))  9.46 us
    ppermute x3, waiting for transfers between devices, fast_shards(): lax.ppermute(reply, 'ctx', facing(count, step))  7.74 us
    pallas_call x1, Pallas kernels, fast_shards(): pl.pallas_call(module_kernel, name='conv_module', out_shape=[jax.ShapeDty...  6.75 us
    ppermute x3, starting transfers between devices, fast_shards(): lax.ppermute(reply, 'ctx', facing(count, step))  4.92 us
    pallas_call x2, Pallas kernels, fast_shards(): pl.pallas_call(functools.partial(attend_kernel, chunk), name='attend', ou...  4.77 us
    ppermute x3, starting transfers between devices, fast_shards(): lax.ppermute(found, 'ctx', facing(count, step))  4.45 us
    ppermute x1, starting transfers between devices, fast_shards(): w_near = lax.ppermute(w_sent, 'fsdp', swap)  3 us
  transfers between devices with their start and end apart: 17, of which 8 were waited for; matrix products, arithmetic and copies ran while one was open for 0% of the time, Pallas kernels for 13%

profile of v5, /device:TPU:0, one launch (start us, length us, event | category | flops | bytes accessed | tf_op | source)
XLA Modules:
  0.0 64.7 jit_solution(5430490902119664714)
XLA Ops:
  0.7 1.9 %pack.1 = (bf16[672,256]{1,0:T(8,128)(2,1)S(1)}, bf16[384,128]{1,0:T(8,128)(2,1)S(1)}, bf16[384,128]{1,0:T(8,128)(2,1)S(1)}, bf16[384,128]{1,0:T(8,128)(2,1)S(1)...) custom-call(bf16[1,128,1024]{2,1,0:T(8,128)(2,1)} %query_ref.3, ...), custom_call_target="tpu_custom_call" | custom-call | tf_op jit(solution)/shard_map/pack/pallas_call | solution.py:556
  2.6 3.0 %collective-permute-start.9 = (bf16[592,768]{1,0:T(8,128)(2,1)S(1)}, bf16[592,768]{1,0:T(8,128)(2,1)S(1)}, u32[]{:S(2)}, u32[]{:S(2)}) collective-permute-start(bf16[592,768]{1,0:T(8,128)(2,1)S(1)} %get-tuple-element.66), channel_id=1, source_target_pairs={{0,2},{2,0},{1,3},{3,1},{4,6},{6,4},{5,7},{7,5},{8,10},{10,8},{9,1... | collective-permute-start | bytes 2727944 | tf_op jit(solution)/shard_map/ppermute | solution.py:591
  5.6 1.6 %collective-permute-start = (bf16[672,256]{1,0:T(8,128)(2,1)S(1)}, bf16[672,256]{1,0:T(8,128)(2,1)S(1)}, u32[]{:S(2)}, u32[]{:S(2)}) collective-permute-start(bf16[672,256]{1,0:T(8,128)(2,1)S(1)} %get-tuple-element.48), channel_id=1, source_target_pairs={{0,4},{4,0},{8,12},{12,8},{1,5},{5,1},{9,13},{13,9},{2,6},{6,2},{1... | collective-permute-start | bytes 1032200 | tf_op jit(solution)/shard_map/ppermute | solution.py:588
  7.2 2.6 %collective-permute-start.4 = (bf16[384,128]{1,0:T(8,128)(2,1)S(1)}, bf16[384,128]{1,0:T(8,128)(2,1)S(1)}, u32[]{:S(2)}, u32[]{:S(2)}) collective-permute-start(bf16[384,128]{1,0:T(8,128)(2,1)S(1)} %get-tuple-element.55), channel_id=1, source_target_pairs={{0,8},{4,12},{8,0},{12,4},{1,9},{5,13},{9,1},{13,5},{2,10},{6,14},... | collective-permute-start | bytes 294920 | tf_op jit(solution)/shard_map/ppermute | solution.py:588
  9.8 0.2 collective-permute-start.5
  10.0 0.7 %collective-permute-start.3 = (bf16[48,1536]{1,0:T(8,128)(2,1)S(1)}, bf16[48,1536]{1,0:T(8,128)(2,1)S(1)}, u32[]{:S(2)}, u32[]{:S(2)}) collective-permute-start(bf16[48,1536]{1,0:T(8,128)(2,1)S(1)} %get-tuple-element.51), channel_id=1, source_target_pairs={{4,8},{8,4},{5,9},{9,5},{6,10},{10,6},{7,11},{11,7},{20,24},{24,20... | collective-permute-start | bytes 442376 | tf_op jit(solution)/shard_map/ppermute | solution.py:590
  10.7 6.8 %collective-permute-done.4.refs_1_ = bf16[384,128]{1,0:T(8,128)(2,1)S(1)} collective-permute-done((bf16[384,128]{1,0:T(8,128)(2,1)S(1)}, bf16[384,128]{1,0:T(8,128)(2,1)S(1)}, u32[]{:S(2)}, u32[]{:S(2)}) %collective-permute-start.4) | collective-permute-done | bytes 98336 | tf_op jit(solution)/shard_map/ppermute | solution.py:588
  17.4 3.4 %collective-permute-start.1 = (bf16[384,128]{1,0:T(8,128)(2,1)S(1)}, bf16[384,128]{1,0:T(8,128)(2,1)S(1)}, u32[]{:S(2)}, u32[]{:S(2)}) collective-permute-start(bf16[384,128]{1,0:T(8,128)(2,1)S(1)} %get-tuple-element.49), channel_id=1, source_target_pairs={{0,8},{4,12},{8,0},{12,4},{1,9},{5,13},{9,1},{13,5},{2,10},{6,14},... | collective-permute-start | bytes 294920 | tf_op jit(solution)/shard_map/ppermute | solution.py:588
  20.9 0.8 %collective-permute-done.5.refs_2_ = bf16[384,128]{1,0:T(8,128)(2,1)S(1)} collective-permute-done((bf16[384,128]{1,0:T(8,128)(2,1)S(1)}, bf16[384,128]{1,0:T(8,128)(2,1)S(1)}, u32[]{:S(2)}, u32[]{:S(2)}) %collective-permute-start.5) | collective-permute-done | bytes 98336 | tf_op jit(solution)/shard_map/ppermute | solution.py:588
  21.7 1.6 %collective-permute-start.2 = (bf16[384,128]{1,0:T(8,128)(2,1)S(1)}, bf16[384,128]{1,0:T(8,128)(2,1)S(1)}, u32[]{:S(2)}, u32[]{:S(2)}) collective-permute-start(bf16[384,128]{1,0:T(8,128)(2,1)S(1)} %get-tuple-element.50), channel_id=1, source_target_pairs={{0,12},{4,8},{8,4},{12,0},{1,13},{5,9},{9,5},{13,1},{2,14},{6,10},... | collective-permute-start | bytes 294920 | tf_op jit(solution)/shard_map/ppermute | solution.py:588
  24.1 2.4 %attend.2 = (bf16[192,128]{1,0:T(8,128)(2,1)S(1)}, bf16[192,128]{1,0:T(8,128)(2,1)S(1)}, bf16[192,128]{1,0:T(8,128)(2,1)S(1)}, bf16[192,128]{1,0:T(8,128)(2,1)S(1)}) custom-call(s32[1]{0:T(128)S(6)} %copy.15.length_ref.refs_0_, bf16[1,128,1024]{2,1,0:T(8,128)(2,1)S(1)} %copy-done.2, bf16[1,128,1024]{2,1,0:T(8,128)(2,1)S(1)} %copy-done.3, ...), custom_call_target="tpu_custom_call" | custom-call | flops 1 | bytes 1 | tf_op jit(solution)/shard_map/attend/pallas_call | solution.py:600
  26.5 1.9 %collective-permute-done.1.refs_1_ = bf16[384,128]{1,0:T(8,128)(2,1)S(1)} collective-permute-done((bf16[384,128]{1,0:T(8,128)(2,1)S(1)}, bf16[384,128]{1,0:T(8,128)(2,1)S(1)}, u32[]{:S(2)}, u32[]{:S(2)}) %collective-permute-start.1) | collective-permute-done | bytes 98336 | tf_op jit(solution)/shard_map/ppermute | solution.py:588
  28.4 2.4 %attend.3 = (bf16[192,256]{1,0:T(8,128)(2,1)S(1)}, bf16[192,256]{1,0:T(8,128)(2,1)S(1)}, bf16[192,256]{1,0:T(8,128)(2,1)S(1)}, bf16[192,256]{1,0:T(8,128)(2,1)S(1)}) custom-call(s32[1]{0:T(128)S(6)} %copy.15.length_ref.refs_0_, bf16[1,128,1024]{2,1,0:T(8,128)(2,1)S(1)} %copy-done.2, bf16[1,128,1024]{2,1,0:T(8,128)(2,1)S(1)} %copy-done.3, ...), custom_call_target="tpu_custom_call" | custom-call | flops 1 | bytes 1 | tf_op jit(solution)/shard_map/attend/pallas_call | solution.py:600
  30.8 0.1 collective-permute-start.10
  30.9 2.5 %collective-permute-start.6 = (bf16[192,256]{1,0:T(8,128)(2,1)S(1)}, bf16[192,256]{1,0:T(8,128)(2,1)S(1)}, u32[]{:S(2)}, u32[]{:S(2)}) collective-permute-start(bf16[192,256]{1,0:T(8,128)(2,1)S(1)} %get-tuple-element.61), channel_id=1, source_target_pairs={{0,4},{4,0},{8,12},{12,8},{1,5},{5,1},{9,13},{13,9},{2,6},{6,2},{1... | collective-permute-start | bytes 294920 | tf_op jit(solution)/shard_map/ppermute | solution.py:616
  33.4 1.1 %collective-permute-start.7 = (bf16[192,256]{1,0:T(8,128)(2,1)S(1)}, bf16[192,256]{1,0:T(8,128)(2,1)S(1)}, u32[]{:S(2)}, u32[]{:S(2)}) collective-permute-start(bf16[192,256]{1,0:T(8,128)(2,1)S(1)} %get-tuple-element.62), channel_id=1, source_target_pairs={{0,8},{4,12},{8,0},{12,4},{1,9},{5,13},{9,1},{13,5},{2,10},{6,14},... | collective-permute-start | bytes 294920 | tf_op jit(solution)/shard_map/ppermute | solution.py:616
  34.4 1.3 %collective-permute-start.8 = (bf16[192,256]{1,0:T(8,128)(2,1)S(1)}, bf16[192,256]{1,0:T(8,128)(2,1)S(1)}, u32[]{:S(2)}, u32[]{:S(2)}) collective-permute-start(bf16[192,256]{1,0:T(8,128)(2,1)S(1)} %get-tuple-element.63), channel_id=1, source_target_pairs={{0,12},{4,8},{8,4},{12,0},{1,13},{5,9},{9,5},{13,1},{2,14},{6,10},... | collective-permute-start | bytes 294920 | tf_op jit(solution)/shard_map/ppermute | solution.py:616
  35.8 0.5 prepare.1
  36.4 0.4 collective-permute-done.6.refs_1_
  36.7 7.4 %collective-permute-done.7.refs_2_ = bf16[192,256]{1,0:T(8,128)(2,1)S(1)} collective-permute-done((bf16[192,256]{1,0:T(8,128)(2,1)S(1)}, bf16[192,256]{1,0:T(8,128)(2,1)S(1)}, u32[]{:S(2)}, u32[]{:S(2)}) %collective-permute-start.7) | collective-permute-done | bytes 98336 | tf_op jit(solution)/shard_map/ppermute | solution.py:616
  44.1 6.8 %conv_module.1 = (bf16[128,1536]{1,0:T(8,128)(2,1)}, f32[12,200,128]{2,1,0:T(8,128)S(1)}, f32[12,168,128]{2,1,0:T(8,128)S(1)}, f32[128,128]{1,0:T(8,128)S(1)}, b...) custom-call(s32[1]{0:T(128)S(6)} %copy.15.length_ref.refs_0_, ...), custom_call_target="tpu_custom_call" | custom-call | flops 628359168 | bytes 5505024 | tf_op jit(solution)/shard_map/conv_module/pallas_call | solution.py:655
  51.0 0.7 %collective-permute-start.12 = (bf16[32,768]{1,0:T(8,128)(2,1)S(1)}, bf16[32,768]{1,0:T(8,128)(2,1)S(1)}, u32[]{:S(2)}, u32[]{:S(2)}) collective-permute-start(bf16[32,768]{1,0:T(8,128)(2,1)S(1)} %get-tuple-element.73), channel_id=1, source_target_pairs={{0,3},{3,0},{1,2},{2,1},{4,7},{7,4},{5,6},{6,5},{8,11},{11,8},{9,1... | collective-permute-start | bytes 147464 | tf_op jit(solution)/shard_map/ppermute | solution.py:693
  51.6 1.5 %collective-permute-start.11 = (bf16[32,768]{1,0:T(8,128)(2,1)S(1)}, bf16[32,768]{1,0:T(8,128)(2,1)S(1)}, u32[]{:S(2)}, u32[]{:S(2)}) collective-permute-start(bf16[32,768]{1,0:T(8,128)(2,1)S(1)} %get-tuple-element.73), channel_id=1, source_target_pairs={{0,2},{2,0},{1,3},{3,1},{4,6},{6,4},{5,7},{7,5},{8,10},{10,8},{9,1... | collective-permute-start | bytes 147464 | tf_op jit(solution)/shard_map/ppermute | solution.py:692
  53.1 2.0 %conv_backward.1 = (f32[12,128,128]{2,1,0:T(8,128)S(1)}, f32[2,128,128]{2,1,0:T(8,128)S(1)}) custom-call(s32[1]{0:T(128)S(6)} %copy.15.length_ref.refs_0_, f32[12,200,128]{2,1,0:T(8,128)S(1)} %get-tuple-element.74.normed, f32[12,168,128]{2,1,0:T(8,128)S(1)} %get-tuple-element.75.wide_grad, f32[12,40,128]{2,1,0:T(8,128)S(1)} %get-tuple-element.70.refs_6_.params), custom_call_target="tpu_custom_call" | custom-call | flops 12189696 | bytes 2359296 | tf_op jit(solution)/shard_map/conv_backward/pallas_call | solution.py:696
  55.1 1.0 %collective-permute-done.11 = bf16[32,768]{1,0:T(8,128)(2,1)S(1)} collective-permute-done((bf16[32,768]{1,0:T(8,128)(2,1)S(1)}, bf16[32,768]{1,0:T(8,128)(2,1)S(1)}, u32[]{:S(2)}, u32[]{:S(2)}) %collective-permute-start.11) | collective-permute-done | bytes 49184 | tf_op jit(solution)/shard_map/ppermute | solution.py:692
  56.1 2.2 %collective-permute-start.16 = (bf16[32,768]{1,0:T(8,128)(2,1)S(1)}, bf16[32,768]{1,0:T(8,128)(2,1)S(1)}, u32[]{:S(2)}, u32[]{:S(2)}) collective-permute-start(bf16[32,768]{1,0:T(8,128)(2,1)S(1)} %add_convert_fusion.mine), channel_id=1, source_target_pairs={{0,12},{4,8},{8,4},{12,0},{1,13},{5,9},{9,5},{13,1},{2,14},{6,10},... | collective-permute-start | bytes 147464 | tf_op jit(solution)/shard_map/ppermute | solution.py:717
  58.4 1.2 %collective-permute-start.15 = (bf16[32,768]{1,0:T(8,128)(2,1)S(1)}, bf16[32,768]{1,0:T(8,128)(2,1)S(1)}, u32[]{:S(2)}, u32[]{:S(2)}) collective-permute-start(bf16[32,768]{1,0:T(8,128)(2,1)S(1)} %add_convert_fusion.mine), channel_id=1, source_target_pairs={{0,8},{4,12},{8,0},{12,4},{1,9},{5,13},{9,1},{13,5},{2,10},{6,14},... | collective-permute-start | bytes 147464 | tf_op jit(solution)/shard_map/ppermute | solution.py:717
  59.6 1.0 %collective-permute-start.14 = (bf16[32,768]{1,0:T(8,128)(2,1)S(1)}, bf16[32,768]{1,0:T(8,128)(2,1)S(1)}, u32[]{:S(2)}, u32[]{:S(2)}) collective-permute-start(bf16[32,768]{1,0:T(8,128)(2,1)S(1)} %add_convert_fusion.mine), channel_id=1, source_target_pairs={{0,4},{4,0},{8,12},{12,8},{1,5},{5,1},{9,13},{13,9},{2,6},{6,2},{1... | collective-permute-start | bytes 147464 | tf_op jit(solution)/shard_map/ppermute | solution.py:717
  60.6 0.9 %hidden_grad.1 = bf16[128,1536]{1,0:T(8,128)(2,1)} custom-call(bf16[128,1536]{1,0:T(8,128)(2,1)S(1)} %bitcast.5, f32[12,200,128]{2,1,0:T(8,128)S(1)} %get-tuple-element.74.normed, f32[128,128]{1,0:T(8,128)S(1)} %get-tuple-element.80.inv_rows, f32[12,128,128]{2,1,0:T(8,128)S(1)} %get-tuple-element.81.grad_hat, f32[2,128,128]{2,1,0:T(8,128)S(1)} %get-tuple-element.82.means), custom_call_target="tpu_custom_call" | custom-call | flops 1179648 | bytes 2359296 | tf_op jit(solution)/shard_map/hidden_grad/pallas_call | solution.py:718
  61.5 1.1 %collective-permute-done.16.three = bf16[32,768]{1,0:T(8,128)(2,1)S(1)} collective-permute-done((bf16[32,768]{1,0:T(8,128)(2,1)S(1)}, bf16[32,768]{1,0:T(8,128)(2,1)S(1)}, u32[]{:S(2)}, u32[]{:S(2)}) %collective-permute-start.16) | collective-permute-done | bytes 49184 | tf_op jit(solution)/shard_map/ppermute | solution.py:717
  62.6 1.4 %collective-permute-done.15.two = bf16[32,768]{1,0:T(8,128)(2,1)S(1)} collective-permute-done((bf16[32,768]{1,0:T(8,128)(2,1)S(1)}, bf16[32,768]{1,0:T(8,128)(2,1)S(1)}, u32[]{:S(2)}, u32[]{:S(2)}) %collective-permute-start.15) | collective-permute-done | bytes 49184 | tf_op jit(solution)/shard_map/ppermute | solution.py:717
  64.0 0.7 %finish.1 = (f32[31,768]{1,0:T(8,128)}, f32[768]{0:T(1024)}, f32[768]{0:T(1024)}) custom-call(bf16[32,768]{1,0:T(8,128)(2,1)S(1)} %add_convert_fusion.mine, bf16[32,768]{1,0:T(8,128)(2,1)S(1)} %collective-permute-done.14.one, bf16[32,768]{1,0:T(8,128)(2,1)S(1)} %collective-permute-done.15.two, bf16[32,768]{1,0:T(8,128)(2,1)S(1)} %collective-permute-done.16.three, ...), custom_call_target="tpu_custom_call" | custom-call | tf_op jit(solution)/shard_map/finish/pallas_call | solution.py:735
  (29 shorter events, 0.2 us)
Async XLA Ops:
  0.6 23.5 %copy-start.4 = (bf16[1,128,1024]{2,1,0:T(8,128)(2,1)S(1)}, bf16[1,128,1024]{2,1,0:T(8,128)(2,1)}, u32[]{:S(2)}) copy-start(bf16[1,128,1024]{2,1,0:T(8,128)(2,1)} %value_ref.3) | copy-start | bytes 786436
  0.6 23.5 %copy-start.3 = (bf16[1,128,1024]{2,1,0:T(8,128)(2,1)S(1)}, bf16[1,128,1024]{2,1,0:T(8,128)(2,1)}, u32[]{:S(2)}) copy-start(bf16[1,128,1024]{2,1,0:T(8,128)(2,1)} %key_ref.3) | copy-start | bytes 786436
  0.7 23.5 %copy-start.2 = (bf16[1,128,1024]{2,1,0:T(8,128)(2,1)S(1)}, bf16[1,128,1024]{2,1,0:T(8,128)(2,1)}, u32[]{:S(2)}) copy-start(bf16[1,128,1024]{2,1,0:T(8,128)(2,1)} %query_ref.3) | copy-start | bytes 786436
  2.6 28.2 %collective-permute-start.9 = (bf16[592,768]{1,0:T(8,128)(2,1)S(1)}, bf16[592,768]{1,0:T(8,128)(2,1)S(1)}, u32[]{:S(2)}, u32[]{:S(2)}) collective-permute-start(bf16[592,768]{1,0:T(8,128)(2,1)S(1)} %get-tuple-element.66), channel_id=1, source_target_pairs={{0,2},{2,0},{1,3},{3,1},{4,6},{6,4},{5,7},{7,5},{8,10},{10,8},{9,1... | collective-permute-start | bytes 2727944 | tf_op jit(solution)/shard_map/ppermute | solution.py:591
  5.6 18.5 %collective-permute-start = (bf16[672,256]{1,0:T(8,128)(2,1)S(1)}, bf16[672,256]{1,0:T(8,128)(2,1)S(1)}, u32[]{:S(2)}, u32[]{:S(2)}) collective-permute-start(bf16[672,256]{1,0:T(8,128)(2,1)S(1)} %get-tuple-element.48), channel_id=1, source_target_pairs={{0,4},{4,0},{8,12},{12,8},{1,5},{5,1},{9,13},{13,9},{2,6},{6,2},{1... | collective-permute-start | bytes 1032200 | tf_op jit(solution)/shard_map/ppermute | solution.py:588
  7.2 10.2 %collective-permute-start.4 = (bf16[384,128]{1,0:T(8,128)(2,1)S(1)}, bf16[384,128]{1,0:T(8,128)(2,1)S(1)}, u32[]{:S(2)}, u32[]{:S(2)}) collective-permute-start(bf16[384,128]{1,0:T(8,128)(2,1)S(1)} %get-tuple-element.55), channel_id=1, source_target_pairs={{0,8},{4,12},{8,0},{12,4},{1,9},{5,13},{9,1},{13,5},{2,10},{6,14},... | collective-permute-start | bytes 294920 | tf_op jit(solution)/shard_map/ppermute | solution.py:588
  9.8 11.9 %collective-permute-start.5 = (bf16[384,128]{1,0:T(8,128)(2,1)S(1)}, bf16[384,128]{1,0:T(8,128)(2,1)S(1)}, u32[]{:S(2)}, u32[]{:S(2)}) collective-permute-start(bf16[384,128]{1,0:T(8,128)(2,1)S(1)} %get-tuple-element.56), channel_id=1, source_target_pairs={{0,12},{4,8},{8,4},{12,0},{1,13},{5,9},{9,5},{13,1},{2,14},{6,10},... | collective-permute-start | bytes 294920 | tf_op jit(solution)/shard_map/ppermute | solution.py:588
  10.0 18.4 %collective-permute-start.3 = (bf16[48,1536]{1,0:T(8,128)(2,1)S(1)}, bf16[48,1536]{1,0:T(8,128)(2,1)S(1)}, u32[]{:S(2)}, u32[]{:S(2)}) collective-permute-start(bf16[48,1536]{1,0:T(8,128)(2,1)S(1)} %get-tuple-element.51), channel_id=1, source_target_pairs={{4,8},{8,4},{5,9},{9,5},{6,10},{10,6},{7,11},{11,7},{20,24},{24,20... | collective-permute-start | bytes 442376 | tf_op jit(solution)/shard_map/ppermute | solution.py:590
  17.4 10.9 %collective-permute-start.1 = (bf16[384,128]{1,0:T(8,128)(2,1)S(1)}, bf16[384,128]{1,0:T(8,128)(2,1)S(1)}, u32[]{:S(2)}, u32[]{:S(2)}) collective-permute-start(bf16[384,128]{1,0:T(8,128)(2,1)S(1)} %get-tuple-element.49), channel_id=1, source_target_pairs={{0,8},{4,12},{8,0},{12,4},{1,9},{5,13},{9,1},{13,5},{2,10},{6,14},... | collective-permute-start | bytes 294920 | tf_op jit(solution)/shard_map/ppermute | solution.py:588
  21.7 6.6 %collective-permute-start.2 = (bf16[384,128]{1,0:T(8,128)(2,1)S(1)}, bf16[384,128]{1,0:T(8,128)(2,1)S(1)}, u32[]{:S(2)}, u32[]{:S(2)}) collective-permute-start(bf16[384,128]{1,0:T(8,128)(2,1)S(1)} %get-tuple-element.50), channel_id=1, source_target_pairs={{0,12},{4,8},{8,4},{12,0},{1,13},{5,9},{9,5},{13,1},{2,14},{6,10},... | collective-permute-start | bytes 294920 | tf_op jit(solution)/shard_map/ppermute | solution.py:588
  24.0 11.8 %copy-start = (bf16[1024,768]{1,0:T(8,128)(2,1)S(1)}, bf16[1024,768]{1,0:T(8,128)(2,1)}, u32[]{:S(2)}) copy-start(bf16[1024,768]{1,0:T(8,128)(2,1)} %refs_7_.3) | copy-start | bytes 4718596
  24.0 11.8 %copy-start.1 = (bf16[1,128,1536]{2,1,0:T(8,128)(2,1)S(1)}, bf16[1,128,1536]{2,1,0:T(8,128)(2,1)}, u32[]{:S(2)}) copy-start(bf16[1,128,1536]{2,1,0:T(8,128)(2,1)} %refs_4_.1) | copy-start | bytes 1179652
  24.0 11.8 %copy-start.5 = (bf16[1,128,1536]{2,1,0:T(8,128)(2,1)S(1)}, bf16[1,128,1536]{2,1,0:T(8,128)(2,1)}, u32[]{:S(2)}) copy-start(bf16[1,128,1536]{2,1,0:T(8,128)(2,1)} %refs_3_.1) | copy-start | bytes 1179652
  24.0 11.8 %copy-start.6 = (f32[31,768]{1,0:T(8,128)S(1)}, f32[31,768]{1,0:T(8,128)}, u32[]{:S(2)}) copy-start(f32[31,768]{1,0:T(8,128)} %refs_9_.1) | copy-start | bytes 285700
  24.1 11.8 %copy-start.7 = (f32[768]{0:T(1024)S(1)}, f32[768]{0:T(1024)}, u32[]{:S(2)}) copy-start(f32[768]{0:T(1024)} %refs_10_.1) | copy-start | bytes 9220
  24.1 11.8 %copy-start.8 = (f32[768]{0:T(1024)S(1)}, f32[768]{0:T(1024)}, u32[]{:S(2)}) copy-start(f32[768]{0:T(1024)} %refs_11_.1) | copy-start | bytes 9220
  30.8 5.0 %collective-permute-start.10 = (bf16[592,768]{1,0:T(8,128)(2,1)S(1)}, bf16[592,768]{1,0:T(8,128)(2,1)S(1)}, u32[]{:S(2)}, u32[]{:S(2)}) collective-permute-start(bf16[592,768]{1,0:T(8,128)(2,1)S(1)} %collective-permute-done.9.refs_7_.refs_8_), channel_id=1, source_target_pairs={{0,1},{1,0},{2,3},{3,2},{4,5},{5,4},{6,7},{7,6},{8,9},{9,8},{10,11... | collective-permute-start | bytes 2727944 | tf_op jit(solution)/shard_map/ppermute | solution.py:620
  30.9 5.9 %collective-permute-start.6 = (bf16[192,256]{1,0:T(8,128)(2,1)S(1)}, bf16[192,256]{1,0:T(8,128)(2,1)S(1)}, u32[]{:S(2)}, u32[]{:S(2)}) collective-permute-start(bf16[192,256]{1,0:T(8,128)(2,1)S(1)} %get-tuple-element.61), channel_id=1, source_target_pairs={{0,4},{4,0},{8,12},{12,8},{1,5},{5,1},{9,13},{13,9},{2,6},{6,2},{1... | collective-permute-start | bytes 294920 | tf_op jit(solution)/shard_map/ppermute | solution.py:616
  33.4 10.8 %collective-permute-start.7 = (bf16[192,256]{1,0:T(8,128)(2,1)S(1)}, bf16[192,256]{1,0:T(8,128)(2,1)S(1)}, u32[]{:S(2)}, u32[]{:S(2)}) collective-permute-start(bf16[192,256]{1,0:T(8,128)(2,1)S(1)} %get-tuple-element.62), channel_id=1, source_target_pairs={{0,8},{4,12},{8,0},{12,4},{1,9},{5,13},{9,1},{13,5},{2,10},{6,14},... | collective-permute-start | bytes 294920 | tf_op jit(solution)/shard_map/ppermute | solution.py:616
  34.4 9.7 %collective-permute-start.8 = (bf16[192,256]{1,0:T(8,128)(2,1)S(1)}, bf16[192,256]{1,0:T(8,128)(2,1)S(1)}, u32[]{:S(2)}, u32[]{:S(2)}) collective-permute-start(bf16[192,256]{1,0:T(8,128)(2,1)S(1)} %get-tuple-element.63), channel_id=1, source_target_pairs={{0,12},{4,8},{8,4},{12,0},{1,13},{5,9},{9,5},{13,1},{2,14},{6,10},... | collective-permute-start | bytes 294920 | tf_op jit(solution)/shard_map/ppermute | solution.py:616
  50.9 4.2 %collective-permute-start.13 = (bf16[32,768]{1,0:T(8,128)(2,1)S(1)}, bf16[32,768]{1,0:T(8,128)(2,1)S(1)}, u32[]{:S(2)}, u32[]{:S(2)}) collective-permute-start(bf16[32,768]{1,0:T(8,128)(2,1)S(1)} %get-tuple-element.72), channel_id=1, source_target_pairs={{0,1},{1,0},{2,3},{3,2},{4,5},{5,4},{6,7},{7,6},{8,9},{9,8},{10,11... | collective-permute-start | bytes 147464 | tf_op jit(solution)/shard_map/ppermute | solution.py:694
  51.0 4.1 %collective-permute-start.12 = (bf16[32,768]{1,0:T(8,128)(2,1)S(1)}, bf16[32,768]{1,0:T(8,128)(2,1)S(1)}, u32[]{:S(2)}, u32[]{:S(2)}) collective-permute-start(bf16[32,768]{1,0:T(8,128)(2,1)S(1)} %get-tuple-element.73), channel_id=1, source_target_pairs={{0,3},{3,0},{1,2},{2,1},{4,7},{7,4},{5,6},{6,5},{8,11},{11,8},{9,1... | collective-permute-start | bytes 147464 | tf_op jit(solution)/shard_map/ppermute | solution.py:693
  51.6 4.5 %collective-permute-start.11 = (bf16[32,768]{1,0:T(8,128)(2,1)S(1)}, bf16[32,768]{1,0:T(8,128)(2,1)S(1)}, u32[]{:S(2)}, u32[]{:S(2)}) collective-permute-start(bf16[32,768]{1,0:T(8,128)(2,1)S(1)} %get-tuple-element.73), channel_id=1, source_target_pairs={{0,2},{2,0},{1,3},{3,1},{4,6},{6,4},{5,7},{7,5},{8,10},{10,8},{9,1... | collective-permute-start | bytes 147464 | tf_op jit(solution)/shard_map/ppermute | solution.py:692
  56.1 6.5 %collective-permute-start.16 = (bf16[32,768]{1,0:T(8,128)(2,1)S(1)}, bf16[32,768]{1,0:T(8,128)(2,1)S(1)}, u32[]{:S(2)}, u32[]{:S(2)}) collective-permute-start(bf16[32,768]{1,0:T(8,128)(2,1)S(1)} %add_convert_fusion.mine), channel_id=1, source_target_pairs={{0,12},{4,8},{8,4},{12,0},{1,13},{5,9},{9,5},{13,1},{2,14},{6,10},... | collective-permute-start | bytes 147464 | tf_op jit(solution)/shard_map/ppermute | solution.py:717
  58.4 5.7 %collective-permute-start.15 = (bf16[32,768]{1,0:T(8,128)(2,1)S(1)}, bf16[32,768]{1,0:T(8,128)(2,1)S(1)}, u32[]{:S(2)}, u32[]{:S(2)}) collective-permute-start(bf16[32,768]{1,0:T(8,128)(2,1)S(1)} %add_convert_fusion.mine), channel_id=1, source_target_pairs={{0,8},{4,12},{8,0},{12,4},{1,9},{5,13},{9,1},{13,5},{2,10},{6,14},... | collective-permute-start | bytes 147464 | tf_op jit(solution)/shard_map/ppermute | solution.py:717
  59.6 4.5 %collective-permute-start.14 = (bf16[32,768]{1,0:T(8,128)(2,1)S(1)}, bf16[32,768]{1,0:T(8,128)(2,1)S(1)}, u32[]{:S(2)}, u32[]{:S(2)}) collective-permute-start(bf16[32,768]{1,0:T(8,128)(2,1)S(1)} %add_convert_fusion.mine), channel_id=1, source_target_pairs={{0,4},{4,0},{8,12},{12,8},{1,5},{5,1},{9,13},{13,9},{2,6},{6,2},{1... | collective-permute-start | bytes 147464 | tf_op jit(solution)/shard_map/ppermute | solution.py:717

commit v6 on v5

--- a/solution.py
+++ b/solution.py
@@ -462,7 +462,7 @@
         sums[tile] = jnp.sum(partial[...], axis=1)
         return carry
 
-    lax.fori_loop(0, tiles, one_tile, 0, unroll=2)
+    lax.fori_loop(0, tiles, one_tile, 0, unroll=4)
     for tile in range(half_tiles):
         cols = slice(tile * LANES, (tile + 1) * LANES)
         sums_own[:, cols] = sums[side * half_tiles + tile].astype(sums_own.dtype)
@@ -492,7 +492,7 @@
         mean_two[...] += grad * normed[tile, WIDE : WIDE + rows]
         return carry
 
-    lax.fori_loop(0, tiles, one_tile, 0, unroll=2)
+    lax.fori_loop(0, tiles, one_tile, 0, unroll=4)
     for index, total in enumerate((mean_one, mean_two)):
         mean = jnp.sum(total[...], axis=1, keepdims=True) * (1.0 / (tiles * LANES))
         means[index] = jnp.broadcast_to(mean, (rows, LANES))

time: 64.9 us -> 64.8 us (level)
  no operation moved by 1% of the time
where the time goes in v6:
time: 64.8 us; the launch traced here: 64.6 us
  starting transfers between devices  24.8 us (38%)
  waiting for transfers between devices  20.8 us (32%)
  Pallas kernels  17.4 us (27%)
  between operations  1.54 us (2%)
    ppermute x5, waiting for transfers between devices, fast_shards(): lax.ppermute(one, 'ctx', facing(count, step))  9.47 us
    ppermute x5, starting transfers between devices, fast_shards(): lax.ppermute(one, 'ctx', facing(count, step))  9.46 us
    ppermute x3, waiting for transfers between devices, fast_shards(): lax.ppermute(reply, 'ctx', facing(count, step))  7.74 us
    pallas_call x1, Pallas kernels, fast_shards(): pl.pallas_call(module_kernel, name='conv_module', out_shape=[jax.ShapeDty...  6.62 us
    ppermute x3, starting transfers between devices, fast_shards(): lax.ppermute(reply, 'ctx', facing(count, step))  4.92 us
    pallas_call x2, Pallas kernels, fast_shards(): pl.pallas_call(functools.partial(attend_kernel, chunk), name='attend', ou...  4.77 us
    ppermute x3, starting transfers between devices, fast_shards(): lax.ppermute(found, 'ctx', facing(count, step))  4.45 us
    ppermute x1, starting transfers between devices, fast_shards(): w_near = lax.ppermute(w_sent, 'fsdp', swap)  3 us
  transfers between devices with their start and end apart: 17, of which 8 were waited for; matrix products, arithmetic and copies ran while one was open for 0% of the time, Pallas kernels for 13%

profile of v6, /device:TPU:0, one launch (start us, length us, event | category | flops | bytes accessed | tf_op | source)
XLA Modules:
  0.0 64.6 jit_solution(8016074269050860475)
XLA Ops:
  0.7 1.9 %pack.1 = (bf16[672,256]{1,0:T(8,128)(2,1)S(1)}, bf16[384,128]{1,0:T(8,128)(2,1)S(1)}, bf16[384,128]{1,0:T(8,128)(2,1)S(1)}, bf16[384,128]{1,0:T(8,128)(2,1)S(1)...) custom-call(bf16[1,128,1024]{2,1,0:T(8,128)(2,1)} %query_ref.3, ...), custom_call_target="tpu_custom_call" | custom-call | tf_op jit(solution)/shard_map/pack/pallas_call | solution.py:556
  2.6 3.0 %collective-permute-start.9 = (bf16[592,768]{1,0:T(8,128)(2,1)S(1)}, bf16[592,768]{1,0:T(8,128)(2,1)S(1)}, u32[]{:S(2)}, u32[]{:S(2)}) collective-permute-start(bf16[592,768]{1,0:T(8,128)(2,1)S(1)} %get-tuple-element.66), channel_id=1, source_target_pairs={{0,2},{2,0},{1,3},{3,1},{4,6},{6,4},{5,7},{7,5},{8,10},{10,8},{9,1... | collective-permute-start | bytes 2727944 | tf_op jit(solution)/shard_map/ppermute | solution.py:591
  5.6 1.6 %collective-permute-start = (bf16[672,256]{1,0:T(8,128)(2,1)S(1)}, bf16[672,256]{1,0:T(8,128)(2,1)S(1)}, u32[]{:S(2)}, u32[]{:S(2)}) collective-permute-start(bf16[672,256]{1,0:T(8,128)(2,1)S(1)} %get-tuple-element.48), channel_id=1, source_target_pairs={{0,4},{4,0},{8,12},{12,8},{1,5},{5,1},{9,13},{13,9},{2,6},{6,2},{1... | collective-permute-start | bytes 1032200 | tf_op jit(solution)/shard_map/ppermute | solution.py:588
  7.2 2.6 %collective-permute-start.4 = (bf16[384,128]{1,0:T(8,128)(2,1)S(1)}, bf16[384,128]{1,0:T(8,128)(2,1)S(1)}, u32[]{:S(2)}, u32[]{:S(2)}) collective-permute-start(bf16[384,128]{1,0:T(8,128)(2,1)S(1)} %get-tuple-element.55), channel_id=1, source_target_pairs={{0,8},{4,12},{8,0},{12,4},{1,9},{5,13},{9,1},{13,5},{2,10},{6,14},... | collective-permute-start | bytes 294920 | tf_op jit(solution)/shard_map/ppermute | solution.py:588
  9.8 0.2 collective-permute-start.5
  10.0 0.7 %collective-permute-start.3 = (bf16[48,1536]{1,0:T(8,128)(2,1)S(1)}, bf16[48,1536]{1,0:T(8,128)(2,1)S(1)}, u32[]{:S(2)}, u32[]{:S(2)}) collective-permute-start(bf16[48,1536]{1,0:T(8,128)(2,1)S(1)} %get-tuple-element.51), channel_id=1, source_target_pairs={{4,8},{8,4},{5,9},{9,5},{6,10},{10,6},{7,11},{11,7},{20,24},{24,20... | collective-permute-start | bytes 442376 | tf_op jit(solution)/shard_map/ppermute | solution.py:590
  10.7 6.8 %collective-permute-done.4.refs_1_ = bf16[384,128]{1,0:T(8,128)(2,1)S(1)} collective-permute-done((bf16[384,128]{1,0:T(8,128)(2,1)S(1)}, bf16[384,128]{1,0:T(8,128)(2,1)S(1)}, u32[]{:S(2)}, u32[]{:S(2)}) %collective-permute-start.4) | collective-permute-done | bytes 98336 | tf_op jit(solution)/shard_map/ppermute | solution.py:588
  17.4 3.4 %collective-permute-start.1 = (bf16[384,128]{1,0:T(8,128)(2,1)S(1)}, bf16[384,128]{1,0:T(8,128)(2,1)S(1)}, u32[]{:S(2)}, u32[]{:S(2)}) collective-permute-start(bf16[384,128]{1,0:T(8,128)(2,1)S(1)} %get-tuple-element.49), channel_id=1, source_target_pairs={{0,8},{4,12},{8,0},{12,4},{1,9},{5,13},{9,1},{13,5},{2,10},{6,14},... | collective-permute-start | bytes 294920 | tf_op jit(solution)/shard_map/ppermute | solution.py:588
  20.9 0.8 %collective-permute-done.5.refs_2_ = bf16[384,128]{1,0:T(8,128)(2,1)S(1)} collective-permute-done((bf16[384,128]{1,0:T(8,128)(2,1)S(1)}, bf16[384,128]{1,0:T(8,128)(2,1)S(1)}, u32[]{:S(2)}, u32[]{:S(2)}) %collective-permute-start.5) | collective-permute-done | bytes 98336 | tf_op jit(solution)/shard_map/ppermute | solution.py:588
  21.7 1.6 %collective-permute-start.2 = (bf16[384,128]{1,0:T(8,128)(2,1)S(1)}, bf16[384,128]{1,0:T(8,128)(2,1)S(1)}, u32[]{:S(2)}, u32[]{:S(2)}) collective-permute-start(bf16[384,128]{1,0:T(8,128)(2,1)S(1)} %get-tuple-element.50), channel_id=1, source_target_pairs={{0,12},{4,8},{8,4},{12,0},{1,13},{5,9},{9,5},{13,1},{2,14},{6,10},... | collective-permute-start | bytes 294920 | tf_op jit(solution)/shard_map/ppermute | solution.py:588
  24.1 2.4 %attend.2 = (bf16[192,128]{1,0:T(8,128)(2,1)S(1)}, bf16[192,128]{1,0:T(8,128)(2,1)S(1)}, bf16[192,128]{1,0:T(8,128)(2,1)S(1)}, bf16[192,128]{1,0:T(8,128)(2,1)S(1)}) custom-call(s32[1]{0:T(128)S(6)} %copy.15.length_ref.refs_0_, bf16[1,128,1024]{2,1,0:T(8,128)(2,1)S(1)} %copy-done.2, bf16[1,128,1024]{2,1,0:T(8,128)(2,1)S(1)} %copy-done.3, ...), custom_call_target="tpu_custom_call" | custom-call | flops 1 | bytes 1 | tf_op jit(solution)/shard_map/attend/pallas_call | solution.py:600
  26.5 1.9 %collective-permute-done.1.refs_1_ = bf16[384,128]{1,0:T(8,128)(2,1)S(1)} collective-permute-done((bf16[384,128]{1,0:T(8,128)(2,1)S(1)}, bf16[384,128]{1,0:T(8,128)(2,1)S(1)}, u32[]{:S(2)}, u32[]{:S(2)}) %collective-permute-start.1) | collective-permute-done | bytes 98336 | tf_op jit(solution)/shard_map/ppermute | solution.py:588
  28.4 2.4 %attend.3 = (bf16[192,256]{1,0:T(8,128)(2,1)S(1)}, bf16[192,256]{1,0:T(8,128)(2,1)S(1)}, bf16[192,256]{1,0:T(8,128)(2,1)S(1)}, bf16[192,256]{1,0:T(8,128)(2,1)S(1)}) custom-call(s32[1]{0:T(128)S(6)} %copy.15.length_ref.refs_0_, bf16[1,128,1024]{2,1,0:T(8,128)(2,1)S(1)} %copy-done.2, bf16[1,128,1024]{2,1,0:T(8,128)(2,1)S(1)} %copy-done.3, ...), custom_call_target="tpu_custom_call" | custom-call | flops 1 | bytes 1 | tf_op jit(solution)/shard_map/attend/pallas_call | solution.py:600
  30.8 0.1 collective-permute-start.10
  30.9 2.5 %collective-permute-start.6 = (bf16[192,256]{1,0:T(8,128)(2,1)S(1)}, bf16[192,256]{1,0:T(8,128)(2,1)S(1)}, u32[]{:S(2)}, u32[]{:S(2)}) collective-permute-start(bf16[192,256]{1,0:T(8,128)(2,1)S(1)} %get-tuple-element.61), channel_id=1, source_target_pairs={{0,4},{4,0},{8,12},{12,8},{1,5},{5,1},{9,13},{13,9},{2,6},{6,2},{1... | collective-permute-start | bytes 294920 | tf_op jit(solution)/shard_map/ppermute | solution.py:616
  33.4 1.1 %collective-permute-start.7 = (bf16[192,256]{1,0:T(8,128)(2,1)S(1)}, bf16[192,256]{1,0:T(8,128)(2,1)S(1)}, u32[]{:S(2)}, u32[]{:S(2)}) collective-permute-start(bf16[192,256]{1,0:T(8,128)(2,1)S(1)} %get-tuple-element.62), channel_id=1, source_target_pairs={{0,8},{4,12},{8,0},{12,4},{1,9},{5,13},{9,1},{13,5},{2,10},{6,14},... | collective-permute-start | bytes 294920 | tf_op jit(solution)/shard_map/ppermute | solution.py:616
  34.4 1.3 %collective-permute-start.8 = (bf16[192,256]{1,0:T(8,128)(2,1)S(1)}, bf16[192,256]{1,0:T(8,128)(2,1)S(1)}, u32[]{:S(2)}, u32[]{:S(2)}) collective-permute-start(bf16[192,256]{1,0:T(8,128)(2,1)S(1)} %get-tuple-element.63), channel_id=1, source_target_pairs={{0,12},{4,8},{8,4},{12,0},{1,13},{5,9},{9,5},{13,1},{2,14},{6,10},... | collective-permute-start | bytes 294920 | tf_op jit(solution)/shard_map/ppermute | solution.py:616
  35.8 0.5 prepare.1
  36.4 0.4 collective-permute-done.6.refs_1_
  36.7 7.4 %collective-permute-done.7.refs_2_ = bf16[192,256]{1,0:T(8,128)(2,1)S(1)} collective-permute-done((bf16[192,256]{1,0:T(8,128)(2,1)S(1)}, bf16[192,256]{1,0:T(8,128)(2,1)S(1)}, u32[]{:S(2)}, u32[]{:S(2)}) %collective-permute-start.7) | collective-permute-done | bytes 98336 | tf_op jit(solution)/shard_map/ppermute | solution.py:616
  44.1 6.6 %conv_module.1 = (bf16[128,1536]{1,0:T(8,128)(2,1)}, f32[12,200,128]{2,1,0:T(8,128)S(1)}, f32[12,168,128]{2,1,0:T(8,128)S(1)}, f32[128,128]{1,0:T(8,128)S(1)}, b...) custom-call(s32[1]{0:T(128)S(6)} %copy.15.length_ref.refs_0_, ...), custom_call_target="tpu_custom_call" | custom-call | flops 628359168 | bytes 5505024 | tf_op jit(solution)/shard_map/conv_module/pallas_call | solution.py:655
  50.8 0.7 %collective-permute-start.12 = (bf16[32,768]{1,0:T(8,128)(2,1)S(1)}, bf16[32,768]{1,0:T(8,128)(2,1)S(1)}, u32[]{:S(2)}, u32[]{:S(2)}) collective-permute-start(bf16[32,768]{1,0:T(8,128)(2,1)S(1)} %get-tuple-element.73), channel_id=1, source_target_pairs={{0,3},{3,0},{1,2},{2,1},{4,7},{7,4},{5,6},{6,5},{8,11},{11,8},{9,1... | collective-permute-start | bytes 147464 | tf_op jit(solution)/shard_map/ppermute | solution.py:693
  51.5 1.5 %collective-permute-start.11 = (bf16[32,768]{1,0:T(8,128)(2,1)S(1)}, bf16[32,768]{1,0:T(8,128)(2,1)S(1)}, u32[]{:S(2)}, u32[]{:S(2)}) collective-permute-start(bf16[32,768]{1,0:T(8,128)(2,1)S(1)} %get-tuple-element.73), channel_id=1, source_target_pairs={{0,2},{2,0},{1,3},{3,1},{4,6},{6,4},{5,7},{7,5},{8,10},{10,8},{9,1... | collective-permute-start | bytes 147464 | tf_op jit(solution)/shard_map/ppermute | solution.py:692
  53.0 1.9 %conv_backward.1 = (f32[12,128,128]{2,1,0:T(8,128)S(1)}, f32[2,128,128]{2,1,0:T(8,128)S(1)}) custom-call(s32[1]{0:T(128)S(6)} %copy.15.length_ref.refs_0_, f32[12,200,128]{2,1,0:T(8,128)S(1)} %get-tuple-element.74.normed, f32[12,168,128]{2,1,0:T(8,128)S(1)} %get-tuple-element.75.wide_grad, f32[12,40,128]{2,1,0:T(8,128)S(1)} %get-tuple-element.70.refs_6_.params), custom_call_target="tpu_custom_call" | custom-call | flops 12189696 | bytes 2359296 | tf_op jit(solution)/shard_map/conv_backward/pallas_call | solution.py:696
  54.9 1.1 %collective-permute-done.11 = bf16[32,768]{1,0:T(8,128)(2,1)S(1)} collective-permute-done((bf16[32,768]{1,0:T(8,128)(2,1)S(1)}, bf16[32,768]{1,0:T(8,128)(2,1)S(1)}, u32[]{:S(2)}, u32[]{:S(2)}) %collective-permute-start.11) | collective-permute-done | bytes 49184 | tf_op jit(solution)/shard_map/ppermute | solution.py:692
  56.0 2.2 %collective-permute-start.16 = (bf16[32,768]{1,0:T(8,128)(2,1)S(1)}, bf16[32,768]{1,0:T(8,128)(2,1)S(1)}, u32[]{:S(2)}, u32[]{:S(2)}) collective-permute-start(bf16[32,768]{1,0:T(8,128)(2,1)S(1)} %add_convert_fusion.mine), channel_id=1, source_target_pairs={{0,12},{4,8},{8,4},{12,0},{1,13},{5,9},{9,5},{13,1},{2,14},{6,10},... | collective-permute-start | bytes 147464 | tf_op jit(solution)/shard_map/ppermute | solution.py:717
  58.2 1.2 %collective-permute-start.15 = (bf16[32,768]{1,0:T(8,128)(2,1)S(1)}, bf16[32,768]{1,0:T(8,128)(2,1)S(1)}, u32[]{:S(2)}, u32[]{:S(2)}) collective-permute-start(bf16[32,768]{1,0:T(8,128)(2,1)S(1)} %add_convert_fusion.mine), channel_id=1, source_target_pairs={{0,8},{4,12},{8,0},{12,4},{1,9},{5,13},{9,1},{13,5},{2,10},{6,14},... | collective-permute-start | bytes 147464 | tf_op jit(solution)/shard_map/ppermute | solution.py:717
  59.4 1.0 %collective-permute-start.14 = (bf16[32,768]{1,0:T(8,128)(2,1)S(1)}, bf16[32,768]{1,0:T(8,128)(2,1)S(1)}, u32[]{:S(2)}, u32[]{:S(2)}) collective-permute-start(bf16[32,768]{1,0:T(8,128)(2,1)S(1)} %add_convert_fusion.mine), channel_id=1, source_target_pairs={{0,4},{4,0},{8,12},{12,8},{1,5},{5,1},{9,13},{13,9},{2,6},{6,2},{1... | collective-permute-start | bytes 147464 | tf_op jit(solution)/shard_map/ppermute | solution.py:717
  60.5 0.9 %hidden_grad.1 = bf16[128,1536]{1,0:T(8,128)(2,1)} custom-call(bf16[128,1536]{1,0:T(8,128)(2,1)S(1)} %bitcast.5, f32[12,200,128]{2,1,0:T(8,128)S(1)} %get-tuple-element.74.normed, f32[128,128]{1,0:T(8,128)S(1)} %get-tuple-element.80.inv_rows, f32[12,128,128]{2,1,0:T(8,128)S(1)} %get-tuple-element.81.grad_hat, f32[2,128,128]{2,1,0:T(8,128)S(1)} %get-tuple-element.82.means), custom_call_target="tpu_custom_call" | custom-call | flops 1179648 | bytes 2359296 | tf_op jit(solution)/shard_map/hidden_grad/pallas_call | solution.py:718
  61.4 1.1 %collective-permute-done.16.three = bf16[32,768]{1,0:T(8,128)(2,1)S(1)} collective-permute-done((bf16[32,768]{1,0:T(8,128)(2,1)S(1)}, bf16[32,768]{1,0:T(8,128)(2,1)S(1)}, u32[]{:S(2)}, u32[]{:S(2)}) %collective-permute-start.16) | collective-permute-done | bytes 49184 | tf_op jit(solution)/shard_map/ppermute | solution.py:717
  62.5 1.4 %collective-permute-done.15.two = bf16[32,768]{1,0:T(8,128)(2,1)S(1)} collective-permute-done((bf16[32,768]{1,0:T(8,128)(2,1)S(1)}, bf16[32,768]{1,0:T(8,128)(2,1)S(1)}, u32[]{:S(2)}, u32[]{:S(2)}) %collective-permute-start.15) | collective-permute-done | bytes 49184 | tf_op jit(solution)/shard_map/ppermute | solution.py:717
  63.9 0.7 %finish.1 = (f32[31,768]{1,0:T(8,128)}, f32[768]{0:T(1024)}, f32[768]{0:T(1024)}) custom-call(bf16[32,768]{1,0:T(8,128)(2,1)S(1)} %add_convert_fusion.mine, bf16[32,768]{1,0:T(8,128)(2,1)S(1)} %collective-permute-done.14.one, bf16[32,768]{1,0:T(8,128)(2,1)S(1)} %collective-permute-done.15.two, bf16[32,768]{1,0:T(8,128)(2,1)S(1)} %collective-permute-done.16.three, ...), custom_call_target="tpu_custom_call" | custom-call | tf_op jit(solution)/shard_map/finish/pallas_call | solution.py:735
  (29 shorter events, 0.2 us)
Async XLA Ops:
  0.6 23.5 %copy-start.4 = (bf16[1,128,1024]{2,1,0:T(8,128)(2,1)S(1)}, bf16[1,128,1024]{2,1,0:T(8,128)(2,1)}, u32[]{:S(2)}) copy-start(bf16[1,128,1024]{2,1,0:T(8,128)(2,1)} %value_ref.3) | copy-start | bytes 786436
  0.6 23.5 %copy-start.3 = (bf16[1,128,1024]{2,1,0:T(8,128)(2,1)S(1)}, bf16[1,128,1024]{2,1,0:T(8,128)(2,1)}, u32[]{:S(2)}) copy-start(bf16[1,128,1024]{2,1,0:T(8,128)(2,1)} %key_ref.3) | copy-start | bytes 786436
  0.7 23.5 %copy-start.2 = (bf16[1,128,1024]{2,1,0:T(8,128)(2,1)S(1)}, bf16[1,128,1024]{2,1,0:T(8,128)(2,1)}, u32[]{:S(2)}) copy-start(bf16[1,128,1024]{2,1,0:T(8,128)(2,1)} %query_ref.3) | copy-start | bytes 786436
  2.6 28.2 %collective-permute-start.9 = (bf16[592,768]{1,0:T(8,128)(2,1)S(1)}, bf16[592,768]{1,0:T(8,128)(2,1)S(1)}, u32[]{:S(2)}, u32[]{:S(2)}) collective-permute-start(bf16[592,768]{1,0:T(8,128)(2,1)S(1)} %get-tuple-element.66), channel_id=1, source_target_pairs={{0,2},{2,0},{1,3},{3,1},{4,6},{6,4},{5,7},{7,5},{8,10},{10,8},{9,1... | collective-permute-start | bytes 2727944 | tf_op jit(solution)/shard_map/ppermute | solution.py:591
  5.6 18.5 %collective-permute-start = (bf16[672,256]{1,0:T(8,128)(2,1)S(1)}, bf16[672,256]{1,0:T(8,128)(2,1)S(1)}, u32[]{:S(2)}, u32[]{:S(2)}) collective-permute-start(bf16[672,256]{1,0:T(8,128)(2,1)S(1)} %get-tuple-element.48), channel_id=1, source_target_pairs={{0,4},{4,0},{8,12},{12,8},{1,5},{5,1},{9,13},{13,9},{2,6},{6,2},{1... | collective-permute-start | bytes 1032200 | tf_op jit(solution)/shard_map/ppermute | solution.py:588
  7.2 10.2 %collective-permute-start.4 = (bf16[384,128]{1,0:T(8,128)(2,1)S(1)}, bf16[384,128]{1,0:T(8,128)(2,1)S(1)}, u32[]{:S(2)}, u32[]{:S(2)}) collective-permute-start(bf16[384,128]{1,0:T(8,128)(2,1)S(1)} %get-tuple-element.55), channel_id=1, source_target_pairs={{0,8},{4,12},{8,0},{12,4},{1,9},{5,13},{9,1},{13,5},{2,10},{6,14},... | collective-permute-start | bytes 294920 | tf_op jit(solution)/shard_map/ppermute | solution.py:588
  9.8 11.9 %collective-permute-start.5 = (bf16[384,128]{1,0:T(8,128)(2,1)S(1)}, bf16[384,128]{1,0:T(8,128)(2,1)S(1)}, u32[]{:S(2)}, u32[]{:S(2)}) collective-permute-start(bf16[384,128]{1,0:T(8,128)(2,1)S(1)} %get-tuple-element.56), channel_id=1, source_target_pairs={{0,12},{4,8},{8,4},{12,0},{1,13},{5,9},{9,5},{13,1},{2,14},{6,10},... | collective-permute-start | bytes 294920 | tf_op jit(solution)/shard_map/ppermute | solution.py:588
  10.0 18.4 %collective-permute-start.3 = (bf16[48,1536]{1,0:T(8,128)(2,1)S(1)}, bf16[48,1536]{1,0:T(8,128)(2,1)S(1)}, u32[]{:S(2)}, u32[]{:S(2)}) collective-permute-start(bf16[48,1536]{1,0:T(8,128)(2,1)S(1)} %get-tuple-element.51), channel_id=1, source_target_pairs={{4,8},{8,4},{5,9},{9,5},{6,10},{10,6},{7,11},{11,7},{20,24},{24,20... | collective-permute-start | bytes 442376 | tf_op jit(solution)/shard_map/ppermute | solution.py:590
  17.4 10.9 %collective-permute-start.1 = (bf16[384,128]{1,0:T(8,128)(2,1)S(1)}, bf16[384,128]{1,0:T(8,128)(2,1)S(1)}, u32[]{:S(2)}, u32[]{:S(2)}) collective-permute-start(bf16[384,128]{1,0:T(8,128)(2,1)S(1)} %get-tuple-element.49), channel_id=1, source_target_pairs={{0,8},{4,12},{8,0},{12,4},{1,9},{5,13},{9,1},{13,5},{2,10},{6,14},... | collective-permute-start | bytes 294920 | tf_op jit(solution)/shard_map/ppermute | solution.py:588
  21.7 6.6 %collective-permute-start.2 = (bf16[384,128]{1,0:T(8,128)(2,1)S(1)}, bf16[384,128]{1,0:T(8,128)(2,1)S(1)}, u32[]{:S(2)}, u32[]{:S(2)}) collective-permute-start(bf16[384,128]{1,0:T(8,128)(2,1)S(1)} %get-tuple-element.50), channel_id=1, source_target_pairs={{0,12},{4,8},{8,4},{12,0},{1,13},{5,9},{9,5},{13,1},{2,14},{6,10},... | collective-permute-start | bytes 294920 | tf_op jit(solution)/shard_map/ppermute | solution.py:588
  24.0 11.8 %copy-start = (bf16[1024,768]{1,0:T(8,128)(2,1)S(1)}, bf16[1024,768]{1,0:T(8,128)(2,1)}, u32[]{:S(2)}) copy-start(bf16[1024,768]{1,0:T(8,128)(2,1)} %refs_7_.3) | copy-start | bytes 4718596
  24.0 11.8 %copy-start.1 = (bf16[1,128,1536]{2,1,0:T(8,128)(2,1)S(1)}, bf16[1,128,1536]{2,1,0:T(8,128)(2,1)}, u32[]{:S(2)}) copy-start(bf16[1,128,1536]{2,1,0:T(8,128)(2,1)} %refs_4_.1) | copy-start | bytes 1179652
  24.0 11.8 %copy-start.5 = (bf16[1,128,1536]{2,1,0:T(8,128)(2,1)S(1)}, bf16[1,128,1536]{2,1,0:T(8,128)(2,1)}, u32[]{:S(2)}) copy-start(bf16[1,128,1536]{2,1,0:T(8,128)(2,1)} %refs_3_.1) | copy-start | bytes 1179652
  24.0 11.8 %copy-start.6 = (f32[31,768]{1,0:T(8,128)S(1)}, f32[31,768]{1,0:T(8,128)}, u32[]{:S(2)}) copy-start(f32[31,768]{1,0:T(8,128)} %refs_9_.1) | copy-start | bytes 285700
  24.1 11.8 %copy-start.7 = (f32[768]{0:T(1024)S(1)}, f32[768]{0:T(1024)}, u32[]{:S(2)}) copy-start(f32[768]{0:T(1024)} %refs_10_.1) | copy-start | bytes 9220
  24.1 11.8 %copy-start.8 = (f32[768]{0:T(1024)S(1)}, f32[768]{0:T(1024)}, u32[]{:S(2)}) copy-start(f32[768]{0:T(1024)} %refs_11_.1) | copy-start | bytes 9220
  30.8 5.0 %collective-permute-start.10 = (bf16[592,768]{1,0:T(8,128)(2,1)S(1)}, bf16[592,768]{1,0:T(8,128)(2,1)S(1)}, u32[]{:S(2)}, u32[]{:S(2)}) collective-permute-start(bf16[592,768]{1,0:T(8,128)(2,1)S(1)} %collective-permute-done.9.refs_7_.refs_8_), channel_id=1, source_target_pairs={{0,1},{1,0},{2,3},{3,2},{4,5},{5,4},{6,7},{7,6},{8,9},{9,8},{10,11... | collective-permute-start | bytes 2727944 | tf_op jit(solution)/shard_map/ppermute | solution.py:620
  30.9 5.9 %collective-permute-start.6 = (bf16[192,256]{1,0:T(8,128)(2,1)S(1)}, bf16[192,256]{1,0:T(8,128)(2,1)S(1)}, u32[]{:S(2)}, u32[]{:S(2)}) collective-permute-start(bf16[192,256]{1,0:T(8,128)(2,1)S(1)} %get-tuple-element.61), channel_id=1, source_target_pairs={{0,4},{4,0},{8,12},{12,8},{1,5},{5,1},{9,13},{13,9},{2,6},{6,2},{1... | collective-permute-start | bytes 294920 | tf_op jit(solution)/shard_map/ppermute | solution.py:616
  33.4 10.8 %collective-permute-start.7 = (bf16[192,256]{1,0:T(8,128)(2,1)S(1)}, bf16[192,256]{1,0:T(8,128)(2,1)S(1)}, u32[]{:S(2)}, u32[]{:S(2)}) collective-permute-start(bf16[192,256]{1,0:T(8,128)(2,1)S(1)} %get-tuple-element.62), channel_id=1, source_target_pairs={{0,8},{4,12},{8,0},{12,4},{1,9},{5,13},{9,1},{13,5},{2,10},{6,14},... | collective-permute-start | bytes 294920 | tf_op jit(solution)/shard_map/ppermute | solution.py:616
  34.4 9.7 %collective-permute-start.8 = (bf16[192,256]{1,0:T(8,128)(2,1)S(1)}, bf16[192,256]{1,0:T(8,128)(2,1)S(1)}, u32[]{:S(2)}, u32[]{:S(2)}) collective-permute-start(bf16[192,256]{1,0:T(8,128)(2,1)S(1)} %get-tuple-element.63), channel_id=1, source_target_pairs={{0,12},{4,8},{8,4},{12,0},{1,13},{5,9},{9,5},{13,1},{2,14},{6,10},... | collective-permute-start | bytes 294920 | tf_op jit(solution)/shard_map/ppermute | solution.py:616
  50.7 4.1 %collective-permute-start.13 = (bf16[32,768]{1,0:T(8,128)(2,1)S(1)}, bf16[32,768]{1,0:T(8,128)(2,1)S(1)}, u32[]{:S(2)}, u32[]{:S(2)}) collective-permute-start(bf16[32,768]{1,0:T(8,128)(2,1)S(1)} %get-tuple-element.72), channel_id=1, source_target_pairs={{0,1},{1,0},{2,3},{3,2},{4,5},{5,4},{6,7},{7,6},{8,9},{9,8},{10,11... | collective-permute-start | bytes 147464 | tf_op jit(solution)/shard_map/ppermute | solution.py:694
  50.8 4.1 %collective-permute-start.12 = (bf16[32,768]{1,0:T(8,128)(2,1)S(1)}, bf16[32,768]{1,0:T(8,128)(2,1)S(1)}, u32[]{:S(2)}, u32[]{:S(2)}) collective-permute-start(bf16[32,768]{1,0:T(8,128)(2,1)S(1)} %get-tuple-element.73), channel_id=1, source_target_pairs={{0,3},{3,0},{1,2},{2,1},{4,7},{7,4},{5,6},{6,5},{8,11},{11,8},{9,1... | collective-permute-start | bytes 147464 | tf_op jit(solution)/shard_map/ppermute | solution.py:693
  51.5 4.5 %collective-permute-start.11 = (bf16[32,768]{1,0:T(8,128)(2,1)S(1)}, bf16[32,768]{1,0:T(8,128)(2,1)S(1)}, u32[]{:S(2)}, u32[]{:S(2)}) collective-permute-start(bf16[32,768]{1,0:T(8,128)(2,1)S(1)} %get-tuple-element.73), channel_id=1, source_target_pairs={{0,2},{2,0},{1,3},{3,1},{4,6},{6,4},{5,7},{7,5},{8,10},{10,8},{9,1... | collective-permute-start | bytes 147464 | tf_op jit(solution)/shard_map/ppermute | solution.py:692
  56.0 6.5 %collective-permute-start.16 = (bf16[32,768]{1,0:T(8,128)(2,1)S(1)}, bf16[32,768]{1,0:T(8,128)(2,1)S(1)}, u32[]{:S(2)}, u32[]{:S(2)}) collective-permute-start(bf16[32,768]{1,0:T(8,128)(2,1)S(1)} %add_convert_fusion.mine), channel_id=1, source_target_pairs={{0,12},{4,8},{8,4},{12,0},{1,13},{5,9},{9,5},{13,1},{2,14},{6,10},... | collective-permute-start | bytes 147464 | tf_op jit(solution)/shard_map/ppermute | solution.py:717
  58.2 5.7 %collective-permute-start.15 = (bf16[32,768]{1,0:T(8,128)(2,1)S(1)}, bf16[32,768]{1,0:T(8,128)(2,1)S(1)}, u32[]{:S(2)}, u32[]{:S(2)}) collective-permute-start(bf16[32,768]{1,0:T(8,128)(2,1)S(1)} %add_convert_fusion.mine), channel_id=1, source_target_pairs={{0,8},{4,12},{8,0},{12,4},{1,9},{5,13},{9,1},{13,5},{2,10},{6,14},... | collective-permute-start | bytes 147464 | tf_op jit(solution)/shard_map/ppermute | solution.py:717
  59.4 4.5 %collective-permute-start.14 = (bf16[32,768]{1,0:T(8,128)(2,1)S(1)}, bf16[32,768]{1,0:T(8,128)(2,1)S(1)}, u32[]{:S(2)}, u32[]{:S(2)}) collective-permute-start(bf16[32,768]{1,0:T(8,128)(2,1)S(1)} %add_convert_fusion.mine), channel_id=1, source_target_pairs={{0,4},{4,0},{8,12},{12,8},{1,5},{5,1},{9,13},{13,9},{2,6},{6,2},{1... | collective-permute-start | bytes 147464 | tf_op jit(solution)/shard_map/ppermute | solution.py:717

commit v7 on v5

--- a/solution.py
+++ b/solution.py
@@ -310,20 +310,20 @@
         ]
         for start in range(0, frames, QUERY_ROWS):
             queries = query_all[start : start + QUERY_ROWS, cols]
-            total = jnp.zeros((QUERY_ROWS, LANES), jnp.float32)
-            for key_head, value_head in heads:
+            rounded, sums = [], []
+            for key_head, _ in heads:
                 scores = lax.dot_general(
                     queries, key_head, (((1,), (1,)), ((), ())), preferred_element_type=jnp.float32
                 ) * (1.0 / math.sqrt(HD))
                 scores = jnp.where(usable, scores, NEG_FILL)
                 weights = jnp.exp(scores - jnp.max(scores, axis=1, keepdims=True))
-                sums = jnp.sum(weights, axis=1, keepdims=True)
-                total += (
-                    jnp.dot(
-                        weights.astype(jnp.bfloat16), value_head, preferred_element_type=jnp.float32
-                    )
-                    / sums
-                )
+                sums.append(jnp.sum(weights, axis=1, keepdims=True))
+                rounded.append(weights.astype(jnp.bfloat16))
+            total = jnp.dot(
+                jnp.concatenate(rounded, axis=1),
+                jnp.concatenate([value_head for _, value_head in heads], axis=0),
+                preferred_element_type=jnp.float32,
+            ) / jnp.where(lane < HD, sums[0], sums[1])
             attended[WIDE + start : WIDE + start + QUERY_ROWS, cols] = total.astype(attended.dtype)
     for step in range(4):
         owner = place ^ step

time: 64.9 us -> 64.1 us (0.988)
  Pallas kernels: 17.6 us -> 15.8 us
  waiting for transfers between devices: 20.8 us -> 21.6 us
    pallas_call x2, Pallas kernels: 4.77 us -> 3.04 us  [fast_shards(): pl.pallas_call(functools.partial(attend_kernel, chunk), name='attend', ou...]
    ppermute x5, waiting for transfers between devices: 9.47 us -> 10.3 us  [fast_shards(): lax.ppermute(one, 'ctx', facing(count, step))]
  transfers between devices with their start and end apart: 17 -> 17, of which waited for: 8 -> 8; matrix products, arithmetic and copies ran while one was open for 0% -> 0% of each run, Pallas kernels for 13% -> 10%
where the time goes in v7:
time: 64.1 us; the launch traced here: 63.9 us
  starting transfers between devices  24.8 us (39%)
  waiting for transfers between devices  21.6 us (34%)
  Pallas kernels  15.8 us (25%)
  between operations  1.54 us (2%)
    ppermute x5, waiting for transfers between devices, fast_shards(): lax.ppermute(one, 'ctx', facing(count, step))  10.3 us
    ppermute x5, starting transfers between devices, fast_shards(): lax.ppermute(one, 'ctx', facing(count, step))  9.46 us
    ppermute x3, waiting for transfers between devices, fast_shards(): lax.ppermute(reply, 'ctx', facing(count, step))  7.74 us
    pallas_call x1, Pallas kernels, fast_shards(): pl.pallas_call(module_kernel, name='conv_module', out_shape=[jax.ShapeDty...  6.76 us
    ppermute x3, starting transfers between devices, fast_shards(): lax.ppermute(reply, 'ctx', facing(count, step))  4.92 us
    ppermute x3, starting transfers between devices, fast_shards(): lax.ppermute(found, 'ctx', facing(count, step))  4.45 us
    pallas_call x2, Pallas kernels, fast_shards(): pl.pallas_call(functools.partial(attend_kernel, chunk), name='attend', ou...  3.04 us
    ppermute x1, starting transfers between devices, fast_shards(): w_near = lax.ppermute(w_sent, 'fsdp', swap)  3 us
  transfers between devices with their start and end apart: 17, of which 8 were waited for; matrix products, arithmetic and copies ran while one was open for 0% of the time, Pallas kernels for 10%

profile of v7, /device:TPU:0, one launch (start us, length us, event | category | flops | bytes accessed | tf_op | source)
XLA Modules:
  0.0 63.9 jit_solution(11528144907975417342)
XLA Ops:
  0.7 1.9 %pack.1 = (bf16[672,256]{1,0:T(8,128)(2,1)S(1)}, bf16[384,128]{1,0:T(8,128)(2,1)S(1)}, bf16[384,128]{1,0:T(8,128)(2,1)S(1)}, bf16[384,128]{1,0:T(8,128)(2,1)S(1)...) custom-call(bf16[1,128,1024]{2,1,0:T(8,128)(2,1)} %query_ref.3, ...), custom_call_target="tpu_custom_call" | custom-call | tf_op jit(solution)/shard_map/pack/pallas_call | solution.py:556
  2.6 3.0 %collective-permute-start.9 = (bf16[592,768]{1,0:T(8,128)(2,1)S(1)}, bf16[592,768]{1,0:T(8,128)(2,1)S(1)}, u32[]{:S(2)}, u32[]{:S(2)}) collective-permute-start(bf16[592,768]{1,0:T(8,128)(2,1)S(1)} %get-tuple-element.66), channel_id=1, source_target_pairs={{0,2},{2,0},{1,3},{3,1},{4,6},{6,4},{5,7},{7,5},{8,10},{10,8},{9,1... | collective-permute-start | bytes 2727944 | tf_op jit(solution)/shard_map/ppermute | solution.py:591
  5.6 1.6 %collective-permute-start = (bf16[672,256]{1,0:T(8,128)(2,1)S(1)}, bf16[672,256]{1,0:T(8,128)(2,1)S(1)}, u32[]{:S(2)}, u32[]{:S(2)}) collective-permute-start(bf16[672,256]{1,0:T(8,128)(2,1)S(1)} %get-tuple-element.48), channel_id=1, source_target_pairs={{0,4},{4,0},{8,12},{12,8},{1,5},{5,1},{9,13},{13,9},{2,6},{6,2},{1... | collective-permute-start | bytes 1032200 | tf_op jit(solution)/shard_map/ppermute | solution.py:588
  7.2 2.6 %collective-permute-start.4 = (bf16[384,128]{1,0:T(8,128)(2,1)S(1)}, bf16[384,128]{1,0:T(8,128)(2,1)S(1)}, u32[]{:S(2)}, u32[]{:S(2)}) collective-permute-start(bf16[384,128]{1,0:T(8,128)(2,1)S(1)} %get-tuple-element.55), channel_id=1, source_target_pairs={{0,8},{4,12},{8,0},{12,4},{1,9},{5,13},{9,1},{13,5},{2,10},{6,14},... | collective-permute-start | bytes 294920 | tf_op jit(solution)/shard_map/ppermute | solution.py:588
  9.8 0.2 collective-permute-start.5
  10.0 0.7 %collective-permute-start.3 = (bf16[48,1536]{1,0:T(8,128)(2,1)S(1)}, bf16[48,1536]{1,0:T(8,128)(2,1)S(1)}, u32[]{:S(2)}, u32[]{:S(2)}) collective-permute-start(bf16[48,1536]{1,0:T(8,128)(2,1)S(1)} %get-tuple-element.51), channel_id=1, source_target_pairs={{4,8},{8,4},{5,9},{9,5},{6,10},{10,6},{7,11},{11,7},{20,24},{24,20... | collective-permute-start | bytes 442376 | tf_op jit(solution)/shard_map/ppermute | solution.py:590
  10.7 6.8 %collective-permute-done.4.refs_1_ = bf16[384,128]{1,0:T(8,128)(2,1)S(1)} collective-permute-done((bf16[384,128]{1,0:T(8,128)(2,1)S(1)}, bf16[384,128]{1,0:T(8,128)(2,1)S(1)}, u32[]{:S(2)}, u32[]{:S(2)}) %collective-permute-start.4) | collective-permute-done | bytes 98336 | tf_op jit(solution)/shard_map/ppermute | solution.py:588
  17.4 3.4 %collective-permute-start.1 = (bf16[384,128]{1,0:T(8,128)(2,1)S(1)}, bf16[384,128]{1,0:T(8,128)(2,1)S(1)}, u32[]{:S(2)}, u32[]{:S(2)}) collective-permute-start(bf16[384,128]{1,0:T(8,128)(2,1)S(1)} %get-tuple-element.49), channel_id=1, source_target_pairs={{0,8},{4,12},{8,0},{12,4},{1,9},{5,13},{9,1},{13,5},{2,10},{6,14},... | collective-permute-start | bytes 294920 | tf_op jit(solution)/shard_map/ppermute | solution.py:588
  20.9 0.8 %collective-permute-done.5.refs_2_ = bf16[384,128]{1,0:T(8,128)(2,1)S(1)} collective-permute-done((bf16[384,128]{1,0:T(8,128)(2,1)S(1)}, bf16[384,128]{1,0:T(8,128)(2,1)S(1)}, u32[]{:S(2)}, u32[]{:S(2)}) %collective-permute-start.5) | collective-permute-done | bytes 98336 | tf_op jit(solution)/shard_map/ppermute | solution.py:588
  21.7 1.6 %collective-permute-start.2 = (bf16[384,128]{1,0:T(8,128)(2,1)S(1)}, bf16[384,128]{1,0:T(8,128)(2,1)S(1)}, u32[]{:S(2)}, u32[]{:S(2)}) collective-permute-start(bf16[384,128]{1,0:T(8,128)(2,1)S(1)} %get-tuple-element.50), channel_id=1, source_target_pairs={{0,12},{4,8},{8,4},{12,0},{1,13},{5,9},{9,5},{13,1},{2,14},{6,10},... | collective-permute-start | bytes 294920 | tf_op jit(solution)/shard_map/ppermute | solution.py:588
  24.1 1.5 %attend.2 = (bf16[192,128]{1,0:T(8,128)(2,1)S(1)}, bf16[192,128]{1,0:T(8,128)(2,1)S(1)}, bf16[192,128]{1,0:T(8,128)(2,1)S(1)}, bf16[192,128]{1,0:T(8,128)(2,1)S(1)}) custom-call(s32[1]{0:T(128)S(6)} %copy.15.length_ref.refs_0_, bf16[1,128,1024]{2,1,0:T(8,128)(2,1)S(1)} %copy-done.2, bf16[1,128,1024]{2,1,0:T(8,128)(2,1)S(1)} %copy-done.3, ...), custom_call_target="tpu_custom_call" | custom-call | flops 1 | bytes 1 | tf_op jit(solution)/shard_map/attend/pallas_call | solution.py:600
  25.6 2.7 %collective-permute-done.1.refs_1_ = bf16[384,128]{1,0:T(8,128)(2,1)S(1)} collective-permute-done((bf16[384,128]{1,0:T(8,128)(2,1)S(1)}, bf16[384,128]{1,0:T(8,128)(2,1)S(1)}, u32[]{:S(2)}, u32[]{:S(2)}) %collective-permute-start.1) | collective-permute-done | bytes 98336 | tf_op jit(solution)/shard_map/ppermute | solution.py:588
  28.4 1.5 %attend.3 = (bf16[192,256]{1,0:T(8,128)(2,1)S(1)}, bf16[192,256]{1,0:T(8,128)(2,1)S(1)}, bf16[192,256]{1,0:T(8,128)(2,1)S(1)}, bf16[192,256]{1,0:T(8,128)(2,1)S(1)}) custom-call(s32[1]{0:T(128)S(6)} %copy.15.length_ref.refs_0_, bf16[1,128,1024]{2,1,0:T(8,128)(2,1)S(1)} %copy-done.2, bf16[1,128,1024]{2,1,0:T(8,128)(2,1)S(1)} %copy-done.3, ...), custom_call_target="tpu_custom_call" | custom-call | flops 1 | bytes 1 | tf_op jit(solution)/shard_map/attend/pallas_call | solution.py:600
  30.0 2.5 %collective-permute-start.6 = (bf16[192,256]{1,0:T(8,128)(2,1)S(1)}, bf16[192,256]{1,0:T(8,128)(2,1)S(1)}, u32[]{:S(2)}, u32[]{:S(2)}) collective-permute-start(bf16[192,256]{1,0:T(8,128)(2,1)S(1)} %get-tuple-element.61), channel_id=1, source_target_pairs={{0,4},{4,0},{8,12},{12,8},{1,5},{5,1},{9,13},{13,9},{2,6},{6,2},{1... | collective-permute-start | bytes 294920 | tf_op jit(solution)/shard_map/ppermute | solution.py:616
  32.5 1.1 %collective-permute-start.7 = (bf16[192,256]{1,0:T(8,128)(2,1)S(1)}, bf16[192,256]{1,0:T(8,128)(2,1)S(1)}, u32[]{:S(2)}, u32[]{:S(2)}) collective-permute-start(bf16[192,256]{1,0:T(8,128)(2,1)S(1)} %get-tuple-element.62), channel_id=1, source_target_pairs={{0,8},{4,12},{8,0},{12,4},{1,9},{5,13},{9,1},{13,5},{2,10},{6,14},... | collective-permute-start | bytes 294920 | tf_op jit(solution)/shard_map/ppermute | solution.py:616
  33.6 1.3 %collective-permute-start.8 = (bf16[192,256]{1,0:T(8,128)(2,1)S(1)}, bf16[192,256]{1,0:T(8,128)(2,1)S(1)}, u32[]{:S(2)}, u32[]{:S(2)}) collective-permute-start(bf16[192,256]{1,0:T(8,128)(2,1)S(1)} %get-tuple-element.63), channel_id=1, source_target_pairs={{0,12},{4,8},{8,4},{12,0},{1,13},{5,9},{9,5},{13,1},{2,14},{6,10},... | collective-permute-start | bytes 294920 | tf_op jit(solution)/shard_map/ppermute | solution.py:616
  35.0 0.5 prepare.1
  35.5 0.4 collective-permute-done.6.refs_1_
  35.9 7.4 %collective-permute-done.7.refs_2_ = bf16[192,256]{1,0:T(8,128)(2,1)S(1)} collective-permute-done((bf16[192,256]{1,0:T(8,128)(2,1)S(1)}, bf16[192,256]{1,0:T(8,128)(2,1)S(1)}, u32[]{:S(2)}, u32[]{:S(2)}) %collective-permute-start.7) | collective-permute-done | bytes 98336 | tf_op jit(solution)/shard_map/ppermute | solution.py:616
  43.2 6.8 %conv_module.1 = (bf16[128,1536]{1,0:T(8,128)(2,1)}, f32[12,200,128]{2,1,0:T(8,128)S(1)}, f32[12,168,128]{2,1,0:T(8,128)S(1)}, f32[128,128]{1,0:T(8,128)S(1)}, b...) custom-call(s32[1]{0:T(128)S(6)} %copy.15.length_ref.refs_0_, ...), custom_call_target="tpu_custom_call" | custom-call | flops 628359168 | bytes 5505024 | tf_op jit(solution)/shard_map/conv_module/pallas_call | solution.py:655
  50.0 0.1 collective-permute-start.13
  50.1 0.7 %collective-permute-start.12 = (bf16[32,768]{1,0:T(8,128)(2,1)S(1)}, bf16[32,768]{1,0:T(8,128)(2,1)S(1)}, u32[]{:S(2)}, u32[]{:S(2)}) collective-permute-start(bf16[32,768]{1,0:T(8,128)(2,1)S(1)} %get-tuple-element.73), channel_id=1, source_target_pairs={{0,3},{3,0},{1,2},{2,1},{4,7},{7,4},{5,6},{6,5},{8,11},{11,8},{9,1... | collective-permute-start | bytes 147464 | tf_op jit(solution)/shard_map/ppermute | solution.py:693
  50.8 1.5 %collective-permute-start.11 = (bf16[32,768]{1,0:T(8,128)(2,1)S(1)}, bf16[32,768]{1,0:T(8,128)(2,1)S(1)}, u32[]{:S(2)}, u32[]{:S(2)}) collective-permute-start(bf16[32,768]{1,0:T(8,128)(2,1)S(1)} %get-tuple-element.73), channel_id=1, source_target_pairs={{0,2},{2,0},{1,3},{3,1},{4,6},{6,4},{5,7},{7,5},{8,10},{10,8},{9,1... | collective-permute-start | bytes 147464 | tf_op jit(solution)/shard_map/ppermute | solution.py:692
  52.2 2.0 %conv_backward.1 = (f32[12,128,128]{2,1,0:T(8,128)S(1)}, f32[2,128,128]{2,1,0:T(8,128)S(1)}) custom-call(s32[1]{0:T(128)S(6)} %copy.15.length_ref.refs_0_, f32[12,200,128]{2,1,0:T(8,128)S(1)} %get-tuple-element.74.normed, f32[12,168,128]{2,1,0:T(8,128)S(1)} %get-tuple-element.75.wide_grad, f32[12,40,128]{2,1,0:T(8,128)S(1)} %get-tuple-element.70.refs_6_.params), custom_call_target="tpu_custom_call" | custom-call | flops 12189696 | bytes 2359296 | tf_op jit(solution)/shard_map/conv_backward/pallas_call | solution.py:696
  54.2 1.0 %collective-permute-done.11 = bf16[32,768]{1,0:T(8,128)(2,1)S(1)} collective-permute-done((bf16[32,768]{1,0:T(8,128)(2,1)S(1)}, bf16[32,768]{1,0:T(8,128)(2,1)S(1)}, u32[]{:S(2)}, u32[]{:S(2)}) %collective-permute-start.11) | collective-permute-done | bytes 49184 | tf_op jit(solution)/shard_map/ppermute | solution.py:692
  55.3 2.2 %collective-permute-start.16 = (bf16[32,768]{1,0:T(8,128)(2,1)S(1)}, bf16[32,768]{1,0:T(8,128)(2,1)S(1)}, u32[]{:S(2)}, u32[]{:S(2)}) collective-permute-start(bf16[32,768]{1,0:T(8,128)(2,1)S(1)} %add_convert_fusion.mine), channel_id=1, source_target_pairs={{0,12},{4,8},{8,4},{12,0},{1,13},{5,9},{9,5},{13,1},{2,14},{6,10},... | collective-permute-start | bytes 147464 | tf_op jit(solution)/shard_map/ppermute | solution.py:717
  57.5 1.2 %collective-permute-start.15 = (bf16[32,768]{1,0:T(8,128)(2,1)S(1)}, bf16[32,768]{1,0:T(8,128)(2,1)S(1)}, u32[]{:S(2)}, u32[]{:S(2)}) collective-permute-start(bf16[32,768]{1,0:T(8,128)(2,1)S(1)} %add_convert_fusion.mine), channel_id=1, source_target_pairs={{0,8},{4,12},{8,0},{12,4},{1,9},{5,13},{9,1},{13,5},{2,10},{6,14},... | collective-permute-start | bytes 147464 | tf_op jit(solution)/shard_map/ppermute | solution.py:717
  58.7 1.0 %collective-permute-start.14 = (bf16[32,768]{1,0:T(8,128)(2,1)S(1)}, bf16[32,768]{1,0:T(8,128)(2,1)S(1)}, u32[]{:S(2)}, u32[]{:S(2)}) collective-permute-start(bf16[32,768]{1,0:T(8,128)(2,1)S(1)} %add_convert_fusion.mine), channel_id=1, source_target_pairs={{0,4},{4,0},{8,12},{12,8},{1,5},{5,1},{9,13},{13,9},{2,6},{6,2},{1... | collective-permute-start | bytes 147464 | tf_op jit(solution)/shard_map/ppermute | solution.py:717
  59.7 0.9 %hidden_grad.1 = bf16[128,1536]{1,0:T(8,128)(2,1)} custom-call(bf16[128,1536]{1,0:T(8,128)(2,1)S(1)} %bitcast.5, f32[12,200,128]{2,1,0:T(8,128)S(1)} %get-tuple-element.74.normed, f32[128,128]{1,0:T(8,128)S(1)} %get-tuple-element.80.inv_rows, f32[12,128,128]{2,1,0:T(8,128)S(1)} %get-tuple-element.81.grad_hat, f32[2,128,128]{2,1,0:T(8,128)S(1)} %get-tuple-element.82.means), custom_call_target="tpu_custom_call" | custom-call | flops 1179648 | bytes 2359296 | tf_op jit(solution)/shard_map/hidden_grad/pallas_call | solution.py:718
  60.6 1.1 %collective-permute-done.16.three = bf16[32,768]{1,0:T(8,128)(2,1)S(1)} collective-permute-done((bf16[32,768]{1,0:T(8,128)(2,1)S(1)}, bf16[32,768]{1,0:T(8,128)(2,1)S(1)}, u32[]{:S(2)}, u32[]{:S(2)}) %collective-permute-start.16) | collective-permute-done | bytes 49184 | tf_op jit(solution)/shard_map/ppermute | solution.py:717
  61.8 1.4 %collective-permute-done.15.two = bf16[32,768]{1,0:T(8,128)(2,1)S(1)} collective-permute-done((bf16[32,768]{1,0:T(8,128)(2,1)S(1)}, bf16[32,768]{1,0:T(8,128)(2,1)S(1)}, u32[]{:S(2)}, u32[]{:S(2)}) %collective-permute-start.15) | collective-permute-done | bytes 49184 | tf_op jit(solution)/shard_map/ppermute | solution.py:717
  63.2 0.7 %finish.1 = (f32[31,768]{1,0:T(8,128)}, f32[768]{0:T(1024)}, f32[768]{0:T(1024)}) custom-call(bf16[32,768]{1,0:T(8,128)(2,1)S(1)} %add_convert_fusion.mine, bf16[32,768]{1,0:T(8,128)(2,1)S(1)} %collective-permute-done.14.one, bf16[32,768]{1,0:T(8,128)(2,1)S(1)} %collective-permute-done.15.two, bf16[32,768]{1,0:T(8,128)(2,1)S(1)} %collective-permute-done.16.three, ...), custom_call_target="tpu_custom_call" | custom-call | tf_op jit(solution)/shard_map/finish/pallas_call | solution.py:735
  (29 shorter events, 0.2 us)
Async XLA Ops:
  0.6 23.5 %copy-start.4 = (bf16[1,128,1024]{2,1,0:T(8,128)(2,1)S(1)}, bf16[1,128,1024]{2,1,0:T(8,128)(2,1)}, u32[]{:S(2)}) copy-start(bf16[1,128,1024]{2,1,0:T(8,128)(2,1)} %value_ref.3) | copy-start | bytes 786436
  0.6 23.5 %copy-start.3 = (bf16[1,128,1024]{2,1,0:T(8,128)(2,1)S(1)}, bf16[1,128,1024]{2,1,0:T(8,128)(2,1)}, u32[]{:S(2)}) copy-start(bf16[1,128,1024]{2,1,0:T(8,128)(2,1)} %key_ref.3) | copy-start | bytes 786436
  0.7 23.5 %copy-start.2 = (bf16[1,128,1024]{2,1,0:T(8,128)(2,1)S(1)}, bf16[1,128,1024]{2,1,0:T(8,128)(2,1)}, u32[]{:S(2)}) copy-start(bf16[1,128,1024]{2,1,0:T(8,128)(2,1)} %query_ref.3) | copy-start | bytes 786436
  2.6 27.3 %collective-permute-start.9 = (bf16[592,768]{1,0:T(8,128)(2,1)S(1)}, bf16[592,768]{1,0:T(8,128)(2,1)S(1)}, u32[]{:S(2)}, u32[]{:S(2)}) collective-permute-start(bf16[592,768]{1,0:T(8,128)(2,1)S(1)} %get-tuple-element.66), channel_id=1, source_target_pairs={{0,2},{2,0},{1,3},{3,1},{4,6},{6,4},{5,7},{7,5},{8,10},{10,8},{9,1... | collective-permute-start | bytes 2727944 | tf_op jit(solution)/shard_map/ppermute | solution.py:591
  5.6 18.5 %collective-permute-start = (bf16[672,256]{1,0:T(8,128)(2,1)S(1)}, bf16[672,256]{1,0:T(8,128)(2,1)S(1)}, u32[]{:S(2)}, u32[]{:S(2)}) collective-permute-start(bf16[672,256]{1,0:T(8,128)(2,1)S(1)} %get-tuple-element.48), channel_id=1, source_target_pairs={{0,4},{4,0},{8,12},{12,8},{1,5},{5,1},{9,13},{13,9},{2,6},{6,2},{1... | collective-permute-start | bytes 1032200 | tf_op jit(solution)/shard_map/ppermute | solution.py:588
  7.2 10.2 %collective-permute-start.4 = (bf16[384,128]{1,0:T(8,128)(2,1)S(1)}, bf16[384,128]{1,0:T(8,128)(2,1)S(1)}, u32[]{:S(2)}, u32[]{:S(2)}) collective-permute-start(bf16[384,128]{1,0:T(8,128)(2,1)S(1)} %get-tuple-element.55), channel_id=1, source_target_pairs={{0,8},{4,12},{8,0},{12,4},{1,9},{5,13},{9,1},{13,5},{2,10},{6,14},... | collective-permute-start | bytes 294920 | tf_op jit(solution)/shard_map/ppermute | solution.py:588
  9.8 11.9 %collective-permute-start.5 = (bf16[384,128]{1,0:T(8,128)(2,1)S(1)}, bf16[384,128]{1,0:T(8,128)(2,1)S(1)}, u32[]{:S(2)}, u32[]{:S(2)}) collective-permute-start(bf16[384,128]{1,0:T(8,128)(2,1)S(1)} %get-tuple-element.56), channel_id=1, source_target_pairs={{0,12},{4,8},{8,4},{12,0},{1,13},{5,9},{9,5},{13,1},{2,14},{6,10},... | collective-permute-start | bytes 294920 | tf_op jit(solution)/shard_map/ppermute | solution.py:588
  10.0 18.4 %collective-permute-start.3 = (bf16[48,1536]{1,0:T(8,128)(2,1)S(1)}, bf16[48,1536]{1,0:T(8,128)(2,1)S(1)}, u32[]{:S(2)}, u32[]{:S(2)}) collective-permute-start(bf16[48,1536]{1,0:T(8,128)(2,1)S(1)} %get-tuple-element.51), channel_id=1, source_target_pairs={{4,8},{8,4},{5,9},{9,5},{6,10},{10,6},{7,11},{11,7},{20,24},{24,20... | collective-permute-start | bytes 442376 | tf_op jit(solution)/shard_map/ppermute | solution.py:590
  17.4 10.9 %collective-permute-start.1 = (bf16[384,128]{1,0:T(8,128)(2,1)S(1)}, bf16[384,128]{1,0:T(8,128)(2,1)S(1)}, u32[]{:S(2)}, u32[]{:S(2)}) collective-permute-start(bf16[384,128]{1,0:T(8,128)(2,1)S(1)} %get-tuple-element.49), channel_id=1, source_target_pairs={{0,8},{4,12},{8,0},{12,4},{1,9},{5,13},{9,1},{13,5},{2,10},{6,14},... | collective-permute-start | bytes 294920 | tf_op jit(solution)/shard_map/ppermute | solution.py:588
  21.7 6.6 %collective-permute-start.2 = (bf16[384,128]{1,0:T(8,128)(2,1)S(1)}, bf16[384,128]{1,0:T(8,128)(2,1)S(1)}, u32[]{:S(2)}, u32[]{:S(2)}) collective-permute-start(bf16[384,128]{1,0:T(8,128)(2,1)S(1)} %get-tuple-element.50), channel_id=1, source_target_pairs={{0,12},{4,8},{8,4},{12,0},{1,13},{5,9},{9,5},{13,1},{2,14},{6,10},... | collective-permute-start | bytes 294920 | tf_op jit(solution)/shard_map/ppermute | solution.py:588
  24.0 10.9 %copy-start = (bf16[1024,768]{1,0:T(8,128)(2,1)S(1)}, bf16[1024,768]{1,0:T(8,128)(2,1)}, u32[]{:S(2)}) copy-start(bf16[1024,768]{1,0:T(8,128)(2,1)} %refs_7_.3) | copy-start | bytes 4718596
  24.0 10.9 %copy-start.1 = (bf16[1,128,1536]{2,1,0:T(8,128)(2,1)S(1)}, bf16[1,128,1536]{2,1,0:T(8,128)(2,1)}, u32[]{:S(2)}) copy-start(bf16[1,128,1536]{2,1,0:T(8,128)(2,1)} %refs_4_.1) | copy-start | bytes 1179652
  24.0 10.9 %copy-start.5 = (bf16[1,128,1536]{2,1,0:T(8,128)(2,1)S(1)}, bf16[1,128,1536]{2,1,0:T(8,128)(2,1)}, u32[]{:S(2)}) copy-start(bf16[1,128,1536]{2,1,0:T(8,128)(2,1)} %refs_3_.1) | copy-start | bytes 1179652
  24.0 10.9 %copy-start.6 = (f32[31,768]{1,0:T(8,128)S(1)}, f32[31,768]{1,0:T(8,128)}, u32[]{:S(2)}) copy-start(f32[31,768]{1,0:T(8,128)} %refs_9_.1) | copy-start | bytes 285700
  24.1 10.9 %copy-start.7 = (f32[768]{0:T(1024)S(1)}, f32[768]{0:T(1024)}, u32[]{:S(2)}) copy-start(f32[768]{0:T(1024)} %refs_10_.1) | copy-start | bytes 9220
  24.1 10.9 %copy-start.8 = (f32[768]{0:T(1024)S(1)}, f32[768]{0:T(1024)}, u32[]{:S(2)}) copy-start(f32[768]{0:T(1024)} %refs_11_.1) | copy-start | bytes 9220
  29.9 5.0 %collective-permute-start.10 = (bf16[592,768]{1,0:T(8,128)(2,1)S(1)}, bf16[592,768]{1,0:T(8,128)(2,1)S(1)}, u32[]{:S(2)}, u32[]{:S(2)}) collective-permute-start(bf16[592,768]{1,0:T(8,128)(2,1)S(1)} %collective-permute-done.9.refs_7_.refs_8_), channel_id=1, source_target_pairs={{0,1},{1,0},{2,3},{3,2},{4,5},{5,4},{6,7},{7,6},{8,9},{9,8},{10,11... | collective-permute-start | bytes 2727944 | tf_op jit(solution)/shard_map/ppermute | solution.py:620
  30.0 5.9 %collective-permute-start.6 = (bf16[192,256]{1,0:T(8,128)(2,1)S(1)}, bf16[192,256]{1,0:T(8,128)(2,1)S(1)}, u32[]{:S(2)}, u32[]{:S(2)}) collective-permute-start(bf16[192,256]{1,0:T(8,128)(2,1)S(1)} %get-tuple-element.61), channel_id=1, source_target_pairs={{0,4},{4,0},{8,12},{12,8},{1,5},{5,1},{9,13},{13,9},{2,6},{6,2},{1... | collective-permute-start | bytes 294920 | tf_op jit(solution)/shard_map/ppermute | solution.py:616
  32.5 10.8 %collective-permute-start.7 = (bf16[192,256]{1,0:T(8,128)(2,1)S(1)}, bf16[192,256]{1,0:T(8,128)(2,1)S(1)}, u32[]{:S(2)}, u32[]{:S(2)}) collective-permute-start(bf16[192,256]{1,0:T(8,128)(2,1)S(1)} %get-tuple-element.62), channel_id=1, source_target_pairs={{0,8},{4,12},{8,0},{12,4},{1,9},{5,13},{9,1},{13,5},{2,10},{6,14},... | collective-permute-start | bytes 294920 | tf_op jit(solution)/shard_map/ppermute | solution.py:616
  33.6 9.7 %collective-permute-start.8 = (bf16[192,256]{1,0:T(8,128)(2,1)S(1)}, bf16[192,256]{1,0:T(8,128)(2,1)S(1)}, u32[]{:S(2)}, u32[]{:S(2)}) collective-permute-start(bf16[192,256]{1,0:T(8,128)(2,1)S(1)} %get-tuple-element.63), channel_id=1, source_target_pairs={{0,12},{4,8},{8,4},{12,0},{1,13},{5,9},{9,5},{13,1},{2,14},{6,10},... | collective-permute-start | bytes 294920 | tf_op jit(solution)/shard_map/ppermute | solution.py:616
  50.0 4.2 %collective-permute-start.13 = (bf16[32,768]{1,0:T(8,128)(2,1)S(1)}, bf16[32,768]{1,0:T(8,128)(2,1)S(1)}, u32[]{:S(2)}, u32[]{:S(2)}) collective-permute-start(bf16[32,768]{1,0:T(8,128)(2,1)S(1)} %get-tuple-element.72), channel_id=1, source_target_pairs={{0,1},{1,0},{2,3},{3,2},{4,5},{5,4},{6,7},{7,6},{8,9},{9,8},{10,11... | collective-permute-start | bytes 147464 | tf_op jit(solution)/shard_map/ppermute | solution.py:694
  50.1 4.1 %collective-permute-start.12 = (bf16[32,768]{1,0:T(8,128)(2,1)S(1)}, bf16[32,768]{1,0:T(8,128)(2,1)S(1)}, u32[]{:S(2)}, u32[]{:S(2)}) collective-permute-start(bf16[32,768]{1,0:T(8,128)(2,1)S(1)} %get-tuple-element.73), channel_id=1, source_target_pairs={{0,3},{3,0},{1,2},{2,1},{4,7},{7,4},{5,6},{6,5},{8,11},{11,8},{9,1... | collective-permute-start | bytes 147464 | tf_op jit(solution)/shard_map/ppermute | solution.py:693
  50.8 4.5 %collective-permute-start.11 = (bf16[32,768]{1,0:T(8,128)(2,1)S(1)}, bf16[32,768]{1,0:T(8,128)(2,1)S(1)}, u32[]{:S(2)}, u32[]{:S(2)}) collective-permute-start(bf16[32,768]{1,0:T(8,128)(2,1)S(1)} %get-tuple-element.73), channel_id=1, source_target_pairs={{0,2},{2,0},{1,3},{3,1},{4,6},{6,4},{5,7},{7,5},{8,10},{10,8},{9,1... | collective-permute-start | bytes 147464 | tf_op jit(solution)/shard_map/ppermute | solution.py:692
  55.3 6.5 %collective-permute-start.16 = (bf16[32,768]{1,0:T(8,128)(2,1)S(1)}, bf16[32,768]{1,0:T(8,128)(2,1)S(1)}, u32[]{:S(2)}, u32[]{:S(2)}) collective-permute-start(bf16[32,768]{1,0:T(8,128)(2,1)S(1)} %add_convert_fusion.mine), channel_id=1, source_target_pairs={{0,12},{4,8},{8,4},{12,0},{1,13},{5,9},{9,5},{13,1},{2,14},{6,10},... | collective-permute-start | bytes 147464 | tf_op jit(solution)/shard_map/ppermute | solution.py:717
  57.5 5.7 %collective-permute-start.15 = (bf16[32,768]{1,0:T(8,128)(2,1)S(1)}, bf16[32,768]{1,0:T(8,128)(2,1)S(1)}, u32[]{:S(2)}, u32[]{:S(2)}) collective-permute-start(bf16[32,768]{1,0:T(8,128)(2,1)S(1)} %add_convert_fusion.mine), channel_id=1, source_target_pairs={{0,8},{4,12},{8,0},{12,4},{1,9},{5,13},{9,1},{13,5},{2,10},{6,14},... | collective-permute-start | bytes 147464 | tf_op jit(solution)/shard_map/ppermute | solution.py:717
  58.7 4.5 %collective-permute-start.14 = (bf16[32,768]{1,0:T(8,128)(2,1)S(1)}, bf16[32,768]{1,0:T(8,128)(2,1)S(1)}, u32[]{:S(2)}, u32[]{:S(2)}) collective-permute-start(bf16[32,768]{1,0:T(8,128)(2,1)S(1)} %add_convert_fusion.mine), channel_id=1, source_target_pairs={{0,4},{4,0},{8,12},{12,8},{1,5},{5,1},{9,13},{13,9},{2,6},{6,2},{1... | collective-permute-start | bytes 147464 | tf_op jit(solution)/shard_map/ppermute | solution.py:717
